TPU v7x, 128 devices: a whole 4x4x4 slice. The times are simulated.
128 devices in a mesh: group: 4 (over x), cluster: 32 (over z, y, core).
Axes of the slice: x: 4, y: 4, z: 4, core: 2. Of those that a mesh axis runs over, the one named last changes fastest.
Arguments:
- charges: float32 [1048576, 128], P(('group', 'cluster')), may hold values from -6 to 6
- leaf_size: int32 [4096], P(('group', 'cluster')), may hold values from 1 to 256, 786432 in all
- leaf_basis: float32 [4096, 64, 256], P(('group', 'cluster')), may hold values from -0.375 to 0.375
- leaf_transfer: float32 [4096, 64, 64], P(('group', 'cluster')), may hold values from -0.375 to 0.375
- mid_transfer: float32 [1024, 64, 64], P(('group', 'cluster')), may hold values from -0.25 to 0.25
- leaf_parent: int32 [4096], P(('group', 'cluster')), may hold values from 0 to 7, as said below
- send_leaf: int32 [32768], P(('group', 'cluster')), may hold values from 0 to 32, as said below
- pair_leaf: int32 [4096, 12], P(('group', 'cluster')), may hold values from 0 to 256, as said below
- leaf_coupling: float32 [4096, 64, 768], P(('group', 'cluster')), may hold values from -0.21875 to 0.21875
- send_mid: int32 [32768], P(('group', 'cluster')), may hold values from 0 to 8, as said below
- pair_mid: int32 [1024, 32], P(('group', 'cluster')), may hold values from 0 to 256, as said below
- mid_coupling: float32 [1024, 64, 2048], P(('group', 'cluster')), may hold values from -0.125 to 0.125
- top_pairs: int32 [128, 4], P('group'), may hold values from 0 to 128, as said below
- top_coupling: float32 [128, 64, 256], P('group'), may hold values from -0.375 to 0.375
Outputs:
- far_field: float32 [1048576, 128], P(('group', 'cluster'))
Inputs may be any that keep to these rules, and one draw needn't show every extreme that they name: `send_leaf`: entry (d * 128 + r) * 2 + j is the leaf, local to device d, whose block d puts in slot j for device r, or 32 for an empty slot; the leaves in one sender's slots to one receiver are distinct; some receiver has every slot from every sender filled. `pair_leaf`: row t names leaf t's admissible partners as positions 2 * d + j among the slots its owner receives, filled slots only and distinct within a row, or 256 for no partner; every filled slot is named by some row of its receiver. `send_mid`: as send_leaf, for level-one clusters: local indices below 8, 8 for an empty slot; some receiver has every slot from every sender filled. `pair_mid`: as pair_leaf, for level-one clusters; every filled slot is named by some row of its receiver. `leaf_parent`: every level-one cluster of a device is the parent of at least one of its leaves. `top_pairs`: row o names coarse clusters other than o, distinct within a row, at least one a row, or 128 for no partner.
All inputs are finite; a program needn't handle non-finite values. No bound on the sum of `leaf_size` on one device may be relied on, other than what follows from the above.
Results may differ from a plain program's by a relative error of at most 0.000062.
Values sent between devices are 32-bit elements; how exact they have to be, the bound alone decides.
A program may use at most 128 MiB of HBM per device.

v0:
```python
import jax
import jax.numpy as jnp
from jax import lax
from jax.sharding import PartitionSpec as P

exact_mode = lax.Precision.HIGHEST


def couple(coupling, coef, index):
    stacked = jnp.take(coef, index, axis=0, mode="fill", fill_value=0.0)
    stacked = stacked.reshape(index.shape[0], index.shape[1] * coef.shape[1], coef.shape[2])
    return jnp.einsum("nkq,nqp->nkp", coupling, stacked, precision=exact_mode)


def body(
    charges,
    leaf_size,
    leaf_basis,
    leaf_transfer,
    mid_transfer,
    leaf_parent,
    send_leaf,
    pair_leaf,
    leaf_coupling,
    send_mid,
    pair_mid,
    mid_coupling,
    top_pairs,
    top_coupling,
):
    leaf_count, coef_rank, leaf_points = leaf_basis.shape
    port_count = charges.shape[1]
    mid_count = mid_transfer.shape[0]
    point_mask = (jnp.arange(leaf_points, dtype=jnp.int32)[None, :] < leaf_size[:, None]).astype(
        jnp.float32
    )
    blocks = charges.reshape(leaf_count, leaf_points, port_count) * point_mask[:, :, None]
    coef_leaf = jnp.einsum("lkm,lmp->lkp", leaf_basis, blocks, precision=exact_mode)
    outgoing_leaf = jnp.take(coef_leaf, send_leaf, axis=0, mode="fill", fill_value=0.0)
    arrived_leaf = lax.all_to_all(
        outgoing_leaf, ("group", "cluster"), split_axis=0, concat_axis=0, tiled=True
    )
    moved_up = jnp.einsum("ljk,lkp->ljp", leaf_transfer, coef_leaf, precision=exact_mode)
    parent_map = (leaf_parent[None, :] == jnp.arange(mid_count, dtype=jnp.int32)[:, None]).astype(
        jnp.float32
    )
    coef_mid = jnp.einsum("ml,ljp->mjp", parent_map, moved_up, precision=exact_mode)
    outgoing_mid = jnp.take(coef_mid, send_mid, axis=0, mode="fill", fill_value=0.0)
    arrived_mid = lax.all_to_all(
        outgoing_mid, ("group", "cluster"), split_axis=0, concat_axis=0, tiled=True
    )
    coef_top = jnp.einsum("mjk,mkp->jp", mid_transfer, coef_mid, precision=exact_mode)
    listed = top_pairs.shape[1]
    position = lax.axis_index("cluster")
    wanted = lax.dynamic_slice_in_dim(top_pairs, position, 1, 0)[0]
    own_coupling = lax.dynamic_slice_in_dim(top_coupling, position, 1, 0)[0]
    shard_rows = lax.all_gather(coef_top[None], ("group", "cluster"), axis=0, tiled=True)
    inside = (wanted >= 0) & (wanted < shard_rows.shape[0])
    taken_rows = jnp.take(shard_rows, jnp.clip(wanted, 0, shard_rows.shape[0] - 1), axis=0)
    picked = jnp.where(
        inside[:, None, None], taken_rows, jnp.zeros((listed, coef_rank, port_count), jnp.float32)
    )
    near_top = jnp.einsum(
        "kq,qp->kp",
        own_coupling,
        picked.reshape(listed * coef_rank, port_count),
        precision=exact_mode,
    )
    near_leaf = couple(leaf_coupling, arrived_leaf, pair_leaf)
    near_mid = couple(mid_coupling, arrived_mid, pair_mid)
    down_mid = near_mid + jnp.einsum("mjk,jp->mkp", mid_transfer, near_top, precision=exact_mode)
    from_parent = jnp.einsum("ml,mkp->lkp", parent_map, down_mid, precision=exact_mode)
    down_leaf = near_leaf + jnp.einsum(
        "ljk,ljp->lkp", leaf_transfer, from_parent, precision=exact_mode
    )
    far_field = (
        jnp.einsum("lkm,lkp->lmp", leaf_basis, down_leaf, precision=exact_mode)
        * point_mask[:, :, None]
    )
    return far_field.reshape(leaf_count * leaf_points, port_count)


def solution(mesh):
    in_specs = (
        P(("group", "cluster"), None),
        P(("group", "cluster")),
        P(("group", "cluster"), None, None),
        P(("group", "cluster"), None, None),
        P(("group", "cluster"), None, None),
        P(("group", "cluster")),
        P(("group", "cluster")),
        P(("group", "cluster"), None),
        P(("group", "cluster"), None, None),
        P(("group", "cluster")),
        P(("group", "cluster"), None),
        P(("group", "cluster"), None, None),
        P("group", None),
        P("group", None, None),
    )
    out_specs = P(("group", "cluster"), None)
    return jax.shard_map(body, mesh=mesh, in_specs=in_specs, out_specs=out_specs, check_vma=False)
```

profile of v0, /device:TPU:24, one launch (start us, length us, event | category | flops | bytes accessed | tf_op | source)
XLA Modules:
  0.0 346.1 jit_solution(12034021296340804855)
XLA Ops:
  8.8 5.1 %fusion = f32[32,128,64]{1,2,0:T(8,128)S(1)} fusion(f32[32,64,256]{2,1,0:T(8,128)S(1)} %copy-done, f32[32,256,128]{2,1,0:T(8,128)} %bitcast.58, f32[32,256]{1,0:T(8,128)S(1)} %fusion.11), kind=kOutput, calls=%fused_computation.10 | convolution fusion | flops 806354944 | bytes 7372800 | tf_op jit(solution)/shard_map/lkm,lmp->lkp/dot_general | solution.py:38
  13.9 2.3 fusion.20
  18.0 4.4 %gather_fusion.2 = f32[256,64,128]{2,1,0:T(8,128)} fusion(f32[8,64,128]{2,1,0:T(8,128)S(1)} %copy.19, s32[1024]{0:T(1024)S(1)} %pad_clamp_fusion.2), kind=kCustom, calls=%fused_computation.2 | custom fusion | bytes 16778240 | tf_op jit(solution)/shard_map/jit(_take)/gather | solution.py:48
  22.4 6.0 %broadcast_select_fusion = f32[256,64,128]{2,1,0:T(8,128)} fusion(f32[256,64,128]{2,1,0:T(8,128)} %gather_fusion.2, pred[256]{0:T(512)(128)(4,1)S(1)} %compare_and_fusion.3), kind=kLoop, calls=%fused_computation.8 | loop fusion | flops 2097152 | bytes 16777472 | tf_op jit(solution)/shard_map/jit(_take)/select_n | solution.py:48
  28.4 10.7 %all-to-all-start.1 = ((f32[256,64,128]{2,1,0:T(8,128)}), f32[256,64,128]{2,1,0:T(8,128)}, u32[]{:S(2)}, u32[]{:S(2)}) async-start(f32[256,64,128]{2,1,0:T(8,128)} %broadcast_select_fusion), calls=%async_computation.1 | async-start | bytes 16777216 | tf_op jit(solution)/shard_map/all_to_all | solution.py:49
  39.2 1.8 copy.24
  41.0 2.2 convolution_bitcast_fusion.3
  43.2 4.4 %gather_fusion = f32[256,64,128]{2,1,0:T(8,128)} fusion(f32[32,64,128]{2,1,0:T(8,128)S(1)} %bitcast.55, s32[1024]{0:T(1024)S(1)} %pad_clamp_fusion.4), kind=kCustom, calls=%fused_computation | custom fusion | bytes 16778240 | tf_op jit(solution)/shard_map/jit(_take)/gather | solution.py:39
  47.5 6.0 %broadcast_select_fusion.1 = f32[256,64,128]{2,1,0:T(8,128)} fusion(f32[256,64,128]{2,1,0:T(8,128)} %gather_fusion, pred[256]{0:T(512)(128)(4,1)S(1)} %compare_and_fusion.4), kind=kLoop, calls=%fused_computation.9 | loop fusion | flops 2097152 | bytes 16777472 | tf_op jit(solution)/shard_map/jit(_take)/select_n | solution.py:39
  53.5 86.9 %all-to-all-done.1 = f32[256,64,128]{2,1,0:T(8,128)} async-done(((f32[256,64,128]{2,1,0:T(8,128)}), f32[256,64,128]{2,1,0:T(8,128)}, u32[]{:S(2)}, u32[]{:S(2)}) %all-to-all-start.1) | async-done | bytes 8388640 | tf_op jit(solution)/shard_map/all_to_all | solution.py:49
  140.4 13.4 %all-to-all-start = ((f32[256,64,128]{2,1,0:T(8,128)}), f32[256,64,128]{2,1,0:T(8,128)}, u32[]{:S(2)}, u32[]{:S(2)}) async-start(f32[256,64,128]{2,1,0:T(8,128)} %broadcast_select_fusion.1), calls=%async_computation | async-start | bytes 16777216 | tf_op jit(solution)/shard_map/all_to_all | solution.py:40
  155.2 107.0 %all-gather.3.cloned.1.call-done = f32[8192,128]{1,0:T(8,128)} async-done(((f32[64,128]{1,0:T(8,128)}), f32[8192,128]{1,0:T(8,128)}) %all-gather.3.cloned.1.call-update) | async-done | bytes 4194320 | tf_op jit(solution)/shard_map/all_gather | solution.py:57
  262.1 2.7 gather_fusion.4
  266.0 1.4 convolution_bitcast_fusion.1
  267.5 7.7 %gather_fusion.3 = f32[256,64,128]{2,1,0:T(8,128)} fusion(f32[256,64,128]{2,1,0:T(8,128)} %all-to-all-done.1, s32[1024]{0:T(1024)S(1)} %pad_clamp_fusion.1), kind=kCustom, calls=%fused_computation.3 | custom fusion | bytes 16778240 | tf_op jit(solution)/shard_map/jit(_take)/gather | solution.py:10
  275.2 7.5 %bitcast_select_fusion.1 = f32[8,2048,128]{2,1,0:T(8,128)S(1)} fusion(pred[8,2048]{1,0:T(8,128)(4,1)S(1)} %broadcast_in_dim.94, f32[8,2048,128]{2,1,0:T(8,128)} %bitcast.57), kind=kLoop, calls=%fused_computation.6 | loop fusion | flops 2097152 | bytes 16793600 | tf_op jit(solution)/shard_map/jit(_take)/select_n | solution.py:10
  282.7 14.3 %fusion.3 = f32[8,64,128]{1,2,0:T(8,128)} fusion(f32[8,64,128]{1,2,0:T(8,128)S(1)} %copy-done.6, f32[8,2048,128]{2,1,0:T(8,128)S(1)} %bitcast_select_fusion.1, f32[8,64,2048]{2,1,0:T(8,128)S(1)} %copy-done.3), kind=kOutput, calls=%fused_computation.15 | convolution fusion | flops 1610678272 | bytes 13107200 | tf_op jit(solution)/shard_map/nkq,nqp->nkp/dot_general | solution.py:12
  297.0 1.2 copy.25
  298.8 3.3 fusion.6
  302.2 9.3 %gather_fusion.1 = f32[384,64,128]{2,1,0:T(8,128)} fusion(f32[256,64,128]{2,1,0:T(8,128)} %all-to-all-done, s32[1024]{0:T(1024)S(1)} %pad_clamp_fusion.3), kind=kCustom, calls=%fused_computation.1 | custom fusion | bytes 25167360 | tf_op jit(solution)/shard_map/jit(_take)/gather | solution.py:10
  311.5 6.1 %bitcast_select_fusion = f32[32,768,128]{2,1,0:T(8,128)S(1)} fusion(pred[32,768]{1,0:T(8,128)(4,1)S(1)} %broadcast_in_dim.86, f32[32,768,128]{2,1,0:T(8,128)} %bitcast.56), kind=kLoop, calls=%fused_computation.5 | loop fusion | flops 3145728 | bytes 25190400 | tf_op jit(solution)/shard_map/jit(_take)/select_n | solution.py:10
  317.6 10.9 %convolution_add_fusion = f32[32,128,64]{1,2,0:T(8,128)S(1)} fusion(f32[32,128,64]{1,2,0:T(8,128)S(1)} %copy-done.2, f32[32,768,128]{2,1,0:T(8,128)S(1)} %bitcast_select_fusion, f32[32,64,768]{2,1,0:T(8,128)} %param.22), kind=kOutput, calls=%fused_computation.13 | convolution fusion | flops 2416181248 | bytes 20971520 | tf_op jit(solution)/shard_map/nkq,nqp->nkp/dot_general | solution.py:12
  328.5 5.2 %multiply_bitcast_fusion = f32[32,256,128]{1,2,0:T(8,128)} fusion(f32[32,128,64]{1,2,0:T(8,128)S(1)} %convolution_add_fusion, f32[32,64,256]{2,1,0:T(8,128)S(1)} %copy-done, f32[32,256]{1,0:T(8,128)S(1)} %fusion.11), kind=kOutput, calls=%fused_computation.7 | convolution fusion | flops 806354944 | bytes 7372800 | tf_op jit(solution)/shard_map/lkm,lkp->lmp/dot_general | solution.py:77
  333.7 5.6 %copy.21 = f32[32,256,128]{2,1,0:T(8,128)} copy(f32[32,256,128]{1,2,0:T(8,128)} %multiply_bitcast_fusion) | data formatting | bytes 8388608 | tf_op jit(solution)/shard_map/mul | solution.py:77
  (60 shorter events, 7.2 us)
Async XLA Ops:
  6.5 2.3 copy-start
  6.5 9.7 %copy-start.11 = (s32[32]{0:T(128)S(1)}, s32[32]{0:T(128)}, u32[]{:S(2)}) copy-start(s32[32]{0:T(128)} %param.19) | copy-start | bytes 388
  17.3 0.7 copy-start.4
  28.4 12.6 %copy-start.5 = (f32[8,64,128]{2,0,1:T(8,128)S(1)}, f32[8,64,128]{2,0,1:T(8,128)}, u32[]{:S(2)}) copy-start(f32[8,64,128]{2,0,1:T(8,128)} %copy-done.4) | copy-start | bytes 786436
  28.4 14.8 %copy-start.12 = (s32[256]{0:T(256)S(1)}, s32[256]{0:T(256)}, u32[]{:S(2)}) copy-start(s32[256]{0:T(256)} %param.20) | copy-start | bytes 3076
  28.4 112.0 %all-to-all-start.1 = ((f32[256,64,128]{2,1,0:T(8,128)}), f32[256,64,128]{2,1,0:T(8,128)}, u32[]{:S(2)}, u32[]{:S(2)}) async-start(f32[256,64,128]{2,1,0:T(8,128)} %broadcast_select_fusion), calls=%async_computation.1 | async-start | bytes 16777216 | tf_op jit(solution)/shard_map/all_to_all | solution.py:49
  39.1 223.0 %all-gather.3.cloned.1.call-start = ((), (), s32[]{:S(2)}) async-start(), calls=%async_computation.2 | async-start | bytes 4227072 | tf_op jit(solution)/shard_map/all_gather | solution.py:57
  53.5 100.3 %copy-start.8 = (s32[32,12]{0,1:T(8,128)S(1)}, s32[32,12]{0,1:T(8,128)}, u32[]{:S(2)}) copy-start(s32[32,12]{0,1:T(8,128)} %param.21) | copy-start | bytes 4612
  53.5 100.4 %copy-start.9 = (s32[8,32]{1,0:T(8,128)S(1)}, s32[8,32]{1,0:T(8,128)}, u32[]{:S(2)}) copy-start(s32[8,32]{1,0:T(8,128)} %param.24) | copy-start | bytes 3076
  53.5 101.2 %copy-start.10 = (s32[32,4]{0,1:T(4,128)S(1)}, s32[32,4]{0,1:T(4,128)}, u32[]{:S(2)}) copy-start(s32[32,4]{0,1:T(4,128)} %param.26) | copy-start | bytes 1540
  53.5 212.5 %copy-start.7 = (f32[8,64,64]{2,1,0:T(8,128)S(1)}, f32[8,64,64]{2,1,0:T(8,128)}, u32[]{:S(2)}) copy-start(f32[8,64,64]{2,1,0:T(8,128)} %param.18) | copy-start | bytes 393220
  140.4 161.8 %all-to-all-start = ((f32[256,64,128]{2,1,0:T(8,128)}), f32[256,64,128]{2,1,0:T(8,128)}, u32[]{:S(2)}, u32[]{:S(2)}) async-start(f32[256,64,128]{2,1,0:T(8,128)} %broadcast_select_fusion.1), calls=%async_computation | async-start | bytes 16777216 | tf_op jit(solution)/shard_map/all_to_all | solution.py:40
  275.2 7.5 %copy-start.3 = (f32[8,64,2048]{2,1,0:T(8,128)S(1)}, f32[8,64,2048]{2,1,0:T(8,128)}, u32[]{:S(2)}) copy-start(f32[8,64,2048]{2,1,0:T(8,128)} %param.25) | copy-start | bytes 12582916
  275.2 7.5 %copy-start.6 = (f32[8,64,128]{1,2,0:T(8,128)S(1)}, f32[8,64,128]{1,2,0:T(8,128)}, u32[]{:S(2)}) copy-start(f32[8,64,128]{1,2,0:T(8,128)} %convolution_bitcast_fusion.1) | copy-start | bytes 786436
  282.7 16.2 %copy-start.1 = (f32[32,64,64]{2,1,0:T(8,128)S(1)}, f32[32,64,64]{2,1,0:T(8,128)}, u32[]{:S(2)}) copy-start(f32[32,64,64]{2,1,0:T(8,128)} %param.17) | copy-start | bytes 1572868
  311.5 6.1 %copy-start.2 = (f32[32,128,64]{1,2,0:T(8,128)S(1)}, f32[32,128,64]{1,2,0:T(8,128)}, u32[]{:S(2)}) copy-start(f32[32,128,64]{1,2,0:T(8,128)} %fusion.6) | copy-start | bytes 3145732
Sparse Core Ops, SparseCore 0:
  43.3 218.8 all-gather.2
where the time goes:
time: 351 us; the launch traced here: 346 us
  waiting for transfers between devices  194 us (55%)
  matrix products  47.4 us (14%)
  local copies, waits for them, and re-layouts  38.7 us (11%)
  other arithmetic  28.3 us (8%)
  starting transfers between devices  24.1 us (7%)
  between operations  13.7 us (4%)
    all_gather x1, waiting for transfers between devices, body(): lax.all_gather(coef_top[None], ('group', 'cluster'), axis=0, tiled=True)  107 us
    all_to_all x1, waiting for transfers between devices, body(): lax.all_to_all(outgoing_mid, ('group', 'cluster'), split_axis=0, concat_a...  86.9 us
    dot_general x2, matrix products, couple(): return jnp.einsum('nkq,nqp->nkp', coupling, stacked, precision=exact_mode)  25.2 us
    gather x2, local copies, waits for them, and re-layouts, couple(): stacked = jnp.take(coef, index, axis=0, mode='fill', fill_value=0.0)  17 us
    select_n x4, other arithmetic, couple(): stacked = jnp.take(coef, index, axis=0, mode='fill', fill_value=0.0)  13.6 us
    all_to_all x1, starting transfers between devices, body(): lax.all_to_all(outgoing_leaf, ('group', 'cluster'), split_axis=0, concat_...  13.4 us
    all_to_all x1, starting transfers between devices, body(): lax.all_to_all(outgoing_mid, ('group', 'cluster'), split_axis=0, concat_a...  10.7 us
  transfers between devices with their start and end apart: 3, of which 2 were waited for; matrix products, arithmetic and copies ran while one was open for 16% of the time, Pallas kernels for 0%

commit v1 on v0

--- a/solution.py
+++ b/solution.py
@@ -31,42 +31,47 @@
     leaf_count, coef_rank, leaf_points = leaf_basis.shape
     port_count = charges.shape[1]
     mid_count = mid_transfer.shape[0]
+    owners = send_leaf.shape[0] // 2
+    slots = 2
     point_mask = (jnp.arange(leaf_points, dtype=jnp.int32)[None, :] < leaf_size[:, None]).astype(
         jnp.float32
     )
     blocks = charges.reshape(leaf_count, leaf_points, port_count) * point_mask[:, :, None]
     coef_leaf = jnp.einsum("lkm,lmp->lkp", leaf_basis, blocks, precision=exact_mode)
-    outgoing_leaf = jnp.take(coef_leaf, send_leaf, axis=0, mode="fill", fill_value=0.0)
-    arrived_leaf = lax.all_to_all(
-        outgoing_leaf, ("group", "cluster"), split_axis=0, concat_axis=0, tiled=True
-    )
     moved_up = jnp.einsum("ljk,lkp->ljp", leaf_transfer, coef_leaf, precision=exact_mode)
     parent_map = (leaf_parent[None, :] == jnp.arange(mid_count, dtype=jnp.int32)[:, None]).astype(
         jnp.float32
     )
     coef_mid = jnp.einsum("ml,ljp->mjp", parent_map, moved_up, precision=exact_mode)
+    coef_top = jnp.einsum("mjk,mkp->jp", mid_transfer, coef_mid, precision=exact_mode)
+
+    outgoing_leaf = jnp.take(coef_leaf, send_leaf, axis=0, mode="fill", fill_value=0.0)
+    outgoing_leaf = outgoing_leaf.reshape(owners, slots, coef_rank, port_count)
+    top_rows = jnp.broadcast_to(coef_top[None, None], (owners, 1, coef_rank, port_count))
+    outgoing = jnp.concatenate([outgoing_leaf, top_rows], axis=1).reshape(
+        owners * (slots + 1), coef_rank, port_count
+    )
+    arrived = lax.all_to_all(outgoing, ("group", "cluster"), split_axis=0, concat_axis=0, tiled=True)
+
     outgoing_mid = jnp.take(coef_mid, send_mid, axis=0, mode="fill", fill_value=0.0)
     arrived_mid = lax.all_to_all(
         outgoing_mid, ("group", "cluster"), split_axis=0, concat_axis=0, tiled=True
     )
-    coef_top = jnp.einsum("mjk,mkp->jp", mid_transfer, coef_mid, precision=exact_mode)
-    listed = top_pairs.shape[1]
+
+    total_rows = owners * (slots + 1)
+    leaf_rows = jnp.where(
+        pair_leaf < owners * slots, pair_leaf + pair_leaf // slots, total_rows
+    )
+    near_leaf = couple(leaf_coupling, arrived, leaf_rows)
+
     position = lax.axis_index("cluster")
-    wanted = lax.dynamic_slice_in_dim(top_pairs, position, 1, 0)[0]
-    own_coupling = lax.dynamic_slice_in_dim(top_coupling, position, 1, 0)[0]
-    shard_rows = lax.all_gather(coef_top[None], ("group", "cluster"), axis=0, tiled=True)
-    inside = (wanted >= 0) & (wanted < shard_rows.shape[0])
-    taken_rows = jnp.take(shard_rows, jnp.clip(wanted, 0, shard_rows.shape[0] - 1), axis=0)
-    picked = jnp.where(
-        inside[:, None, None], taken_rows, jnp.zeros((listed, coef_rank, port_count), jnp.float32)
+    wanted = lax.dynamic_slice_in_dim(top_pairs, position, 1, 0)
+    own_coupling = lax.dynamic_slice_in_dim(top_coupling, position, 1, 0)
+    top_rows_idx = jnp.where(
+        (wanted >= 0) & (wanted < owners), wanted * (slots + 1) + slots, total_rows
     )
-    near_top = jnp.einsum(
-        "kq,qp->kp",
-        own_coupling,
-        picked.reshape(listed * coef_rank, port_count),
-        precision=exact_mode,
-    )
-    near_leaf = couple(leaf_coupling, arrived_leaf, pair_leaf)
+    near_top = couple(own_coupling, arrived, top_rows_idx)[0]
+
     near_mid = couple(mid_coupling, arrived_mid, pair_mid)
     down_mid = near_mid + jnp.einsum("mjk,jp->mkp", mid_transfer, near_top, precision=exact_mode)
     from_parent = jnp.einsum("ml,mkp->lkp", parent_map, down_mid, precision=exact_mode)

time: 351 us -> 384 us (1.094)
  waiting for transfers between devices: 194 us -> 223 us
  between operations: 13.7 us -> 0.3 us
  other arithmetic: 28.3 us -> 40.7 us
    all_to_all x1, waiting for transfers between devices: 0.01 us -> 145 us  [body(): lax.all_to_all(outgoing, ('group', 'cluster'), split_axis=0, concat_axis=...]
    all_gather x1 -> x0, waiting for transfers between devices: 107 us -> none  [body(): lax.all_gather(coef_top[None], ('group', 'cluster'), axis=0, tiled=True)]
    concatenate x0 -> x1, other arithmetic: none -> 10.2 us  [body(): jnp.concatenate([outgoing_leaf, top_rows], axis=1)]
    all_to_all x1, waiting for transfers between devices: 86.9 us -> 78 us  [body(): lax.all_to_all(outgoing_mid, ('group', 'cluster'), split_axis=0, concat_a...]
    gather x2 -> x3, local copies, waits for them, and re-layouts: 17 us -> 23.2 us  [couple(): stacked = jnp.take(coef, index, axis=0, mode='fill', fill_value=0.0)]
    dot_general x2 -> x3, matrix products: 25.2 us -> 29.1 us  [couple(): return jnp.einsum('nkq,nqp->nkp', coupling, stacked, precision=exact_mode)]
    select_n x4 -> x5, other arithmetic: 13.6 us -> 16.3 us  [couple(): stacked = jnp.take(coef, index, axis=0, mode='fill', fill_value=0.0)]
  transfers between devices with their start and end apart: 3 -> 2, of which waited for: 2 -> 2; matrix products, arithmetic and copies ran while one was open for 16% -> 11% of each run, Pallas kernels for 0% -> 0%
where the time goes in v1:
time: 384 us; the launch traced here: 379 us
  waiting for transfers between devices  223 us (58%)
  matrix products  48.9 us (13%)
  local copies, waits for them, and re-layouts  41.9 us (11%)
  other arithmetic  40.7 us (11%)
  starting transfers between devices  23.9 us (6%)
    all_to_all x1, waiting for transfers between devices, body(): lax.all_to_all(outgoing, ('group', 'cluster'), split_axis=0, concat_axis=...  145 us
    all_to_all x1, waiting for transfers between devices, body(): lax.all_to_all(outgoing_mid, ('group', 'cluster'), split_axis=0, concat_a...  78 us
    dot_general x3, matrix products, couple(): return jnp.einsum('nkq,nqp->nkp', coupling, stacked, precision=exact_mode)  29.1 us
    gather x3, local copies, waits for them, and re-layouts, couple(): stacked = jnp.take(coef, index, axis=0, mode='fill', fill_value=0.0)  23.2 us
    select_n x5, other arithmetic, couple(): stacked = jnp.take(coef, index, axis=0, mode='fill', fill_value=0.0)  16.3 us
    all_to_all x1, starting transfers between devices, body(): lax.all_to_all(outgoing, ('group', 'cluster'), split_axis=0, concat_axis=...  13.2 us
    all_to_all x1, starting transfers between devices, body(): lax.all_to_all(outgoing_mid, ('group', 'cluster'), split_axis=0, concat_a...  10.7 us
    concatenate x1, other arithmetic, body(): jnp.concatenate([outgoing_leaf, top_rows], axis=1)  10.2 us
  transfers between devices with their start and end apart: 2, of which 2 were waited for; matrix products, arithmetic and copies ran while one was open for 11% of the time, Pallas kernels for 0%

profile of v1, /device:TPU:24, one launch (start us, length us, event | category | flops | bytes accessed | tf_op | source)
XLA Modules:
  0.0 379.0 jit_solution(4665250790642648612)
XLA Ops:
  2.3 5.1 %fusion = f32[32,128,64]{1,2,0:T(8,128)S(1)} fusion(f32[32,64,256]{2,1,0:T(8,128)S(1)} %copy-done, f32[32,256,128]{2,1,0:T(8,128)} %bitcast.59, f32[32,256]{1,0:T(8,128)S(1)} %fusion.11), kind=kOutput, calls=%fused_computation.11 | convolution fusion | flops 806354944 | bytes 7372800 | tf_op jit(solution)/shard_map/lkm,lmp->lkp/dot_general | solution.py:40
  7.4 2.3 fusion.23
  11.5 4.4 %gather_fusion.2 = f32[256,64,128]{2,1,0:T(8,128)} fusion(f32[8,64,128]{2,1,0:T(8,128)S(1)} %copy.20, s32[1024]{0:T(1024)S(1)} %pad_clamp_fusion.2), kind=kCustom, calls=%fused_computation.2 | custom fusion | bytes 16778240 | tf_op jit(solution)/shard_map/jit(_take)/gather | solution.py:56
  15.9 6.0 %broadcast_select_fusion = f32[256,64,128]{2,1,0:T(8,128)} fusion(f32[256,64,128]{2,1,0:T(8,128)} %gather_fusion.2, pred[256]{0:T(512)(128)(4,1)S(1)} %compare_and_fusion.2), kind=kLoop, calls=%fused_computation.9 | loop fusion | flops 2097152 | bytes 16777472 | tf_op jit(solution)/shard_map/jit(_take)/select_n | solution.py:56
  21.8 10.7 %all-to-all-start.1 = ((f32[256,64,128]{2,1,0:T(8,128)}), f32[256,64,128]{2,1,0:T(8,128)}, u32[]{:S(2)}, u32[]{:S(2)}) async-start(f32[256,64,128]{2,1,0:T(8,128)} %broadcast_select_fusion), calls=%async_computation.1 | async-start | bytes 16777216 | tf_op jit(solution)/shard_map/all_to_all | solution.py:57
  33.7 4.3 %gather_fusion = f32[256,64,128]{2,1,0:T(8,128)} fusion(f32[32,64,128]{2,1,0:T(8,128)S(1)} %bitcast.54, s32[1024]{0:T(1024)S(1)} %pad_clamp_fusion.4), kind=kCustom, calls=%fused_computation | custom fusion | bytes 16778240 | tf_op jit(solution)/shard_map/jit(_take)/gather | solution.py:48
  38.0 1.5 convolution_bitcast_fusion.3
  39.6 5.8 %broadcast_select_fusion.1 = f32[128,2,64,128]{3,2,1,0:T(8,128)} fusion(f32[128,2,64,128]{3,2,1,0:T(8,128)} %bitcast.58, pred[128,2]{1,0:T(8,128)(4,1)S(1)} %broadcast_in_dim.94), kind=kLoop, calls=%fused_computation.10 | loop fusion | flops 2097152 | bytes 16777472 | tf_op jit(solution)/shard_map/jit(_take)/select_n | solution.py:48
  45.9 10.2 %pad_maximum_fusion = f32[128,3,64,128]{3,2,1,0:T(8,128)} fusion(f32[128,1,64,128]{3,2,1,0:T(8,128)S(1)} %broadcast_in_dim.98, f32[128,2,64,128]{3,2,1,0:T(8,128)} %broadcast_select_fusion.1), kind=kLoop, calls=%fused_computation.5 | loop fusion | flops 3145728 | bytes 25165824 | tf_op jit(solution)/shard_map/concatenate | solution.py:51
  56.0 78.0 %all-to-all-done.1 = f32[256,64,128]{2,1,0:T(8,128)} async-done(((f32[256,64,128]{2,1,0:T(8,128)}), f32[256,64,128]{2,1,0:T(8,128)}, u32[]{:S(2)}, u32[]{:S(2)}) %all-to-all-start.1) | async-done | bytes 8388640 | tf_op jit(solution)/shard_map/all_to_all | solution.py:57
  134.1 13.2 %all-to-all-start = ((f32[384,64,128]{2,1,0:T(8,128)}), f32[384,64,128]{2,1,0:T(8,128)}, u32[]{:S(2)}, u32[]{:S(2)}) async-start(f32[384,64,128]{2,1,0:T(8,128)} %bitcast.55), calls=%async_computation | async-start | bytes 25165824 | tf_op jit(solution)/shard_map/all_to_all | solution.py:54
  148.6 7.7 %gather_fusion.3 = f32[256,64,128]{2,1,0:T(8,128)} fusion(f32[256,64,128]{2,1,0:T(8,128)} %all-to-all-done.1, s32[1024]{0:T(1024)S(1)} %pad_clamp_fusion.1), kind=kCustom, calls=%fused_computation.3 | custom fusion | bytes 16778240 | tf_op jit(solution)/shard_map/jit(_take)/gather | solution.py:10
  156.2 10.0 %bitcast_select_fusion.1 = f32[8,2048,128]{2,1,0:T(8,128)} fusion(pred[8,2048]{1,0:T(8,128)(4,1)S(1)} %broadcast_in_dim.102, f32[8,2048,128]{2,1,0:T(8,128)} %bitcast.57), kind=kLoop, calls=%fused_computation.7 | loop fusion | flops 2097152 | bytes 16793600 | tf_op jit(solution)/shard_map/jit(_take)/select_n | solution.py:10
  166.2 145.2 %all-to-all-done = f32[384,64,128]{2,1,0:T(8,128)} async-done(((f32[384,64,128]{2,1,0:T(8,128)}), f32[384,64,128]{2,1,0:T(8,128)}, u32[]{:S(2)}, u32[]{:S(2)}) %all-to-all-start) | async-done | bytes 12582944 | tf_op jit(solution)/shard_map/all_to_all | solution.py:54
  311.4 5.1 %gather_fusion.4 = f32[4,64,128]{2,1,0:T(8,128)S(1)} fusion(f32[384,64,128]{2,1,0:T(8,128)} %all-to-all-done, s32[1024]{0:T(1024)S(1)} %pad_clamp_fusion), kind=kCustom, calls=%fused_computation.4 | custom fusion | bytes 262160 | tf_op jit(solution)/shard_map/jit(_take)/gather | solution.py:10
  316.7 1.1 convolution_bitcast_fusion.2
  318.5 17.0 %fusion.3 = f32[8,64,128]{1,2,0:T(8,128)} fusion(f32[8,64,128]{1,2,0:T(8,128)S(1)} %convolution_bitcast_fusion.1, f32[8,2048,128]{2,1,0:T(8,128)} %bitcast_select_fusion.1, f32[8,64,2048]{2,1,0:T(8,128)} %param.25), kind=kOutput, calls=%fused_computation.16 | convolution fusion | flops 1610678272 | bytes 13107200 | tf_op jit(solution)/shard_map/nkq,nqp->nkp/dot_general | solution.py:12
  335.5 1.2 copy.25
  337.4 3.3 fusion.6
  340.7 10.4 %gather_fusion.1 = f32[384,64,128]{2,1,0:T(8,128)} fusion(f32[384,64,128]{2,1,0:T(8,128)} %all-to-all-done, s32[1024]{0:T(1024)S(1)} %pad_clamp_fusion.3), kind=kCustom, calls=%fused_computation.1 | custom fusion | bytes 25167360 | tf_op jit(solution)/shard_map/jit(_take)/gather | solution.py:10
  351.1 6.1 %bitcast_select_fusion = f32[32,768,128]{2,1,0:T(8,128)S(1)} fusion(pred[32,768]{1,0:T(8,128)(4,1)S(1)} %broadcast_in_dim.92, f32[32,768,128]{2,1,0:T(8,128)} %bitcast.56), kind=kLoop, calls=%fused_computation.6 | loop fusion | flops 3145728 | bytes 25190400 | tf_op jit(solution)/shard_map/jit(_take)/select_n | solution.py:10
  357.3 10.9 %convolution_add_fusion = f32[32,128,64]{1,2,0:T(8,128)S(1)} fusion(f32[32,128,64]{1,2,0:T(8,128)S(1)} %copy-done.2, f32[32,768,128]{2,1,0:T(8,128)S(1)} %bitcast_select_fusion, f32[32,64,768]{2,1,0:T(8,128)} %param.22), kind=kOutput, calls=%fused_computation.14 | convolution fusion | flops 2416181248 | bytes 20971520 | tf_op jit(solution)/shard_map/nkq,nqp->nkp/dot_general | solution.py:12
  368.2 5.2 %multiply_bitcast_fusion = f32[32,256,128]{1,2,0:T(8,128)} fusion(f32[32,128,64]{1,2,0:T(8,128)S(1)} %convolution_add_fusion, f32[32,64,256]{2,1,0:T(8,128)S(1)} %copy-done, f32[32,256]{1,0:T(8,128)S(1)} %fusion.11), kind=kOutput, calls=%fused_computation.8 | convolution fusion | flops 806354944 | bytes 7372800 | tf_op jit(solution)/shard_map/lkm,lkp->lmp/dot_general | solution.py:82
  373.4 5.6 %copy.21 = f32[32,256,128]{2,1,0:T(8,128)} copy(f32[32,256,128]{1,2,0:T(8,128)} %multiply_bitcast_fusion) | data formatting | bytes 8388608 | tf_op jit(solution)/shard_map/mul | solution.py:82
  (55 shorter events, 8.2 us)
Async XLA Ops:
  0.0 2.2 copy-start
  0.0 9.7 %copy-start.9 = (s32[32]{0:T(128)S(1)}, s32[32]{0:T(128)}, u32[]{:S(2)}) copy-start(s32[32]{0:T(128)} %param.19) | copy-start | bytes 388
  10.7 0.7 copy-start.3
  21.8 10.7 %copy-start.5 = (f32[8,64,64]{2,1,0:T(8,128)S(1)}, f32[8,64,64]{2,1,0:T(8,128)}, u32[]{:S(2)}) copy-start(f32[8,64,64]{2,1,0:T(8,128)} %param.18) | copy-start | bytes 393220
  21.8 11.6 %copy-start.11 = (s32[256]{0:T(256)S(1)}, s32[256]{0:T(256)}, u32[]{:S(2)}) copy-start(s32[256]{0:T(256)} %param.20) | copy-start | bytes 3076
  21.8 112.2 %all-to-all-start.1 = ((f32[256,64,128]{2,1,0:T(8,128)}), f32[256,64,128]{2,1,0:T(8,128)}, u32[]{:S(2)}, u32[]{:S(2)}) async-start(f32[256,64,128]{2,1,0:T(8,128)} %broadcast_select_fusion), calls=%async_computation.1 | async-start | bytes 16777216 | tf_op jit(solution)/shard_map/all_to_all | solution.py:57
  33.6 4.4 %copy-start.4 = (f32[8,64,128]{2,0,1:T(8,128)S(1)}, f32[8,64,128]{2,0,1:T(8,128)}, u32[]{:S(2)}) copy-start(f32[8,64,128]{2,0,1:T(8,128)} %copy-done.3) | copy-start | bytes 786436
  134.1 13.2 %copy-start.10 = (s32[32,4]{0,1:T(4,128)S(1)}, s32[32,4]{0,1:T(4,128)}, u32[]{:S(2)}) copy-start(s32[32,4]{0,1:T(4,128)} %param.26) | copy-start | bytes 1540
  134.1 13.5 %copy-start.7 = (s32[8,32]{1,0:T(8,128)S(1)}, s32[8,32]{1,0:T(8,128)}, u32[]{:S(2)}) copy-start(s32[8,32]{1,0:T(8,128)} %param.24) | copy-start | bytes 3076
  134.1 13.8 %copy-start.8 = (s32[32,12]{0,1:T(8,128)S(1)}, s32[32,12]{0,1:T(8,128)}, u32[]{:S(2)}) copy-start(s32[32,12]{0,1:T(8,128)} %param.21) | copy-start | bytes 4612
  134.1 177.4 %all-to-all-start = ((f32[384,64,128]{2,1,0:T(8,128)}), f32[384,64,128]{2,1,0:T(8,128)}, u32[]{:S(2)}, u32[]{:S(2)}) async-start(f32[384,64,128]{2,1,0:T(8,128)} %bitcast.55), calls=%async_computation | async-start | bytes 25165824 | tf_op jit(solution)/shard_map/all_to_all | solution.py:54
  156.2 161.6 %copy-start.6 = (f32[8,64,64]{2,1,0:T(8,128)S(1)}, f32[8,64,64]{2,1,0:T(8,128)}, u32[]{:S(2)}) copy-start(f32[8,64,64]{2,1,0:T(8,128)} %param.18) | copy-start | bytes 393220
  316.7 20.7 %copy-start.1 = (f32[32,64,64]{2,1,0:T(8,128)S(1)}, f32[32,64,64]{2,1,0:T(8,128)}, u32[]{:S(2)}) copy-start(f32[32,64,64]{2,1,0:T(8,128)} %param.17) | copy-start | bytes 1572868
  351.1 6.1 %copy-start.2 = (f32[32,128,64]{1,2,0:T(8,128)S(1)}, f32[32,128,64]{1,2,0:T(8,128)}, u32[]{:S(2)}) copy-start(f32[32,128,64]{1,2,0:T(8,128)} %fusion.6) | copy-start | bytes 3145732

commit v2 on v0

--- a/solution.py
+++ b/solution.py
@@ -31,25 +31,31 @@
     leaf_count, coef_rank, leaf_points = leaf_basis.shape
     port_count = charges.shape[1]
     mid_count = mid_transfer.shape[0]
+    owners = send_leaf.shape[0] // 2
+    slots = 2
     point_mask = (jnp.arange(leaf_points, dtype=jnp.int32)[None, :] < leaf_size[:, None]).astype(
         jnp.float32
     )
     blocks = charges.reshape(leaf_count, leaf_points, port_count) * point_mask[:, :, None]
     coef_leaf = jnp.einsum("lkm,lmp->lkp", leaf_basis, blocks, precision=exact_mode)
-    outgoing_leaf = jnp.take(coef_leaf, send_leaf, axis=0, mode="fill", fill_value=0.0)
-    arrived_leaf = lax.all_to_all(
-        outgoing_leaf, ("group", "cluster"), split_axis=0, concat_axis=0, tiled=True
-    )
     moved_up = jnp.einsum("ljk,lkp->ljp", leaf_transfer, coef_leaf, precision=exact_mode)
     parent_map = (leaf_parent[None, :] == jnp.arange(mid_count, dtype=jnp.int32)[:, None]).astype(
         jnp.float32
     )
     coef_mid = jnp.einsum("ml,ljp->mjp", parent_map, moved_up, precision=exact_mode)
+    coef_top = jnp.einsum("mjk,mkp->jp", mid_transfer, coef_mid, precision=exact_mode)
+
+    outgoing_leaf = jnp.take(coef_leaf, send_leaf, axis=0, mode="fill", fill_value=0.0)
     outgoing_mid = jnp.take(coef_mid, send_mid, axis=0, mode="fill", fill_value=0.0)
-    arrived_mid = lax.all_to_all(
-        outgoing_mid, ("group", "cluster"), split_axis=0, concat_axis=0, tiled=True
-    )
-    coef_top = jnp.einsum("mjk,mkp->jp", mid_transfer, coef_mid, precision=exact_mode)
+    outgoing = jnp.concatenate(
+        [
+            outgoing_leaf.reshape(owners, slots, coef_rank, port_count),
+            outgoing_mid.reshape(owners, slots, coef_rank, port_count),
+        ],
+        axis=1,
+    ).reshape(owners * 2 * slots, coef_rank, port_count)
+    arrived = lax.all_to_all(outgoing, ("group", "cluster"), split_axis=0, concat_axis=0, tiled=True)
+
     listed = top_pairs.shape[1]
     position = lax.axis_index("cluster")
     wanted = lax.dynamic_slice_in_dim(top_pairs, position, 1, 0)[0]
@@ -66,8 +72,14 @@
         picked.reshape(listed * coef_rank, port_count),
         precision=exact_mode,
     )
-    near_leaf = couple(leaf_coupling, arrived_leaf, pair_leaf)
-    near_mid = couple(mid_coupling, arrived_mid, pair_mid)
+
+    total_rows = owners * 2 * slots
+    live_leaf = pair_leaf < owners * slots
+    leaf_rows = jnp.where(live_leaf, pair_leaf + (pair_leaf // slots) * slots, total_rows)
+    near_leaf = couple(leaf_coupling, arrived, leaf_rows)
+    live_mid = pair_mid < owners * slots
+    mid_rows = jnp.where(live_mid, pair_mid + (pair_mid // slots + 1) * slots, total_rows)
+    near_mid = couple(mid_coupling, arrived, mid_rows)
     down_mid = near_mid + jnp.einsum("mjk,jp->mkp", mid_transfer, near_top, precision=exact_mode)
     from_parent = jnp.einsum("ml,mkp->lkp", parent_map, down_mid, precision=exact_mode)
     down_leaf = near_leaf + jnp.einsum(

time: 351 us -> 384 us (1.094)
  waiting for transfers between devices: 194 us -> 235 us
  starting transfers between devices: 24.1 us -> 10.8 us
    all_gather x1, waiting for transfers between devices: 107 us -> 235 us  [body(): lax.all_gather(coef_top[None], ('group', 'cluster'), axis=0, tiled=True)]
    all_to_all x2 -> x1, waiting for transfers between devices: 86.9 us -> 0.01 us  [body(): lax.all_to_all(outgoing, ('group', 'cluster'), split_axis=0, concat_axis=...]
    all_to_all x2 -> x1, starting transfers between devices: 24.1 us -> 10.7 us  [body(): lax.all_to_all(outgoing, ('group', 'cluster'), split_axis=0, concat_axis=...]
    concatenate x0 -> x1, other arithmetic: none -> 6.06 us  [body(): jnp.concatenate([outgoing_leaf.reshape(owners, slots, coef_rank, port_cou...]
    select_n x2 -> x1, other arithmetic: 5.98 us -> 0.83 us  [body(): jnp.take(coef_leaf, send_leaf, axis=0, mode='fill', fill_value=0.0)]
    gather x2, local copies, waits for them, and re-layouts: 17 us -> 21.8 us  [couple(): stacked = jnp.take(coef, index, axis=0, mode='fill', fill_value=0.0)]
    select_n x4 -> x2, other arithmetic: 13.6 us -> 13.6 us  [couple(): stacked = jnp.take(coef, index, axis=0, mode='fill', fill_value=0.0)]
  transfers between devices with their start and end apart: 3 -> 2, of which waited for: 2 -> 1; matrix products, arithmetic and copies ran while one was open for 16% -> 2% of each run, Pallas kernels for 0% -> 0%
where the time goes in v2:
time: 384 us; the launch traced here: 379 us
  waiting for transfers between devices  235 us (61%)
  matrix products  46.5 us (12%)
  local copies, waits for them, and re-layouts  42.1 us (11%)
  other arithmetic  30.3 us (8%)
  between operations  13.7 us (4%)
  starting transfers between devices  10.8 us (3%)
    all_gather x1, waiting for transfers between devices, body(): lax.all_gather(coef_top[None], ('group', 'cluster'), axis=0, tiled=True)  235 us
    dot_general x2, matrix products, couple(): return jnp.einsum('nkq,nqp->nkp', coupling, stacked, precision=exact_mode)  25.2 us
    gather x2, local copies, waits for them, and re-layouts, couple(): stacked = jnp.take(coef, index, axis=0, mode='fill', fill_value=0.0)  21.8 us
    select_n x2, other arithmetic, couple(): stacked = jnp.take(coef, index, axis=0, mode='fill', fill_value=0.0)  13.6 us
    all_to_all x1, starting transfers between devices, body(): lax.all_to_all(outgoing, ('group', 'cluster'), split_axis=0, concat_axis=...  10.7 us
  transfers between devices with their start and end apart: 2, of which 1 were waited for; matrix products, arithmetic and copies ran while one was open for 2% of the time, Pallas kernels for 0%

profile of v2, /device:TPU:24, one launch (start us, length us, event | category | flops | bytes accessed | tf_op | source)
XLA Modules:
  0.0 378.9 jit_solution(8333064227275518542)
XLA Ops:
  6.5 0.8 compare_select_fusion.3
  10.2 5.1 %fusion = f32[32,128,64]{1,2,0:T(8,128)S(1)} fusion(f32[32,64,256]{2,1,0:T(8,128)S(1)} %copy-done, f32[32,256,128]{2,1,0:T(8,128)} %bitcast.64, f32[32,256]{1,0:T(8,128)S(1)} %fusion.11), kind=kOutput, calls=%fused_computation.11 | convolution fusion | flops 806354944 | bytes 7372800 | tf_op jit(solution)/shard_map/lkm,lmp->lkp/dot_general | solution.py:40
  15.3 2.3 fusion.31
  17.6 1.0 fusion.4
  19.8 4.4 %gather_fusion.1 = f32[256,64,128]{2,1,0:T(8,128)} fusion(f32[8,64,128]{2,1,0:T(8,128)S(1)} %copy.19, s32[1024]{0:T(1024)S(1)} %pad_clamp_fusion.3), kind=kCustom, calls=%fused_computation.1 | custom fusion | bytes 16778240 | tf_op jit(solution)/shard_map/jit(_take)/gather | solution.py:49
  24.1 4.4 %gather_fusion = f32[256,64,128]{2,1,0:T(8,128)} fusion(f32[32,64,128]{2,1,0:T(8,128)S(1)} %bitcast.58, s32[1024]{0:T(1024)S(1)} %pad_clamp_fusion.4), kind=kCustom, calls=%fused_computation | custom fusion | bytes 16778240 | tf_op jit(solution)/shard_map/jit(_take)/gather | solution.py:48
  28.5 6.5 %broadcast_select_fusion = (f32[128,2,64,128]{3,2,1,0:T(8,128)S(1)}, f32[128,2,64,128]{3,2,1,0:T(8,128)S(1)}) fusion(f32[128,2,64,128]{3,2,1,0:T(8,128)} %bitcast.61, pred[128,2]{1,0:T(8,128)(4,1)S(1)} %broadcast_in_dim.105, f32[128,2,64,128]{3,2,1,0:T(8,128)} %bitcast.62, pred[128,2]{1,0:T(8,128)(4,1)S(1)} %broadcast_in_dim.101), kind=kLoop, calls=%fused_computation.9 | loop fusion | flops 4194304 | bytes 33554944 | tf_op jit(solution)/shard_map/jit(_take)/select_n | solution.py:49
  35.0 6.1 %pad_maximum_fusion = f32[128,4,64,128]{3,2,1,0:T(8,128)} fusion(f32[128,2,64,128]{3,2,1,0:T(8,128)S(1)} %get-tuple-element.9, f32[128,2,64,128]{3,2,1,0:T(8,128)S(1)} %get-tuple-element.10), kind=kLoop, calls=%fused_computation.5 | loop fusion | flops 4194304 | bytes 33554432 | tf_op jit(solution)/shard_map/concatenate | solution.py:50
  41.1 10.7 %all-to-all-start = ((f32[512,64,128]{2,1,0:T(8,128)}), f32[512,64,128]{2,1,0:T(8,128)}, u32[]{:S(2)}, u32[]{:S(2)}) async-start(f32[512,64,128]{2,1,0:T(8,128)} %bitcast.59), calls=%async_computation | async-start | bytes 33554432 | tf_op jit(solution)/shard_map/all_to_all | solution.py:57
  52.1 1.2 convolution_bitcast_fusion.3
  54.7 235.5 %all-gather.3.cloned.1.call-done = f32[8192,128]{1,0:T(8,128)} async-done(((f32[64,128]{1,0:T(8,128)}), f32[8192,128]{1,0:T(8,128)}) %all-gather.3.cloned.1.call-update) | async-done | bytes 4194320 | tf_op jit(solution)/shard_map/all_gather | solution.py:63
  290.2 2.7 gather_fusion.4
  293.0 1.1 convolution_bitcast_fusion.2
  294.1 1.4 convolution_bitcast_fusion.1
  295.5 10.1 %gather_fusion.3 = f32[256,64,128]{2,1,0:T(8,128)} fusion(f32[512,64,128]{2,1,0:T(8,128)} %all-to-all-done, s32[1024]{0:T(1024)S(1)} %pad_clamp_fusion.1), kind=kCustom, calls=%fused_computation.3 | custom fusion | bytes 16778240 | tf_op jit(solution)/shard_map/jit(_take)/gather | solution.py:10
  305.6 7.5 %bitcast_select_fusion.1 = f32[8,2048,128]{2,1,0:T(8,128)S(1)} fusion(pred[8,2048]{1,0:T(8,128)(4,1)S(1)} %broadcast_in_dim.112, f32[8,2048,128]{2,1,0:T(8,128)} %bitcast.63), kind=kLoop, calls=%fused_computation.7 | loop fusion | flops 2097152 | bytes 16793600 | tf_op jit(solution)/shard_map/jit(_take)/select_n | solution.py:10
  313.1 14.3 %fusion.3 = f32[8,64,128]{1,2,0:T(8,128)} fusion(f32[8,64,128]{1,2,0:T(8,128)S(1)} %copy-done.6, f32[8,2048,128]{2,1,0:T(8,128)S(1)} %bitcast_select_fusion.1, f32[8,64,2048]{2,1,0:T(8,128)S(1)} %copy-done.3), kind=kOutput, calls=%fused_computation.16 | convolution fusion | flops 1610678272 | bytes 13107200 | tf_op jit(solution)/shard_map/nkq,nqp->nkp/dot_general | solution.py:12
  327.4 1.2 copy.26
  329.3 3.3 fusion.6
  332.6 11.7 %gather_fusion.2 = f32[384,64,128]{2,1,0:T(8,128)} fusion(f32[512,64,128]{2,1,0:T(8,128)} %all-to-all-done, s32[1024]{0:T(1024)S(1)} %pad_clamp_fusion.2), kind=kCustom, calls=%fused_computation.2 | custom fusion | bytes 25167360 | tf_op jit(solution)/shard_map/jit(_take)/gather | solution.py:10
  344.3 6.1 %bitcast_select_fusion = f32[32,768,128]{2,1,0:T(8,128)S(1)} fusion(pred[32,768]{1,0:T(8,128)(4,1)S(1)} %broadcast_in_dim.99, f32[32,768,128]{2,1,0:T(8,128)} %bitcast.60), kind=kLoop, calls=%fused_computation.6 | loop fusion | flops 3145728 | bytes 25190400 | tf_op jit(solution)/shard_map/jit(_take)/select_n | solution.py:10
  350.4 10.9 %convolution_add_fusion = f32[32,128,64]{1,2,0:T(8,128)S(1)} fusion(f32[32,128,64]{1,2,0:T(8,128)S(1)} %copy-done.2, f32[32,768,128]{2,1,0:T(8,128)S(1)} %bitcast_select_fusion, f32[32,64,768]{2,1,0:T(8,128)} %param.22), kind=kOutput, calls=%fused_computation.14 | convolution fusion | flops 2416181248 | bytes 20971520 | tf_op jit(solution)/shard_map/nkq,nqp->nkp/dot_general | solution.py:12
  361.3 5.2 %multiply_bitcast_fusion = f32[32,256,128]{1,2,0:T(8,128)} fusion(f32[32,128,64]{1,2,0:T(8,128)S(1)} %convolution_add_fusion, f32[32,64,256]{2,1,0:T(8,128)S(1)} %copy-done, f32[32,256]{1,0:T(8,128)S(1)} %fusion.11), kind=kOutput, calls=%fused_computation.8 | convolution fusion | flops 806354944 | bytes 7372800 | tf_op jit(solution)/shard_map/lkm,lkp->lmp/dot_general | solution.py:89
  366.5 5.6 %copy.22 = f32[32,256,128]{2,1,0:T(8,128)} copy(f32[32,256,128]{1,2,0:T(8,128)} %multiply_bitcast_fusion) | data formatting | bytes 8388608 | tf_op jit(solution)/shard_map/mul | solution.py:89
  (56 shorter events, 6.1 us)
Async XLA Ops:
  6.5 3.6 copy-start
  6.5 11.1 %copy-start.11 = (s32[32]{0:T(128)S(1)}, s32[32]{0:T(128)}, u32[]{:S(2)}) copy-start(s32[32]{0:T(128)} %param.19) | copy-start | bytes 388
  18.6 0.7 copy-start.4
  41.1 10.8 %copy-start.7 = (f32[8,64,64]{2,1,0:T(8,128)S(1)}, f32[8,64,64]{2,1,0:T(8,128)}, u32[]{:S(2)}) copy-start(f32[8,64,64]{2,1,0:T(8,128)} %param.18) | copy-start | bytes 393220
  41.1 11.0 %copy-start.5 = (f32[8,64,128]{2,0,1:T(8,128)S(1)}, f32[8,64,128]{2,0,1:T(8,128)}, u32[]{:S(2)}) copy-start(f32[8,64,128]{2,0,1:T(8,128)} %copy-done.4) | copy-start | bytes 786436
  41.1 12.2 %copy-start.10 = (s32[8,32]{1,0:T(8,128)S(1)}, s32[8,32]{1,0:T(8,128)}, u32[]{:S(2)}) copy-start(s32[8,32]{1,0:T(8,128)} %param.24) | copy-start | bytes 3076
  41.1 12.6 %copy-start.9 = (s32[32,12]{0,1:T(8,128)S(1)}, s32[32,12]{0,1:T(8,128)}, u32[]{:S(2)}) copy-start(s32[32,12]{0,1:T(8,128)} %param.21) | copy-start | bytes 4612
  41.1 13.2 %copy-start.8 = (s32[32,4]{0,1:T(4,128)S(1)}, s32[32,4]{0,1:T(4,128)}, u32[]{:S(2)}) copy-start(s32[32,4]{0,1:T(4,128)} %param.26) | copy-start | bytes 1540
  41.1 254.4 %all-to-all-start = ((f32[512,64,128]{2,1,0:T(8,128)}), f32[512,64,128]{2,1,0:T(8,128)}, u32[]{:S(2)}, u32[]{:S(2)}) async-start(f32[512,64,128]{2,1,0:T(8,128)} %bitcast.59), calls=%async_computation | async-start | bytes 33554432 | tf_op jit(solution)/shard_map/all_to_all | solution.py:57
  51.9 238.3 %all-gather.3.cloned.1.call-start = ((), (), s32[]{:S(2)}) async-start(), calls=%async_computation.1 | async-start | bytes 4227072 | tf_op jit(solution)/shard_map/all_gather | solution.py:63
  305.6 7.5 %copy-start.3 = (f32[8,64,2048]{2,1,0:T(8,128)S(1)}, f32[8,64,2048]{2,1,0:T(8,128)}, u32[]{:S(2)}) copy-start(f32[8,64,2048]{2,1,0:T(8,128)} %param.25) | copy-start | bytes 12582916
  305.6 7.5 %copy-start.6 = (f32[8,64,128]{1,2,0:T(8,128)S(1)}, f32[8,64,128]{1,2,0:T(8,128)}, u32[]{:S(2)}) copy-start(f32[8,64,128]{1,2,0:T(8,128)} %convolution_bitcast_fusion.1) | copy-start | bytes 786436
  313.1 16.2 %copy-start.1 = (f32[32,64,64]{2,1,0:T(8,128)S(1)}, f32[32,64,64]{2,1,0:T(8,128)}, u32[]{:S(2)}) copy-start(f32[32,64,64]{2,1,0:T(8,128)} %param.17) | copy-start | bytes 1572868
  344.3 6.1 %copy-start.2 = (f32[32,128,64]{1,2,0:T(8,128)S(1)}, f32[32,128,64]{1,2,0:T(8,128)}, u32[]{:S(2)}) copy-start(f32[32,128,64]{1,2,0:T(8,128)} %fusion.6) | copy-start | bytes 3145732
Sparse Core Ops, SparseCore 0:
  55.8 234.2 all-gather.2

commit v3 on v2

--- a/solution.py
+++ b/solution.py
@@ -1,6 +1,10 @@
+import functools
+
 import jax
 import jax.numpy as jnp
 from jax import lax
+from jax.experimental import pallas as pl
+from jax.experimental.pallas import tpu as pltpu
 from jax.sharding import PartitionSpec as P
 
 exact_mode = lax.Precision.HIGHEST
@@ -10,6 +14,49 @@
     stacked = jnp.take(coef, index, axis=0, mode="fill", fill_value=0.0)
     stacked = stacked.reshape(index.shape[0], index.shape[1] * coef.shape[1], coef.shape[2])
     return jnp.einsum("nkq,nqp->nkp", coupling, stacked, precision=exact_mode)
+
+
+def couple_kernel(nb, listed, total, idx_ref, arrived_ref, coupling_ref, out_ref):
+    i = pl.program_id(0)
+    rank = arrived_ref.shape[1]
+    for t in range(nb):
+        acc = jnp.zeros(out_ref.shape[1:], jnp.float32)
+        for k in range(listed):
+            r = idx_ref[(i * nb + t) * listed + k]
+            valid = r < total
+            blk = arrived_ref[jnp.minimum(r, total - 1)]
+            c = coupling_ref[t, :, k * rank : (k + 1) * rank]
+            prod = jnp.dot(c, blk, precision=exact_mode, preferred_element_type=jnp.float32)
+            acc = acc + jnp.where(valid, prod, 0.0)
+        out_ref[t] = acc
+
+
+def couple_pallas(coupling, arrived, rows, nb):
+    n, rank, width = coupling.shape
+    listed = rows.shape[1]
+    total, _, ports = arrived.shape
+    grid_spec = pltpu.PrefetchScalarGridSpec(
+        num_scalar_prefetch=1,
+        grid=(n // nb,),
+        in_specs=[
+            pl.BlockSpec(
+                (total, rank, ports), lambda i, idx: (0, 0, 0), pipeline_mode=pl.Buffered(1)
+            ),
+            pl.BlockSpec((nb, rank, width), lambda i, idx: (i, 0, 0)),
+        ],
+        out_specs=pl.BlockSpec((nb, rank, ports), lambda i, idx: (i, 0, 0)),
+    )
+    return pl.pallas_call(
+        functools.partial(couple_kernel, nb, listed, total),
+        grid_spec=grid_spec,
+        out_shape=jax.ShapeDtypeStruct((n, rank, ports), jnp.float32),
+        compiler_params=pltpu.CompilerParams(vmem_limit_bytes=60 * 1024 * 1024),
+        cost_estimate=pl.CostEstimate(
+            flops=2 * n * rank * width * ports,
+            bytes_accessed=4 * (n * rank * width + total * rank * ports + n * rank * ports),
+            transcendentals=0,
+        ),
+    )(rows.reshape(-1), arrived, coupling)
 
 
 def body(
@@ -76,10 +123,10 @@
     total_rows = owners * 2 * slots
     live_leaf = pair_leaf < owners * slots
     leaf_rows = jnp.where(live_leaf, pair_leaf + (pair_leaf // slots) * slots, total_rows)
-    near_leaf = couple(leaf_coupling, arrived, leaf_rows)
+    near_leaf = couple_pallas(leaf_coupling, arrived, leaf_rows, 4)
     live_mid = pair_mid < owners * slots
     mid_rows = jnp.where(live_mid, pair_mid + (pair_mid // slots + 1) * slots, total_rows)
-    near_mid = couple(mid_coupling, arrived, mid_rows)
+    near_mid = couple_pallas(mid_coupling, arrived, mid_rows, 2)
     down_mid = near_mid + jnp.einsum("mjk,jp->mkp", mid_transfer, near_top, precision=exact_mode)
     from_parent = jnp.einsum("ml,mkp->lkp", parent_map, down_mid, precision=exact_mode)
     down_leaf = near_leaf + jnp.einsum(

time: 384 us -> 358 us (0.932)
  Pallas kernels: 0 us -> 34.6 us
  matrix products: 46.5 us -> 21.8 us
  local copies, waits for them, and re-layouts: 42.1 us -> 19.7 us
  other arithmetic: 30.3 us -> 16.8 us
    pallas_call x0 -> x2, Pallas kernels: none -> 34.6 us  [couple_pallas(): pl.pallas_call(functools.partial(couple_kernel, nb, listed, total), grid_...]
    dot_general x2 -> x0, matrix products: 25.2 us -> none  [couple(): return jnp.einsum('nkq,nqp->nkp', coupling, stacked, precision=exact_mode)]
    gather x2 -> x0, local copies, waits for them, and re-layouts: 21.8 us -> none  [couple(): stacked = jnp.take(coef, index, axis=0, mode='fill', fill_value=0.0)]
    select_n x2, other arithmetic: 13.6 us -> 0.02 us  [the longest x1 0.01 us: body(): jnp.where(live_mid, pair_mid + (pair_mid // slots + 1) * slots, total_rows)]
where the time goes in v3:
time: 358 us; the launch traced here: 352 us
  waiting for transfers between devices  235 us (66%)
  Pallas kernels  34.6 us (10%)
  matrix products  21.8 us (6%)
  local copies, waits for them, and re-layouts  19.7 us (6%)
  other arithmetic  16.8 us (5%)
  between operations  13.6 us (4%)
  starting transfers between devices  11 us (3%)
    all_gather x1, waiting for transfers between devices, body(): lax.all_gather(coef_top[None], ('group', 'cluster'), axis=0, tiled=True)  235 us
    pallas_call x2, Pallas kernels, couple_pallas(): pl.pallas_call(functools.partial(couple_kernel, nb, listed, total), grid_...  34.6 us
    all_to_all x1, starting transfers between devices, body(): lax.all_to_all(outgoing, ('group', 'cluster'), split_axis=0, concat_axis=...  10.7 us
    select_n x2, other arithmetic, body(): jnp.take(coef_mid, send_mid, axis=0, mode='fill', fill_value=0.0)  7.22 us
  transfers between devices with their start and end apart: 2, of which 1 were waited for; matrix products, arithmetic and copies ran while one was open for 2% of the time, Pallas kernels for 0%

profile of v3, /device:TPU:24, one launch (start us, length us, event | category | flops | bytes accessed | tf_op | source)
XLA Modules:
  0.0 352.3 jit_solution(16250850650702669888)
XLA Ops:
  6.5 0.8 compare_select_fusion.1
  7.4 0.8 compare_and_fusion.2
  9.5 0.7 fusion.13
  10.3 5.1 %fusion = f32[32,128,64]{1,2,0:T(8,128)S(1)} fusion(f32[32,64,256]{2,1,0:T(8,128)S(1)} %copy-done, f32[32,256,128]{2,1,0:T(8,128)} %bitcast.54, f32[32,256]{1,0:T(8,128)S(1)} %fusion.13), kind=kOutput, calls=%fused_computation.7 | convolution fusion | flops 806354944 | bytes 7372800 | tf_op jit(solution)/shard_map/lkm,lmp->lkp/dot_general | solution.py:87
  15.4 1.1 fusion.32
  16.5 1.0 fusion.5
  17.6 0.7 copy-done.3
  18.7 4.4 %gather_fusion.1 = f32[256,64,128]{2,1,0:T(8,128)} fusion(f32[8,64,128]{2,1,0:T(8,128)S(1)} %copy.18, s32[1024]{0:T(1024)S(1)} %pad_clamp_fusion.1), kind=kCustom, calls=%fused_computation.1 | custom fusion | bytes 16778240 | tf_op jit(solution)/shard_map/jit(_take)/gather | solution.py:96
  23.0 4.4 %gather_fusion = f32[256,64,128]{2,1,0:T(8,128)} fusion(f32[32,64,128]{2,1,0:T(8,128)S(1)} %bitcast.50, s32[1024]{0:T(1024)S(1)} %pad_clamp_fusion.2), kind=kCustom, calls=%fused_computation | custom fusion | bytes 16778240 | tf_op jit(solution)/shard_map/jit(_take)/gather | solution.py:95
  27.4 6.5 %broadcast_select_fusion = (f32[128,2,64,128]{3,2,1,0:T(8,128)S(1)}, f32[128,2,64,128]{3,2,1,0:T(8,128)S(1)}) fusion(f32[128,2,64,128]{3,2,1,0:T(8,128)} %bitcast.52, pred[128,2]{1,0:T(8,128)(4,1)S(1)} %broadcast_in_dim.70, f32[128,2,64,128]{3,2,1,0:T(8,128)} %bitcast.53, pred[128,2]{1,0:T(8,128)(4,1)S(1)} %broadcast_in_dim.66), kind=kLoop, calls=%fused_computation.5 | loop fusion | flops 4194304 | bytes 33554944 | tf_op jit(solution)/shard_map/jit(_take)/select_n | solution.py:96
  34.0 6.1 %pad_maximum_fusion = f32[128,4,64,128]{3,2,1,0:T(8,128)} fusion(f32[128,2,64,128]{3,2,1,0:T(8,128)S(1)} %get-tuple-element.5, f32[128,2,64,128]{3,2,1,0:T(8,128)S(1)} %get-tuple-element.6), kind=kLoop, calls=%fused_computation.3 | loop fusion | flops 4194304 | bytes 33554432 | tf_op jit(solution)/shard_map/concatenate | solution.py:97
  40.1 10.7 %all-to-all-start = ((f32[512,64,128]{2,1,0:T(8,128)}), f32[512,64,128]{2,1,0:T(8,128)}, u32[]{:S(2)}, u32[]{:S(2)}) async-start(f32[512,64,128]{2,1,0:T(8,128)} %bitcast.51), calls=%async_computation | async-start | bytes 33554432 | tf_op jit(solution)/shard_map/all_to_all | solution.py:104
  51.2 1.2 convolution_bitcast_fusion.3
  53.2 0.7 reshape.159.idx_ref
  54.3 234.8 %all-gather.3.cloned.1.call-done = f32[8192,128]{1,0:T(8,128)} async-done(((f32[64,128]{1,0:T(8,128)}), f32[8192,128]{1,0:T(8,128)}) %all-gather.3.cloned.1.call-update) | async-done | bytes 4194320 | tf_op jit(solution)/shard_map/all_gather | solution.py:110
  289.1 2.7 gather_fusion.2
  292.0 1.1 convolution_bitcast_fusion.2
  293.0 15.1 %shard_map.137 = f32[8,64,128]{2,1,0:T(8,128)} custom-call(s32[256]{0:T(256)} %reshape.162.idx_ref, f32[512,64,128]{2,1,0:T(8,128)} %all-to-all-done.arrived_ref, f32[8,64,2048]{2,1,0:T(8,128)} %coupling_ref.3), custom_call_target="tpu_custom_call" | custom-call | flops 268435456 | bytes 21233664 | tf_op jit(solution)/shard_map/pallas_call | solution.py:49
  308.2 1.5 fusion.4
  309.7 1.6 fusion.9
  311.3 19.5 %shard_map.136 = f32[32,64,128]{2,1,0:T(8,128)} custom-call(s32[384]{0:T(512)} %reshape.159.idx_ref, f32[512,64,128]{2,1,0:T(8,128)} %all-to-all-done.arrived_ref, f32[32,64,768]{2,1,0:T(8,128)} %coupling_ref.2), custom_call_target="tpu_custom_call" | custom-call | flops 402653184 | bytes 24117248 | tf_op jit(solution)/shard_map/pallas_call | solution.py:49
  330.8 3.9 %fusion.3 = f32[32,64,128]{2,1,0:T(8,128)S(1)} fusion(f32[32,64,128]{2,1,0:T(8,128)} %shard_map.136, f32[32,64,64]{2,1,0:T(8,128)S(1)} %copy-done.2, f32[32,64,128]{2,0,1:T(8,128)} %fusion.9), kind=kOutput, calls=%fused_computation.11 | convolution fusion | flops 201588736 | bytes 3670016 | tf_op jit(solution)/shard_map/ljk,ljp->lkp/dot_general | solution.py:132
  334.7 5.2 %multiply_bitcast_fusion = f32[32,256,128]{1,2,0:T(8,128)} fusion(f32[32,64,128]{2,1,0:T(8,128)S(1)} %fusion.3, f32[32,64,256]{2,1,0:T(8,128)S(1)} %copy-done, f32[32,256]{1,0:T(8,128)S(1)} %fusion.13), kind=kOutput, calls=%fused_computation.4 | convolution fusion | flops 806354944 | bytes 7372800 | tf_op jit(solution)/shard_map/lkm,lkp->lmp/dot_general | solution.py:136
  339.9 5.6 %copy.20 = f32[32,256,128]{2,1,0:T(8,128)} copy(f32[32,256,128]{1,2,0:T(8,128)} %multiply_bitcast_fusion) | data formatting | bytes 8388608 | tf_op jit(solution)/shard_map/mul | solution.py:136
  (40 shorter events, 3.4 us)
Async XLA Ops:
  6.5 3.7 %copy-start = (f32[32,64,256]{2,1,0:T(8,128)S(1)}, f32[32,64,256]{2,1,0:T(8,128)}, u32[]{:S(2)}) copy-start(f32[32,64,256]{2,1,0:T(8,128)} %param.16) | copy-start | bytes 6291460
  6.5 8.9 %copy-start.1 = (f32[32,64,64]{2,1,0:T(8,128)S(1)}, f32[32,64,64]{2,1,0:T(8,128)}, u32[]{:S(2)}) copy-start(f32[32,64,64]{2,1,0:T(8,128)} %param.17) | copy-start | bytes 1572868
  10.3 6.3 %copy-start.9 = (s32[32]{0:T(128)S(1)}, s32[32]{0:T(128)}, u32[]{:S(2)}) copy-start(s32[32]{0:T(128)} %param.19) | copy-start | bytes 388
  17.6 0.7 copy-start.3
  40.0 11.0 %copy-start.5 = (f32[8,64,64]{2,1,0:T(8,128)S(1)}, f32[8,64,64]{2,1,0:T(8,128)}, u32[]{:S(2)}) copy-start(f32[8,64,64]{2,1,0:T(8,128)} %param.18) | copy-start | bytes 393220
  40.0 11.2 %copy-start.4 = (f32[8,64,128]{2,0,1:T(8,128)S(1)}, f32[8,64,128]{2,0,1:T(8,128)}, u32[]{:S(2)}) copy-start(f32[8,64,128]{2,0,1:T(8,128)} %copy-done.3) | copy-start | bytes 786436
  40.0 12.4 %copy-start.8 = (s32[8,32]{1,0:T(8,128)S(1)}, s32[8,32]{1,0:T(8,128)}, u32[]{:S(2)}) copy-start(s32[8,32]{1,0:T(8,128)} %param.24) | copy-start | bytes 3076
  40.0 13.1 %copy-start.7 = (s32[32,12]{0,1:T(8,128)S(1)}, s32[32,12]{0,1:T(8,128)}, u32[]{:S(2)}) copy-start(s32[32,12]{0,1:T(8,128)} %param.21) | copy-start | bytes 4612
  40.0 13.9 %copy-start.6 = (s32[32,4]{0,1:T(4,128)S(1)}, s32[32,4]{0,1:T(4,128)}, u32[]{:S(2)}) copy-start(s32[32,4]{0,1:T(4,128)} %param.26) | copy-start | bytes 1540
  40.1 253.0 %all-to-all-start = ((f32[512,64,128]{2,1,0:T(8,128)}), f32[512,64,128]{2,1,0:T(8,128)}, u32[]{:S(2)}, u32[]{:S(2)}) async-start(f32[512,64,128]{2,1,0:T(8,128)} %bitcast.51), calls=%async_computation | async-start | bytes 33554432 | tf_op jit(solution)/shard_map/all_to_all | solution.py:104
  50.8 238.3 %all-gather.3.cloned.1.call-start = ((), (), s32[]{:S(2)}) async-start(), calls=%async_computation.1 | async-start | bytes 4227072 | tf_op jit(solution)/shard_map/all_gather | solution.py:110
  311.3 19.5 %copy-start.2 = (f32[32,64,64]{2,1,0:T(8,128)S(1)}, f32[32,64,64]{2,1,0:T(8,128)}, u32[]{:S(2)}) copy-start(f32[32,64,64]{2,1,0:T(8,128)} %param.17) | copy-start | bytes 1572868
Sparse Core Ops, SparseCore 0:
  54.8 234.2 all-gather.2

commit v4 on v3

--- a/solution.py
+++ b/solution.py
@@ -59,6 +59,50 @@
     )(rows.reshape(-1), arrived, coupling)
 
 
+def top_kernel(listed, coarse, idx_ref, pos_ref, gathered_ref, coupling_ref, out_ref):
+    rank = gathered_ref.shape[1]
+    lanes = gathered_ref.shape[0]
+    per_lane = coarse // lanes
+    position = pos_ref[0]
+    for o in range(coupling_ref.shape[0]):
+        out_ref[o] = jnp.zeros(out_ref.shape[1:], jnp.float32)
+        for k in range(listed):
+            s = idx_ref[o * listed + k]
+
+            @pl.when((s < coarse) & (s % per_lane == position))
+            def _():
+                blk = gathered_ref[jnp.minimum(s // per_lane, lanes - 1)]
+                c = coupling_ref[o, :, k * rank : (k + 1) * rank]
+                out_ref[o] += jnp.dot(
+                    c, blk, precision=exact_mode, preferred_element_type=jnp.float32
+                )
+
+
+def top_partial(top_pairs, position, gathered, top_coupling, coarse):
+    n, rank, width = top_coupling.shape
+    listed = top_pairs.shape[1]
+    ports = gathered.shape[2]
+    grid_spec = pltpu.PrefetchScalarGridSpec(
+        num_scalar_prefetch=2,
+        grid=(1,),
+        in_specs=[
+            pl.BlockSpec(gathered.shape, lambda i, idx, pos: (0, 0, 0)),
+            pl.BlockSpec(top_coupling.shape, lambda i, idx, pos: (0, 0, 0)),
+        ],
+        out_specs=pl.BlockSpec((n, rank, ports), lambda i, idx, pos: (0, 0, 0)),
+    )
+    return pl.pallas_call(
+        functools.partial(top_kernel, listed, coarse),
+        grid_spec=grid_spec,
+        out_shape=jax.ShapeDtypeStruct((n, rank, ports), jnp.float32),
+        cost_estimate=pl.CostEstimate(
+            flops=2 * rank * width * ports,
+            bytes_accessed=4 * (n * rank * width + n * rank * ports),
+            transcendentals=0,
+        ),
+    )(top_pairs.reshape(-1), position, gathered, top_coupling)
+
+
 def body(
     charges,
     leaf_size,
@@ -103,22 +147,10 @@
     ).reshape(owners * 2 * slots, coef_rank, port_count)
     arrived = lax.all_to_all(outgoing, ("group", "cluster"), split_axis=0, concat_axis=0, tiled=True)
 
-    listed = top_pairs.shape[1]
-    position = lax.axis_index("cluster")
-    wanted = lax.dynamic_slice_in_dim(top_pairs, position, 1, 0)[0]
-    own_coupling = lax.dynamic_slice_in_dim(top_coupling, position, 1, 0)[0]
-    shard_rows = lax.all_gather(coef_top[None], ("group", "cluster"), axis=0, tiled=True)
-    inside = (wanted >= 0) & (wanted < shard_rows.shape[0])
-    taken_rows = jnp.take(shard_rows, jnp.clip(wanted, 0, shard_rows.shape[0] - 1), axis=0)
-    picked = jnp.where(
-        inside[:, None, None], taken_rows, jnp.zeros((listed, coef_rank, port_count), jnp.float32)
-    )
-    near_top = jnp.einsum(
-        "kq,qp->kp",
-        own_coupling,
-        picked.reshape(listed * coef_rank, port_count),
-        precision=exact_mode,
-    )
+    lanes = lax.all_gather(coef_top[None], "group", axis=0, tiled=True)
+    position = lax.axis_index("cluster").astype(jnp.int32).reshape(1)
+    partial = top_partial(top_pairs, position, lanes, top_coupling, owners)
+    near_top = lax.psum_scatter(partial, "cluster", scatter_dimension=0, tiled=True)[0]
 
     total_rows = owners * 2 * slots
     live_leaf = pair_leaf < owners * slots

time: 358 us -> 423 us (1.18); the launches traced: 352 us -> 422 us
  blocking collectives: 0 us -> 226 us
  waiting for transfers between devices: 235 us -> 77.5 us
  Pallas kernels: 34.6 us -> 40 us
    all_gather x1 -> x0, waiting for transfers between devices: 235 us -> none  [body(): lax.all_gather(coef_top[None], ('group', 'cluster'), axis=0, tiled=True)]
    all_gather x0 -> x1, blocking collectives: none -> 226 us  [body(): lanes = lax.all_gather(coef_top[None], 'group', axis=0, tiled=True)]
    reduce_scatter x0 -> x1, waiting for transfers between devices: none -> 77.4 us  [body(): lax.psum_scatter(partial, 'cluster', scatter_dimension=0, tiled=True)[0]]
    pallas_call x0 -> x1, Pallas kernels: none -> 5.4 us  [top_partial(): pl.pallas_call(functools.partial(top_kernel, listed, coarse), grid_spec=g...]
  transfers between devices with their start and end apart: 2 -> 2, of which waited for: 1 -> 1; matrix products, arithmetic and copies ran while one was open for 2% -> 1% of each run, Pallas kernels for 0% -> 5%
where the time goes in v4:
time: 423 us; the launch traced here: 422 us
  blocking collectives  226 us (53%)
  waiting for transfers between devices  77.5 us (18%)
  Pallas kernels  40 us (9%)
  matrix products  20.1 us (5%)
  local copies, waits for them, and re-layouts  17.7 us (4%)
  other arithmetic  16.3 us (4%)
  between operations  13.6 us (3%)
  starting transfers between devices  10.8 us (3%)
    all_gather x1, blocking collectives, body(): lanes = lax.all_gather(coef_top[None], 'group', axis=0, tiled=True)  226 us
    reduce_scatter x1, waiting for transfers between devices, body(): lax.psum_scatter(partial, 'cluster', scatter_dimension=0, tiled=True)[0]  77.4 us
    pallas_call x2, Pallas kernels, couple_pallas(): pl.pallas_call(functools.partial(couple_kernel, nb, listed, total), grid_...  34.6 us
    all_to_all x1, starting transfers between devices, body(): lax.all_to_all(outgoing, ('group', 'cluster'), split_axis=0, concat_axis=...  10.7 us
  transfers between devices with their start and end apart: 2, of which 1 were waited for; matrix products, arithmetic and copies ran while one was open for 1% of the time, Pallas kernels for 5%

profile of v4, /device:TPU:24, one launch (start us, length us, event | category | flops | bytes accessed | tf_op | source)
XLA Modules:
  0.0 421.8 jit_solution(1641345388861795975)
XLA Ops:
  6.5 0.8 compare_and_fusion.1
  7.4 0.7 compare_select_fusion.1
  8.1 0.7 compare_and_fusion
  9.8 0.8 fusion.12
  10.6 5.1 %fusion = f32[32,128,64]{1,2,0:T(8,128)S(1)} fusion(f32[32,64,256]{2,1,0:T(8,128)S(1)} %copy-done, f32[32,256,128]{2,1,0:T(8,128)} %bitcast.47, f32[32,256]{1,0:T(8,128)S(1)} %fusion.12), kind=kOutput, calls=%fused_computation.6 | convolution fusion | flops 806354944 | bytes 7372800 | tf_op jit(solution)/shard_map/lkm,lmp->lkp/dot_general | solution.py:131
  15.7 1.1 fusion.29
  16.8 1.0 fusion.5
  17.9 0.7 copy-done.3
  18.6 4.4 %gather_fusion.1 = f32[256,64,128]{2,1,0:T(8,128)} fusion(f32[8,64,128]{2,1,0:T(8,128)S(1)} %copy.19, s32[1024]{0:T(1024)S(1)} %pad_clamp_fusion), kind=kCustom, calls=%fused_computation.1 | custom fusion | bytes 16778240 | tf_op jit(solution)/shard_map/jit(_take)/gather | solution.py:140
  23.0 4.4 %gather_fusion = f32[256,64,128]{2,1,0:T(8,128)} fusion(f32[32,64,128]{2,1,0:T(8,128)S(1)} %bitcast.43, s32[1024]{0:T(1024)S(1)} %pad_clamp_fusion.1), kind=kCustom, calls=%fused_computation | custom fusion | bytes 16778240 | tf_op jit(solution)/shard_map/jit(_take)/gather | solution.py:139
  27.4 6.5 %broadcast_select_fusion = (f32[128,2,64,128]{3,2,1,0:T(8,128)S(1)}, f32[128,2,64,128]{3,2,1,0:T(8,128)S(1)}) fusion(f32[128,2,64,128]{3,2,1,0:T(8,128)} %bitcast.45, pred[128,2]{1,0:T(8,128)(4,1)S(1)} %broadcast_in_dim.48, f32[128,2,64,128]{3,2,1,0:T(8,128)} %bitcast.46, pred[128,2]{1,0:T(8,128)(4,1)S(1)} %broadcast_in_dim.44), kind=kLoop, calls=%fused_computation.4 | loop fusion | flops 4194304 | bytes 33554944 | tf_op jit(solution)/shard_map/jit(_take)/select_n | solution.py:140
  33.9 6.1 %pad_maximum_fusion = f32[128,4,64,128]{3,2,1,0:T(8,128)} fusion(f32[128,2,64,128]{3,2,1,0:T(8,128)S(1)} %get-tuple-element.5, f32[128,2,64,128]{3,2,1,0:T(8,128)S(1)} %get-tuple-element.6), kind=kLoop, calls=%fused_computation.2 | loop fusion | flops 4194304 | bytes 33554432 | tf_op jit(solution)/shard_map/concatenate | solution.py:141
  40.0 10.7 %all-to-all-start = ((f32[512,64,128]{2,1,0:T(8,128)}), f32[512,64,128]{2,1,0:T(8,128)}, u32[]{:S(2)}, u32[]{:S(2)}) async-start(f32[512,64,128]{2,1,0:T(8,128)} %bitcast.44), calls=%async_computation | async-start | bytes 33554432 | tf_op jit(solution)/shard_map/all_to_all | solution.py:148
  52.3 225.8 %all-gather = f32[256,128]{1,0:T(8,128)} all-gather(f32[64,128]{1,0:T(8,128)S(1)} %convolution_bitcast_fusion.2), channel_id=2, replica_groups=mesh['group'=4,'cluster'=32] {'group'}, dimensions={0}, use_global_device_ids=true | all-gather | bytes 163840 | tf_op jit(solution)/shard_map/all_gather | solution.py:150
  278.1 5.4 %shard_map.138 = f32[32,64,128]{2,1,0:T(8,128)} custom-call(s32[128]{0:T(128)} %reshape.66.idx_ref, s32[1]{0:T(128)} %bitcast.8.pos_ref, f32[4,64,128]{2,1,0:T(8,128)} %bitcast.48, f32[32,64,256]{2,1,0:T(8,128)} %coupling_ref.5), custom_call_target="tpu_custom_call" | custom-call | flops 4194304 | bytes 3145728 | tf_op jit(solution)/shard_map/pallas_call | solution.py:94
  284.3 0.7 reshape.62.idx_ref
  285.0 15.1 %shard_map.137 = f32[8,64,128]{2,1,0:T(8,128)} custom-call(s32[256]{0:T(256)} %reshape.65.idx_ref, f32[512,64,128]{2,1,0:T(8,128)} %all-to-all-done.arrived_ref, f32[8,64,2048]{2,1,0:T(8,128)} %coupling_ref.4), custom_call_target="tpu_custom_call" | custom-call | flops 268435456 | bytes 21233664 | tf_op jit(solution)/shard_map/pallas_call | solution.py:49
  300.1 77.4 %reduce-scatter.2.cloned.1.call-done = f32[1,64,128]{2,1,0:T(8,128)} async-done(((f32[32,64,128]{2,1,0:T(8,128)}), f32[1,64,128]{2,1,0:T(8,128)}) %reduce-scatter.2.cloned.1.call-update) | async-done | bytes 32784 | tf_op jit(solution)/shard_map/reduce_scatter | solution.py:153
  377.6 1.6 fusion.4
  379.1 1.6 fusion.9
  380.7 19.5 %shard_map.136 = f32[32,64,128]{2,1,0:T(8,128)} custom-call(s32[384]{0:T(512)} %reshape.62.idx_ref, f32[512,64,128]{2,1,0:T(8,128)} %all-to-all-done.arrived_ref, f32[32,64,768]{2,1,0:T(8,128)} %coupling_ref.3), custom_call_target="tpu_custom_call" | custom-call | flops 402653184 | bytes 24117248 | tf_op jit(solution)/shard_map/pallas_call | solution.py:49
  400.2 3.9 fusion.3
  404.1 5.2 %multiply_bitcast_fusion = f32[32,256,128]{1,2,0:T(8,128)} fusion(f32[32,64,128]{2,1,0:T(8,128)S(1)} %fusion.3, f32[32,64,256]{2,1,0:T(8,128)S(1)} %copy-done, f32[32,256]{1,0:T(8,128)S(1)} %fusion.12), kind=kOutput, calls=%fused_computation.3 | convolution fusion | flops 806354944 | bytes 7372800 | tf_op jit(solution)/shard_map/lkm,lkp->lmp/dot_general | solution.py:168
  409.3 5.6 %copy.22 = f32[32,256,128]{2,1,0:T(8,128)} copy(f32[32,256,128]{1,2,0:T(8,128)} %multiply_bitcast_fusion) | data formatting | bytes 8388608 | tf_op jit(solution)/shard_map/mul | solution.py:168
  (36 shorter events, 3.4 us)
Async XLA Ops:
  6.5 4.1 copy-start
  6.5 10.3 %copy-start.8 = (s32[32]{0:T(128)S(1)}, s32[32]{0:T(128)}, u32[]{:S(2)}) copy-start(s32[32]{0:T(128)} %param.19) | copy-start | bytes 388
  9.8 5.9 %copy-start.1 = (f32[32,64,64]{2,1,0:T(8,128)S(1)}, f32[32,64,64]{2,1,0:T(8,128)}, u32[]{:S(2)}) copy-start(f32[32,64,64]{2,1,0:T(8,128)} %param.17) | copy-start | bytes 1572868
  17.9 0.7 copy-start.3
  40.0 10.8 %copy-start.9 = (s32[32,4]{0,1:T(4,128)S(1)}, s32[32,4]{0,1:T(4,128)}, u32[]{:S(2)}) copy-start(s32[32,4]{0,1:T(4,128)} %param.26) | copy-start | bytes 1540
  40.0 11.5 %copy-start.5 = (f32[8,64,64]{2,1,0:T(8,128)S(1)}, f32[8,64,64]{2,1,0:T(8,128)}, u32[]{:S(2)}) copy-start(f32[8,64,64]{2,1,0:T(8,128)} %param.18) | copy-start | bytes 393220
  40.0 11.7 %copy-start.4 = (f32[8,64,128]{2,0,1:T(8,128)S(1)}, f32[8,64,128]{2,0,1:T(8,128)}, u32[]{:S(2)}) copy-start(f32[8,64,128]{2,0,1:T(8,128)} %copy-done.3) | copy-start | bytes 786436
  40.0 243.5 %copy-start.7 = (s32[8,32]{1,0:T(8,128)S(1)}, s32[8,32]{1,0:T(8,128)}, u32[]{:S(2)}) copy-start(s32[8,32]{1,0:T(8,128)} %param.24) | copy-start | bytes 3076
  40.0 244.2 %copy-start.6 = (s32[32,12]{0,1:T(8,128)S(1)}, s32[32,12]{0,1:T(8,128)}, u32[]{:S(2)}) copy-start(s32[32,12]{0,1:T(8,128)} %param.21) | copy-start | bytes 4612
  40.0 245.0 %all-to-all-start = ((f32[512,64,128]{2,1,0:T(8,128)}), f32[512,64,128]{2,1,0:T(8,128)}, u32[]{:S(2)}, u32[]{:S(2)}) async-start(f32[512,64,128]{2,1,0:T(8,128)} %bitcast.44), calls=%async_computation | async-start | bytes 33554432 | tf_op jit(solution)/shard_map/all_to_all | solution.py:148
  50.7 326.8 %reduce-scatter.2.cloned.1.call-start = ((), (), s32[]{:S(2)}) async-start(), calls=%async_computation.2 | async-start | bytes 1081344 | tf_op jit(solution)/shard_map/reduce_scatter | solution.py:153
  380.7 19.5 %copy-start.2 = (f32[32,64,64]{2,1,0:T(8,128)S(1)}, f32[32,64,64]{2,1,0:T(8,128)}, u32[]{:S(2)}) copy-start(f32[32,64,64]{2,1,0:T(8,128)} %param.17) | copy-start | bytes 1572868
Sparse Core Ops, SparseCore 0:
  283.6 93.8 reduce-scatter.1

commit v5 on v3

--- a/solution.py
+++ b/solution.py
@@ -57,6 +57,98 @@
             transcendentals=0,
         ),
     )(rows.reshape(-1), arrived, coupling)
+
+
+def payload_kernel(chunk, size_ref, parent_ref, send_leaf_ref, send_mid_ref, charges_ref, basis_ref,
+                   transfer_ref, mid_transfer_ref, out_ref, top_ref, leaf_sc, mid_sc):
+    i = pl.program_id(0)
+    leaves, rank, points = basis_ref.shape
+    mids = mid_transfer_ref.shape[0]
+
+    @pl.when(i == 0)
+    def _():
+        mid_sc[...] = jnp.zeros(mid_sc.shape, jnp.float32)
+        rows = lax.broadcasted_iota(jnp.int32, (points, 1), 0)
+        for l in range(leaves):
+            blk = charges_ref[l * points:(l + 1) * points, :]
+            blk = jnp.where(rows < size_ref[l], blk, 0.0)
+            coef = jnp.dot(basis_ref[l], blk, precision=exact_mode, preferred_element_type=jnp.float32)
+            leaf_sc[l] = coef
+            up = jnp.dot(transfer_ref[l], coef, precision=exact_mode, preferred_element_type=jnp.float32)
+            p = parent_ref[l]
+            mid_sc[p] = mid_sc[p] + up
+        top = jnp.zeros(top_ref.shape, jnp.float32)
+        for c in range(mids):
+            top = top + jnp.dot(mid_transfer_ref[c], mid_sc[c], precision=exact_mode,
+                                preferred_element_type=jnp.float32)
+        top_ref[...] = top
+
+    per = chunk // 4
+    for q in range(per):
+        r = i * per + q
+        for j in range(2):
+            a = send_leaf_ref[r * 2 + j]
+            out_ref[q * 4 + j] = jnp.where(a < leaves, leaf_sc[jnp.minimum(a, leaves - 1)], 0.0)
+            b = send_mid_ref[r * 2 + j]
+            out_ref[q * 4 + 2 + j] = jnp.where(b < mids, mid_sc[jnp.minimum(b, mids - 1)], 0.0)
+
+def build_payload(charges, leaf_size, leaf_parent, send_leaf, send_mid, leaf_basis, leaf_transfer, mid_transfer, steps=8):
+    leaves, rank, points = leaf_basis.shape
+    ports = charges.shape[1]
+    mids = mid_transfer.shape[0]
+    owners = send_leaf.shape[0] // 2
+    total = owners * 4
+    chunk = total // steps
+    full = lambda shape: pl.BlockSpec(shape, lambda i, *_: (0,) * len(shape), pipeline_mode=pl.Buffered(1))
+    grid_spec = pltpu.PrefetchScalarGridSpec(
+        num_scalar_prefetch=4,
+        grid=(steps,),
+        in_specs=[full(charges.shape), full(leaf_basis.shape), full(leaf_transfer.shape), full(mid_transfer.shape)],
+        out_specs=[pl.BlockSpec((chunk, rank, ports), lambda i, *_: (i, 0, 0)),
+                   pl.BlockSpec((rank, ports), lambda i, *_: (0, 0))],
+        scratch_shapes=[pltpu.VMEM((leaves, rank, ports), jnp.float32), pltpu.VMEM((mids, rank, ports), jnp.float32)],
+    )
+    return pl.pallas_call(
+        functools.partial(payload_kernel, chunk),
+        grid_spec=grid_spec,
+        out_shape=[jax.ShapeDtypeStruct((total, rank, ports), jnp.float32), jax.ShapeDtypeStruct((rank, ports), jnp.float32)],
+        compiler_params=pltpu.CompilerParams(vmem_limit_bytes=60 * 1024 * 1024, dimension_semantics=("arbitrary",)),
+        cost_estimate=pl.CostEstimate(flops=2 * leaves * rank * points * ports, bytes_accessed=4 * (charges.size + leaf_basis.size + total * rank * ports), transcendentals=0),
+    )(leaf_size, leaf_parent, send_leaf, send_mid, charges, leaf_basis, leaf_transfer, mid_transfer)
+
+def far_kernel(nb, size_ref, parent_ref, near_ref, transfer_ref, basis_ref, down_mid_ref, out_ref):
+    i = pl.program_id(0)
+    rank = near_ref.shape[1]
+    points = basis_ref.shape[2]
+    rows = lax.broadcasted_iota(jnp.int32, (points, 1), 0)
+    tdims = (((0,), (0,)), ((), ()))
+    for t in range(nb):
+        l = i * nb + t
+        p = parent_ref[l]
+        dm = down_mid_ref[p]
+        dl = near_ref[t] + lax.dot_general(transfer_ref[t], dm, tdims, precision=exact_mode, preferred_element_type=jnp.float32)
+        far = lax.dot_general(basis_ref[t], dl, tdims, precision=exact_mode, preferred_element_type=jnp.float32)
+        out_ref[t * points:(t + 1) * points, :] = jnp.where(rows < size_ref[l], far, 0.0)
+
+def far_field_pallas(near_leaf, leaf_transfer, leaf_basis, down_mid, leaf_size, leaf_parent, nb=8):
+    leaves, rank, points = leaf_basis.shape
+    ports = near_leaf.shape[2]
+    grid_spec = pltpu.PrefetchScalarGridSpec(
+        num_scalar_prefetch=2,
+        grid=(leaves // nb,),
+        in_specs=[pl.BlockSpec((nb, rank, ports), lambda i, *_: (i, 0, 0)),
+                  pl.BlockSpec((nb, rank, rank), lambda i, *_: (i, 0, 0)),
+                  pl.BlockSpec((nb, rank, points), lambda i, *_: (i, 0, 0)),
+                  pl.BlockSpec(down_mid.shape, lambda i, *_: (0, 0, 0))],
+        out_specs=pl.BlockSpec((nb * points, ports), lambda i, *_: (i, 0)),
+    )
+    return pl.pallas_call(
+        functools.partial(far_kernel, nb),
+        grid_spec=grid_spec,
+        out_shape=jax.ShapeDtypeStruct((leaves * points, ports), jnp.float32),
+        compiler_params=pltpu.CompilerParams(vmem_limit_bytes=60 * 1024 * 1024),
+        cost_estimate=pl.CostEstimate(flops=2 * leaves * rank * points * ports, bytes_accessed=4 * (leaf_basis.size + 2 * leaves * points * ports), transcendentals=0),
+    )(leaf_size, leaf_parent, near_leaf, leaf_transfer, leaf_basis, down_mid)
 
 
 def body(
@@ -80,28 +172,12 @@
     mid_count = mid_transfer.shape[0]
     owners = send_leaf.shape[0] // 2
     slots = 2
-    point_mask = (jnp.arange(leaf_points, dtype=jnp.int32)[None, :] < leaf_size[:, None]).astype(
-        jnp.float32
-    )
-    blocks = charges.reshape(leaf_count, leaf_points, port_count) * point_mask[:, :, None]
-    coef_leaf = jnp.einsum("lkm,lmp->lkp", leaf_basis, blocks, precision=exact_mode)
-    moved_up = jnp.einsum("ljk,lkp->ljp", leaf_transfer, coef_leaf, precision=exact_mode)
-    parent_map = (leaf_parent[None, :] == jnp.arange(mid_count, dtype=jnp.int32)[:, None]).astype(
-        jnp.float32
-    )
-    coef_mid = jnp.einsum("ml,ljp->mjp", parent_map, moved_up, precision=exact_mode)
-    coef_top = jnp.einsum("mjk,mkp->jp", mid_transfer, coef_mid, precision=exact_mode)
-
-    outgoing_leaf = jnp.take(coef_leaf, send_leaf, axis=0, mode="fill", fill_value=0.0)
-    outgoing_mid = jnp.take(coef_mid, send_mid, axis=0, mode="fill", fill_value=0.0)
-    outgoing = jnp.concatenate(
-        [
-            outgoing_leaf.reshape(owners, slots, coef_rank, port_count),
-            outgoing_mid.reshape(owners, slots, coef_rank, port_count),
-        ],
-        axis=1,
-    ).reshape(owners * 2 * slots, coef_rank, port_count)
-    arrived = lax.all_to_all(outgoing, ("group", "cluster"), split_axis=0, concat_axis=0, tiled=True)
+    arrived_rows, coef_top = build_payload(
+        charges, leaf_size, leaf_parent, send_leaf, send_mid, leaf_basis, leaf_transfer, mid_transfer
+    )
+    arrived = lax.all_to_all(
+        arrived_rows, ("group", "cluster"), split_axis=0, concat_axis=0, tiled=True
+    )
 
     listed = top_pairs.shape[1]
     position = lax.axis_index("cluster")
@@ -128,15 +204,7 @@
     mid_rows = jnp.where(live_mid, pair_mid + (pair_mid // slots + 1) * slots, total_rows)
     near_mid = couple_pallas(mid_coupling, arrived, mid_rows, 2)
     down_mid = near_mid + jnp.einsum("mjk,jp->mkp", mid_transfer, near_top, precision=exact_mode)
-    from_parent = jnp.einsum("ml,mkp->lkp", parent_map, down_mid, precision=exact_mode)
-    down_leaf = near_leaf + jnp.einsum(
-        "ljk,ljp->lkp", leaf_transfer, from_parent, precision=exact_mode
-    )
-    far_field = (
-        jnp.einsum("lkm,lkp->lmp", leaf_basis, down_leaf, precision=exact_mode)
-        * point_mask[:, :, None]
-    )
-    return far_field.reshape(leaf_count * leaf_points, port_count)
+    return far_field_pallas(near_leaf, leaf_transfer, leaf_basis, down_mid, leaf_size, leaf_parent)
 
 
 def solution(mesh):

time: 358 us -> 336 us (0.939)
  Pallas kernels: 34.6 us -> 63.2 us
  matrix products: 21.8 us -> 0.57 us
  local copies, waits for them, and re-layouts: 19.7 us -> 4.33 us
  other arithmetic: 16.8 us -> 2.18 us
    pallas_call x0 -> x2, Pallas kernels: none -> 28.8 us  [the longest x1 18.6 us: build_payload(): pl.pallas_call(functools.partial(payload_kernel, chunk), grid_spec=grid_s...]
    dot_general x8 -> x0, matrix products: 20.8 us -> none  [the longest x1 5.25 us: body(): jnp.einsum('lkm,lkp->lmp', leaf_basis, down_leaf, precision=exact_mode)]
    gather x2 -> x0, local copies, waits for them, and re-layouts: 8.73 us -> none  [the longest x1 4.37 us: body(): jnp.take(coef_leaf, send_leaf, axis=0, mode='fill', fill_value=0.0)]
    select_n x3 -> x0, other arithmetic: 8.05 us -> none  [the longest x2 7.22 us: body(): jnp.take(coef_mid, send_mid, axis=0, mode='fill', fill_value=0.0)]
    concatenate x1 -> x0, other arithmetic: 6.06 us -> none  [body(): jnp.concatenate([outgoing_leaf.reshape(owners, slots, coef_rank, port_cou...]
    mul x1 -> x0, local copies, waits for them, and re-layouts: 5.56 us -> none  [body(): jnp.einsum('lkm,lkp->lmp', leaf_basis, down_leaf, precision=exact_mode)]
where the time goes in v5:
time: 336 us; the launch traced here: 331 us
  waiting for transfers between devices  236 us (70%)
  Pallas kernels  63.2 us (19%)
  between operations  13.5 us (4%)
  starting transfers between devices  11 us (3%)
  local copies, waits for them, and re-layouts  4.33 us (1%)
    all_gather x1, waiting for transfers between devices, body(): lax.all_gather(coef_top[None], ('group', 'cluster'), axis=0, tiled=True)  236 us
    pallas_call x2, Pallas kernels, couple_pallas(): pl.pallas_call(functools.partial(couple_kernel, nb, listed, total), grid_...  34.5 us
    pallas_call x1, Pallas kernels, build_payload(): pl.pallas_call(functools.partial(payload_kernel, chunk), grid_spec=grid_s...  18.6 us
    all_to_all x1, starting transfers between devices, body(): lax.all_to_all(arrived_rows, ('group', 'cluster'), split_axis=0, concat_a...  10.7 us
    pallas_call x1, Pallas kernels, far_field_pallas(): pl.pallas_call(functools.partial(far_kernel, nb), grid_spec=grid_spec, ou...  10.1 us
  transfers between devices with their start and end apart: 2, of which 1 were waited for; matrix products, arithmetic and copies ran while one was open for 2% of the time, Pallas kernels for 0%

profile of v5, /device:TPU:24, one launch (start us, length us, event | category | flops | bytes accessed | tf_op | source)
XLA Modules:
  0.0 330.8 jit_solution(6660289751795997494)
XLA Ops:
  6.5 0.0 copy-start
  6.5 18.6 %shard_map.136 = (f32[512,64,128]{2,1,0:T(8,128)}, f32[64,128]{1,0:T(8,128)}) custom-call(s32[32]{0:T(128)} %size_ref.3, s32[32]{0:T(128)} %parent_ref.3, s32[256]{0:T(256)} %send_leaf_ref.1, s32[256]{0:T(256)} %send_mid_ref.1, f32[8192,128]{1,0:T(8,128)} %charges_ref.1, f32[32,64,256]{2,1,0:T(8,128)} %basis_ref.3, f32[32,64,64]{2,1,0:T(8,128)} %transfer_ref.3, ...), custom_call_target="tpu_custom_call" | custom-call | flops 134217728 | bytes 23068672 | tf_op jit(solution)/shard_map/pallas_call | solution.py:111
  25.2 0.0 copy-start.2
  25.2 10.7 %all-to-all-start = ((f32[512,64,128]{2,1,0:T(8,128)}), f32[512,64,128]{2,1,0:T(8,128)}, u32[]{:S(2)}, u32[]{:S(2)}) async-start(f32[512,64,128]{2,1,0:T(8,128)} %get-tuple-element.7), calls=%async_computation | async-start | bytes 33554432 | tf_op jit(solution)/shard_map/all_to_all | solution.py:178
  35.9 0.2 all-gather.3.cloned.1.call-start
  36.2 0.5 all-gather.3.cloned.1.call-update
  36.7 0.0 copy-done.1
  36.7 0.1 copy.17
  36.8 0.0 copy-done.3
  36.8 0.1 copy.16
  36.9 0.7 reshape.109.idx_ref
  37.6 0.7 reshape.110.idx_ref
  38.3 0.2 clamp_reduce_fusion
  38.5 0.2 and_reduce_fusion
  38.7 235.5 %all-gather.3.cloned.1.call-done = f32[8192,128]{1,0:T(8,128)} async-done(((f32[64,128]{1,0:T(8,128)}), f32[8192,128]{1,0:T(8,128)}) %all-gather.3.cloned.1.call-update) | async-done | bytes 4194320 | tf_op jit(solution)/shard_map/all_gather | solution.py:186
  274.2 2.7 gather_fusion
  277.0 0.1 select_select_fusion
  277.1 0.2 fusion
  277.3 0.4 fusion.16
  277.7 0.0 all-to-all-done.arrived_ref
  277.7 15.1 %shard_map.138 = f32[8,64,128]{2,1,0:T(8,128)} custom-call(s32[256]{0:T(256)} %reshape.110.idx_ref, f32[512,64,128]{2,1,0:T(8,128)} %all-to-all-done.arrived_ref, f32[8,64,2048]{2,1,0:T(8,128)} %coupling_ref.3), custom_call_target="tpu_custom_call" | custom-call | flops 268435456 | bytes 21233664 | tf_op jit(solution)/shard_map/pallas_call | solution.py:49
  292.8 1.7 add.40.down_mid_ref
  294.5 19.3 %shard_map.137.near_ref = f32[32,64,128]{2,1,0:T(8,128)} custom-call(s32[384]{0:T(512)} %reshape.109.idx_ref, f32[512,64,128]{2,1,0:T(8,128)} %all-to-all-done.arrived_ref, f32[32,64,768]{2,1,0:T(8,128)} %coupling_ref.2), custom_call_target="tpu_custom_call" | custom-call | flops 402653184 | bytes 24117248 | tf_op jit(solution)/shard_map/pallas_call | solution.py:49
  313.8 10.1 %shard_map.139 = f32[8192,128]{1,0:T(8,128)} custom-call(s32[32]{0:T(128)} %size_ref.3, s32[32]{0:T(128)} %parent_ref.3, f32[32,64,128]{2,1,0:T(8,128)} %shard_map.137.near_ref, f32[32,64,64]{2,1,0:T(8,128)} %transfer_ref.3, f32[32,64,256]{2,1,0:T(8,128)} %basis_ref.3, f32[8,64,128]{2,1,0:T(8,128)} %add.40.down_mid_ref), custom_call_target="tpu_custom_call" | custom-call | flops 134217728 | bytes 10485760 | tf_op jit(solution)/shard_map/pallas_call | solution.py:145
  (11 shorter events, 0.1 us)
Async XLA Ops:
  6.5 270.6 %copy-start = (f32[32,64,256]{2,1,0:T(8,128)S(1)}, f32[32,64,256]{2,1,0:T(8,128)}, u32[]{:S(2)}) copy-start(f32[32,64,256]{2,1,0:T(8,128)} %param.27) | copy-start | bytes 6291460
  25.2 11.5 %copy-start.1 = (f32[8,64,64]{2,1,0:T(8,128)S(1)}, f32[8,64,64]{2,1,0:T(8,128)}, u32[]{:S(2)}) copy-start(f32[8,64,64]{2,1,0:T(8,128)} %mid_transfer_ref.1) | copy-start | bytes 393220
  25.2 11.6 %copy-start.3 = (s32[32,12]{0,1:T(8,128)S(1)}, s32[32,12]{0,1:T(8,128)}, u32[]{:S(2)}) copy-start(s32[32,12]{0,1:T(8,128)} %param.21) | copy-start | bytes 4612
  25.2 12.5 %copy-start.4 = (s32[8,32]{1,0:T(8,128)S(1)}, s32[8,32]{1,0:T(8,128)}, u32[]{:S(2)}) copy-start(s32[8,32]{1,0:T(8,128)} %param.24) | copy-start | bytes 3076
  25.2 13.1 %copy-start.2 = (s32[32,4]{0,1:T(4,128)S(1)}, s32[32,4]{0,1:T(4,128)}, u32[]{:S(2)}) copy-start(s32[32,4]{0,1:T(4,128)} %param.26) | copy-start | bytes 1540
  25.2 252.5 %all-to-all-start = ((f32[512,64,128]{2,1,0:T(8,128)}), f32[512,64,128]{2,1,0:T(8,128)}, u32[]{:S(2)}, u32[]{:S(2)}) async-start(f32[512,64,128]{2,1,0:T(8,128)} %get-tuple-element.7), calls=%async_computation | async-start | bytes 33554432 | tf_op jit(solution)/shard_map/all_to_all | solution.py:178
  35.9 238.3 %all-gather.3.cloned.1.call-start = ((), (), s32[]{:S(2)}) async-start(), calls=%async_computation.1 | async-start | bytes 4227072 | tf_op jit(solution)/shard_map/all_gather | solution.py:186
Sparse Core Ops, SparseCore 0:
  39.9 234.2 all-gather.2

commit v6 on v5

--- a/solution.py
+++ b/solution.py
@@ -151,7 +151,61 @@
     )(leaf_size, leaf_parent, near_leaf, leaf_transfer, leaf_basis, down_mid)
 
 
+def exchange_kernel(axes, sizes, payload_ref, landing_ref, send_sem, recv_sem, local_sem):
+    outer, inner = sizes
+    count = outer * inner
+    me = lax.axis_index(axes[0]) * inner + lax.axis_index(axes[1])
+    barrier = pltpu.get_barrier_semaphore()
+
+    def greet(q, carry):
+        peer = lax.rem(me + q, count)
+        pl.semaphore_signal(barrier, 1, device_id=(peer // inner, peer % inner),
+                            device_id_type=pl.DeviceIdType.MESH)
+        return carry
+
+    lax.fori_loop(1, count, greet, 0)
+    pl.semaphore_wait(barrier, count - 1)
+
+    def send(q, carry):
+        peer = lax.rem(me + q, count)
+        pltpu.make_async_remote_copy(
+            src_ref=payload_ref.at[peer],
+            dst_ref=landing_ref.at[me],
+            send_sem=send_sem,
+            recv_sem=recv_sem,
+            device_id=(peer // inner, peer % inner),
+            device_id_type=pl.DeviceIdType.MESH,
+        ).start()
+        return carry
+
+    lax.fori_loop(1, count, send, 0)
+    own = pltpu.make_async_copy(payload_ref.at[me], landing_ref.at[me], local_sem)
+    own.start()
+    own.wait()
+    everything = pltpu.make_async_remote_copy(
+        src_ref=payload_ref.at[pl.ds(0, count - 1)],
+        dst_ref=landing_ref.at[pl.ds(0, count - 1)],
+        send_sem=send_sem,
+        recv_sem=recv_sem,
+        device_id=(0, 0),
+        device_id_type=pl.DeviceIdType.MESH,
+    )
+    everything.wait_send()
+    everything.wait_recv()
+
+def exchange(payload, axes, sizes):
+    return pl.pallas_call(
+        functools.partial(exchange_kernel, axes, sizes),
+        out_shape=jax.ShapeDtypeStruct(payload.shape, payload.dtype),
+        in_specs=[pl.BlockSpec(memory_space=pl.ANY)],
+        out_specs=pl.BlockSpec(memory_space=pl.ANY),
+        scratch_shapes=[pltpu.SemaphoreType.DMA, pltpu.SemaphoreType.DMA, pltpu.SemaphoreType.DMA],
+        compiler_params=pltpu.CompilerParams(collective_id=0, has_side_effects=True),
+    )(payload)
+
+
 def body(
+    sizes,
     charges,
     leaf_size,
     leaf_basis,
@@ -175,9 +229,13 @@
     arrived_rows, coef_top = build_payload(
         charges, leaf_size, leaf_parent, send_leaf, send_mid, leaf_basis, leaf_transfer, mid_transfer
     )
-    arrived = lax.all_to_all(
-        arrived_rows, ("group", "cluster"), split_axis=0, concat_axis=0, tiled=True
-    )
+    owners_total = send_leaf.shape[0] // 2
+    landing = exchange(
+        arrived_rows.reshape((owners_total, -1) + arrived_rows.shape[1:]),
+        ("group", "cluster"),
+        sizes,
+    )
+    arrived = landing.reshape(arrived_rows.shape)
 
     listed = top_pairs.shape[1]
     position = lax.axis_index("cluster")
@@ -225,4 +283,5 @@
         P("group", None, None),
     )
     out_specs = P(("group", "cluster"), None)
-    return jax.shard_map(body, mesh=mesh, in_specs=in_specs, out_specs=out_specs, check_vma=False)
+    sizes = (mesh.shape["group"], mesh.shape["cluster"])
+    return jax.shard_map(functools.partial(body, sizes), mesh=mesh, in_specs=in_specs, out_specs=out_specs, check_vma=False)

time: 336 us -> 546 us (1.62)
  the two profiles are of different devices: /device:TPU:24 before, /device:TPU:125 now
where the time goes in v6:
time: 546 us
  Pallas kernels  526 us (96%)
  between operations  13.5 us (2%)
    pallas_call x1, Pallas kernels, exchange(): pl.pallas_call(functools.partial(exchange_kernel, axes, sizes), out_shape...  463 us
    pallas_call x2, Pallas kernels, couple_pallas(): pl.pallas_call(functools.partial(couple_kernel, nb, listed, total), grid_...  34.6 us
    pallas_call x1, Pallas kernels, build_payload(): pl.pallas_call(functools.partial(payload_kernel, chunk), grid_spec=grid_s...  18.6 us
  transfers between devices with their start and end apart: 1, of which 0 were waited for; matrix products, arithmetic and copies ran while one was open for 0% of the time, Pallas kernels for 91%

profile of v6, /device:TPU:125, one launch (start us, length us, event | category | flops | bytes accessed | tf_op | source)
XLA Modules:
  0.0 546.0 jit_solution(8813380816966178954)
XLA Ops:
  6.5 0.0 copy-start
  6.5 0.0 all-gather.3.cloned.1.call-start
  6.5 18.6 %shard_map.136 = (f32[512,64,128]{2,1,0:T(8,128)}, f32[64,128]{1,0:T(8,128)}) custom-call(s32[32]{0:T(128)} %size_ref.3, s32[32]{0:T(128)} %parent_ref.3, s32[256]{0:T(256)} %send_leaf_ref.1, s32[256]{0:T(256)} %send_mid_ref.1, f32[8192,128]{1,0:T(8,128)} %charges_ref.1, f32[32,64,256]{2,1,0:T(8,128)} %basis_ref.3, f32[32,64,64]{2,1,0:T(8,128)} %transfer_ref.3, ...), custom_call_target="tpu_custom_call" | custom-call | flops 134217728 | bytes 23068672 | tf_op jit(solution)/shard_map/pallas_call | solution.py:111
  25.2 0.0 all-gather.3.cloned.1.call-update
  25.2 0.0 copy-done.2
  25.2 0.1 copy.17
  25.3 0.0 copy-done.4
  25.4 0.1 copy.16
  25.5 0.7 reshape.115.idx_ref
  26.2 463.0 %shard_map.137 = f32[128,4,64,128]{3,2,1,0:T(8,128)} custom-call(f32[128,4,64,128]{3,2,1,0:T(8,128)} %bitcast.22), custom_call_target="tpu_custom_call" | custom-call | tf_op jit(solution)/shard_map/pallas_call | solution.py:197
  489.2 0.0 copy-done.5
  489.2 0.6 reshape.118.idx_ref
  489.8 0.0 copy-done.3
  489.8 0.2 clamp_reduce_fusion
  490.0 0.2 and_reduce_fusion
  490.2 15.1 %shard_map.139 = f32[8,64,128]{2,1,0:T(8,128)} custom-call(s32[256]{0:T(256)} %reshape.118.idx_ref, f32[512,64,128]{2,1,0:T(8,128)} %bitcast.20, f32[8,64,2048]{2,1,0:T(8,128)} %coupling_ref.3), custom_call_target="tpu_custom_call" | custom-call | flops 268435456 | bytes 21233664 | tf_op jit(solution)/shard_map/pallas_call | solution.py:49
  505.3 19.5 %shard_map.138.near_ref = f32[32,64,128]{2,1,0:T(8,128)} custom-call(s32[384]{0:T(512)} %reshape.115.idx_ref, f32[512,64,128]{2,1,0:T(8,128)} %bitcast.21, f32[32,64,768]{2,1,0:T(8,128)} %coupling_ref.2), custom_call_target="tpu_custom_call" | custom-call | flops 402653184 | bytes 24117248 | tf_op jit(solution)/shard_map/pallas_call | solution.py:49
  524.8 0.0 all-gather.3.cloned.1.call-done
  524.8 2.7 gather_fusion
  527.6 0.1 select_select_fusion
  527.7 0.2 fusion
  527.9 0.4 fusion.16
  528.3 0.7 add.40.down_mid_ref
  529.0 10.1 %shard_map.140 = f32[8192,128]{1,0:T(8,128)} custom-call(s32[32]{0:T(128)} %size_ref.3, s32[32]{0:T(128)} %parent_ref.3, f32[32,64,128]{2,1,0:T(8,128)} %shard_map.138.near_ref, f32[32,64,64]{2,1,0:T(8,128)} %transfer_ref.3, f32[32,64,256]{2,1,0:T(8,128)} %basis_ref.3, f32[8,64,128]{2,1,0:T(8,128)} %add.40.down_mid_ref), custom_call_target="tpu_custom_call" | custom-call | flops 134217728 | bytes 10485760 | tf_op jit(solution)/shard_map/pallas_call | solution.py:145
  (12 shorter events, 0.1 us)
Async XLA Ops:
  6.5 521.2 %copy-start = (f32[32,64,256]{2,1,0:T(8,128)S(1)}, f32[32,64,256]{2,1,0:T(8,128)}, u32[]{:S(2)}) copy-start(f32[32,64,256]{2,1,0:T(8,128)} %param.27) | copy-start | bytes 6291460
  6.5 18.7 %copy-start.2 = (f32[8,64,64]{2,1,0:T(8,128)S(1)}, f32[8,64,64]{2,1,0:T(8,128)}, u32[]{:S(2)}) copy-start(f32[8,64,64]{2,1,0:T(8,128)} %mid_transfer_ref.1) | copy-start | bytes 393220
  6.5 18.8 %copy-start.4 = (s32[32,12]{0,1:T(8,128)S(1)}, s32[32,12]{0,1:T(8,128)}, u32[]{:S(2)}) copy-start(s32[32,12]{0,1:T(8,128)} %param.21) | copy-start | bytes 4612
  6.5 518.3 %all-gather.3.cloned.1.call-start = ((), (), s32[]{:S(2)}) async-start(), calls=%async_computation | async-start | bytes 4227072 | tf_op jit(solution)/shard_map/all_gather | solution.py:244
  26.2 463.0 %copy-start.5 = (s32[8,32]{1,0:T(8,128)S(1)}, s32[8,32]{1,0:T(8,128)}, u32[]{:S(2)}) copy-start(s32[8,32]{1,0:T(8,128)} %param.24) | copy-start | bytes 3076
  26.2 463.7 %copy-start.3 = (s32[32,4]{0,1:T(4,128)S(1)}, s32[32,4]{0,1:T(4,128)}, u32[]{:S(2)}) copy-start(s32[32,4]{0,1:T(4,128)} %param.26) | copy-start | bytes 1540
  505.3 23.0 %copy-start.1 = (f32[8,64,128]{2,1,0:T(8,128)S(1)}, f32[8,64,128]{2,1,0:T(8,128)}, u32[]{:S(2)}) copy-start(f32[8,64,128]{2,1,0:T(8,128)} %shard_map.139) | copy-start | bytes 786436
Sparse Core Ops, SparseCore 0:
  25.3 379.8 all-gather.2

commit v7 on v6

--- a/solution.py
+++ b/solution.py
@@ -1,4 +1,5 @@
 import functools
+import math
 
 import jax
 import jax.numpy as jnp
@@ -166,8 +167,10 @@
     lax.fori_loop(1, count, greet, 0)
     pl.semaphore_wait(barrier, count - 1)
 
-    def send(q, carry):
-        peer = lax.rem(me + q, count)
+    stride = 37 if math.gcd(37, count) == 1 else 1
+
+    def send(k, carry):
+        peer = lax.rem(me + lax.rem(k * stride, count), count)
         pltpu.make_async_remote_copy(
             src_ref=payload_ref.at[peer],
             dst_ref=landing_ref.at[me],

time: 546 us -> 337 us (0.62)
  the two profiles are of different devices: /device:TPU:125 before, /device:TPU:69 now
where the time goes in v7:
time: 337 us
  Pallas kernels  318 us (94%)
  between operations  13.5 us (4%)
  local copies, waits for them, and re-layouts  4.3 us (1%)
    pallas_call x1, Pallas kernels, exchange(): pl.pallas_call(functools.partial(exchange_kernel, axes, sizes), out_shape...  254 us
    pallas_call x2, Pallas kernels, couple_pallas(): pl.pallas_call(functools.partial(couple_kernel, nb, listed, total), grid_...  34.6 us
    pallas_call x1, Pallas kernels, build_payload(): pl.pallas_call(functools.partial(payload_kernel, chunk), grid_spec=grid_s...  18.6 us
    pallas_call x1, Pallas kernels, far_field_pallas(): pl.pallas_call(functools.partial(far_kernel, nb), grid_spec=grid_spec, ou...  10.1 us
  transfers between devices with their start and end apart: 1, of which 0 were waited for; matrix products, arithmetic and copies ran while one was open for 1% of the time, Pallas kernels for 86%

profile of v7, /device:TPU:69, one launch (start us, length us, event | category | flops | bytes accessed | tf_op | source)
XLA Modules:
  0.0 337.2 jit_solution(3236351004545621607)
XLA Ops:
  6.5 0.0 copy-start
  6.5 0.0 all-gather.3.cloned.1.call-start
  6.5 18.6 %shard_map.136 = (f32[512,64,128]{2,1,0:T(8,128)}, f32[64,128]{1,0:T(8,128)}) custom-call(s32[32]{0:T(128)} %size_ref.3, s32[32]{0:T(128)} %parent_ref.3, s32[256]{0:T(256)} %send_leaf_ref.1, s32[256]{0:T(256)} %send_mid_ref.1, f32[8192,128]{1,0:T(8,128)} %charges_ref.1, f32[32,64,256]{2,1,0:T(8,128)} %basis_ref.3, f32[32,64,64]{2,1,0:T(8,128)} %transfer_ref.3, ...), custom_call_target="tpu_custom_call" | custom-call | flops 134217728 | bytes 23068672 | tf_op jit(solution)/shard_map/pallas_call | solution.py:112
  25.2 0.0 all-gather.3.cloned.1.call-update
  25.2 0.0 copy-done.2
  25.2 0.1 copy.17
  25.3 0.0 copy-done.4
  25.4 0.1 copy.16
  25.5 0.7 reshape.115.idx_ref
  26.2 254.2 %shard_map.137 = f32[128,4,64,128]{3,2,1,0:T(8,128)} custom-call(f32[128,4,64,128]{3,2,1,0:T(8,128)} %bitcast.22), custom_call_target="tpu_custom_call" | custom-call | tf_op jit(solution)/shard_map/pallas_call | solution.py:200
  280.3 0.0 copy-done.5
  280.4 0.6 reshape.118.idx_ref
  281.0 0.0 copy-done.3
  281.0 0.2 clamp_reduce_fusion
  281.2 0.2 and_reduce_fusion
  281.4 15.1 %shard_map.139 = f32[8,64,128]{2,1,0:T(8,128)} custom-call(s32[256]{0:T(256)} %reshape.118.idx_ref, f32[512,64,128]{2,1,0:T(8,128)} %bitcast.20, f32[8,64,2048]{2,1,0:T(8,128)} %coupling_ref.3), custom_call_target="tpu_custom_call" | custom-call | flops 268435456 | bytes 21233664 | tf_op jit(solution)/shard_map/pallas_call | solution.py:50
  296.5 19.5 %shard_map.138.near_ref = f32[32,64,128]{2,1,0:T(8,128)} custom-call(s32[384]{0:T(512)} %reshape.115.idx_ref, f32[512,64,128]{2,1,0:T(8,128)} %bitcast.21, f32[32,64,768]{2,1,0:T(8,128)} %coupling_ref.2), custom_call_target="tpu_custom_call" | custom-call | flops 402653184 | bytes 24117248 | tf_op jit(solution)/shard_map/pallas_call | solution.py:50
  316.0 0.0 all-gather.3.cloned.1.call-done
  316.0 2.7 gather_fusion
  318.8 0.1 select_select_fusion
  318.9 0.2 fusion
  319.1 0.4 fusion.16
  319.5 0.7 add.40.down_mid_ref
  320.2 10.1 %shard_map.140 = f32[8192,128]{1,0:T(8,128)} custom-call(s32[32]{0:T(128)} %size_ref.3, s32[32]{0:T(128)} %parent_ref.3, f32[32,64,128]{2,1,0:T(8,128)} %shard_map.138.near_ref, f32[32,64,64]{2,1,0:T(8,128)} %transfer_ref.3, f32[32,64,256]{2,1,0:T(8,128)} %basis_ref.3, f32[8,64,128]{2,1,0:T(8,128)} %add.40.down_mid_ref), custom_call_target="tpu_custom_call" | custom-call | flops 134217728 | bytes 10485760 | tf_op jit(solution)/shard_map/pallas_call | solution.py:146
  (12 shorter events, 0.1 us)
Async XLA Ops:
  6.5 312.3 %copy-start = (f32[32,64,256]{2,1,0:T(8,128)S(1)}, f32[32,64,256]{2,1,0:T(8,128)}, u32[]{:S(2)}) copy-start(f32[32,64,256]{2,1,0:T(8,128)} %param.27) | copy-start | bytes 6291460
  6.5 18.7 %copy-start.2 = (f32[8,64,64]{2,1,0:T(8,128)S(1)}, f32[8,64,64]{2,1,0:T(8,128)}, u32[]{:S(2)}) copy-start(f32[8,64,64]{2,1,0:T(8,128)} %mid_transfer_ref.1) | copy-start | bytes 393220
  6.5 18.8 %copy-start.4 = (s32[32,12]{0,1:T(8,128)S(1)}, s32[32,12]{0,1:T(8,128)}, u32[]{:S(2)}) copy-start(s32[32,12]{0,1:T(8,128)} %param.21) | copy-start | bytes 4612
  6.5 309.5 %all-gather.3.cloned.1.call-start = ((), (), s32[]{:S(2)}) async-start(), calls=%async_computation | async-start | bytes 4227072 | tf_op jit(solution)/shard_map/all_gather | solution.py:247
  26.2 254.2 %copy-start.5 = (s32[8,32]{1,0:T(8,128)S(1)}, s32[8,32]{1,0:T(8,128)}, u32[]{:S(2)}) copy-start(s32[8,32]{1,0:T(8,128)} %param.24) | copy-start | bytes 3076
  26.2 254.8 %copy-start.3 = (s32[32,4]{0,1:T(4,128)S(1)}, s32[32,4]{0,1:T(4,128)}, u32[]{:S(2)}) copy-start(s32[32,4]{0,1:T(4,128)} %param.26) | copy-start | bytes 1540
  296.5 23.0 %copy-start.1 = (f32[8,64,128]{2,1,0:T(8,128)S(1)}, f32[8,64,128]{2,1,0:T(8,128)}, u32[]{:S(2)}) copy-start(f32[8,64,128]{2,1,0:T(8,128)} %shard_map.139) | copy-start | bytes 786436
Sparse Core Ops, SparseCore 0:
  25.3 234.7 all-gather.2

commit v8 on v7

--- a/solution.py
+++ b/solution.py
@@ -27,7 +27,7 @@
             valid = r < total
             blk = arrived_ref[jnp.minimum(r, total - 1)]
             c = coupling_ref[t, :, k * rank : (k + 1) * rank]
-            prod = jnp.dot(c, blk, precision=exact_mode, preferred_element_type=jnp.float32)
+            prod = jnp.dot(c, blk, precision=lax.Precision.HIGH, preferred_element_type=jnp.float32)
             acc = acc + jnp.where(valid, prod, 0.0)
         out_ref[t] = acc
 

time: 337 us -> 329 us (0.976)
  the two profiles are of different devices: /device:TPU:69 before, /device:TPU:24 now
where the time goes in v8:
time: 329 us
  Pallas kernels  309 us (94%)
  between operations  13.5 us (4%)
  local copies, waits for them, and re-layouts  4.3 us (1%)
    pallas_call x1, Pallas kernels, exchange(): pl.pallas_call(functools.partial(exchange_kernel, axes, sizes), out_shape...  253 us
    pallas_call x2, Pallas kernels, couple_pallas(): pl.pallas_call(functools.partial(couple_kernel, nb, listed, total), grid_...  27.4 us
    pallas_call x1, Pallas kernels, build_payload(): pl.pallas_call(functools.partial(payload_kernel, chunk), grid_spec=grid_s...  18.6 us
    pallas_call x1, Pallas kernels, far_field_pallas(): pl.pallas_call(functools.partial(far_kernel, nb), grid_spec=grid_spec, ou...  10.1 us
  transfers between devices with their start and end apart: 1, of which 0 were waited for; matrix products, arithmetic and copies ran while one was open for 1% of the time, Pallas kernels for 85%

profile of v8, /device:TPU:24, one launch (start us, length us, event | category | flops | bytes accessed | tf_op | source)
XLA Modules:
  0.0 328.9 jit_solution(5514926850321561023)
XLA Ops:
  6.5 0.0 copy-start
  6.5 0.0 all-gather.3.cloned.1.call-start
  6.5 18.6 %shard_map.136 = (f32[512,64,128]{2,1,0:T(8,128)}, f32[64,128]{1,0:T(8,128)}) custom-call(s32[32]{0:T(128)} %size_ref.3, s32[32]{0:T(128)} %parent_ref.3, s32[256]{0:T(256)} %send_leaf_ref.1, s32[256]{0:T(256)} %send_mid_ref.1, f32[8192,128]{1,0:T(8,128)} %charges_ref.1, f32[32,64,256]{2,1,0:T(8,128)} %basis_ref.3, f32[32,64,64]{2,1,0:T(8,128)} %transfer_ref.3, ...), custom_call_target="tpu_custom_call" | custom-call | flops 134217728 | bytes 23068672 | tf_op jit(solution)/shard_map/pallas_call | solution.py:112
  25.2 0.0 all-gather.3.cloned.1.call-update
  25.2 0.0 copy-done.2
  25.2 0.1 copy.17
  25.3 0.0 copy-done.4
  25.4 0.1 copy.16
  25.5 0.7 reshape.115.idx_ref
  26.2 253.1 %shard_map.137 = f32[128,4,64,128]{3,2,1,0:T(8,128)} custom-call(f32[128,4,64,128]{3,2,1,0:T(8,128)} %bitcast.22), custom_call_target="tpu_custom_call" | custom-call | tf_op jit(solution)/shard_map/pallas_call | solution.py:200
  279.2 0.0 copy-done.5
  279.3 0.6 reshape.118.idx_ref
  279.9 0.0 copy-done.3
  279.9 0.2 clamp_reduce_fusion
  280.1 0.2 and_reduce_fusion
  280.3 11.9 %shard_map.139 = f32[8,64,128]{2,1,0:T(8,128)} custom-call(s32[256]{0:T(256)} %reshape.118.idx_ref, f32[512,64,128]{2,1,0:T(8,128)} %bitcast.20, f32[8,64,2048]{2,1,0:T(8,128)} %coupling_ref.3), custom_call_target="tpu_custom_call" | custom-call | flops 268435456 | bytes 21233664 | tf_op jit(solution)/shard_map/pallas_call | solution.py:50
  292.2 15.5 %shard_map.138.near_ref = f32[32,64,128]{2,1,0:T(8,128)} custom-call(s32[384]{0:T(512)} %reshape.115.idx_ref, f32[512,64,128]{2,1,0:T(8,128)} %bitcast.21, f32[32,64,768]{2,1,0:T(8,128)} %coupling_ref.2), custom_call_target="tpu_custom_call" | custom-call | flops 402653184 | bytes 24117248 | tf_op jit(solution)/shard_map/pallas_call | solution.py:50
  307.7 0.0 all-gather.3.cloned.1.call-done
  307.7 2.7 gather_fusion
  310.5 0.1 select_select_fusion
  310.6 0.2 fusion
  310.8 0.4 fusion.16
  311.2 0.7 add.40.down_mid_ref
  311.9 10.1 %shard_map.140 = f32[8192,128]{1,0:T(8,128)} custom-call(s32[32]{0:T(128)} %size_ref.3, s32[32]{0:T(128)} %parent_ref.3, f32[32,64,128]{2,1,0:T(8,128)} %shard_map.138.near_ref, f32[32,64,64]{2,1,0:T(8,128)} %transfer_ref.3, f32[32,64,256]{2,1,0:T(8,128)} %basis_ref.3, f32[8,64,128]{2,1,0:T(8,128)} %add.40.down_mid_ref), custom_call_target="tpu_custom_call" | custom-call | flops 134217728 | bytes 10485760 | tf_op jit(solution)/shard_map/pallas_call | solution.py:146
  (12 shorter events, 0.1 us)
Async XLA Ops:
  6.5 304.0 %copy-start = (f32[32,64,256]{2,1,0:T(8,128)S(1)}, f32[32,64,256]{2,1,0:T(8,128)}, u32[]{:S(2)}) copy-start(f32[32,64,256]{2,1,0:T(8,128)} %param.27) | copy-start | bytes 6291460
  6.5 18.7 %copy-start.2 = (f32[8,64,64]{2,1,0:T(8,128)S(1)}, f32[8,64,64]{2,1,0:T(8,128)}, u32[]{:S(2)}) copy-start(f32[8,64,64]{2,1,0:T(8,128)} %mid_transfer_ref.1) | copy-start | bytes 393220
  6.5 18.8 %copy-start.4 = (s32[32,12]{0,1:T(8,128)S(1)}, s32[32,12]{0,1:T(8,128)}, u32[]{:S(2)}) copy-start(s32[32,12]{0,1:T(8,128)} %param.21) | copy-start | bytes 4612
  6.5 301.2 %all-gather.3.cloned.1.call-start = ((), (), s32[]{:S(2)}) async-start(), calls=%async_computation | async-start | bytes 4227072 | tf_op jit(solution)/shard_map/all_gather | solution.py:247
  26.2 253.1 %copy-start.5 = (s32[8,32]{1,0:T(8,128)S(1)}, s32[8,32]{1,0:T(8,128)}, u32[]{:S(2)}) copy-start(s32[8,32]{1,0:T(8,128)} %param.24) | copy-start | bytes 3076
  26.2 253.7 %copy-start.3 = (s32[32,4]{0,1:T(4,128)S(1)}, s32[32,4]{0,1:T(4,128)}, u32[]{:S(2)}) copy-start(s32[32,4]{0,1:T(4,128)} %param.26) | copy-start | bytes 1540
  292.2 19.0 %copy-start.1 = (f32[8,64,128]{2,1,0:T(8,128)S(1)}, f32[8,64,128]{2,1,0:T(8,128)}, u32[]{:S(2)}) copy-start(f32[8,64,128]{2,1,0:T(8,128)} %shard_map.139) | copy-start | bytes 786436
Sparse Core Ops, SparseCore 0:
  25.3 229.3 all-gather.2

commit v9 on v5

--- a/solution.py
+++ b/solution.py
@@ -1,4 +1,5 @@
 import functools
+import math
 
 import jax
 import jax.numpy as jnp
@@ -26,7 +27,7 @@
             valid = r < total
             blk = arrived_ref[jnp.minimum(r, total - 1)]
             c = coupling_ref[t, :, k * rank : (k + 1) * rank]
-            prod = jnp.dot(c, blk, precision=exact_mode, preferred_element_type=jnp.float32)
+            prod = jnp.dot(c, blk, precision=lax.Precision.HIGH, preferred_element_type=jnp.float32)
             acc = acc + jnp.where(valid, prod, 0.0)
         out_ref[t] = acc
 
@@ -60,7 +61,7 @@
 
 
 def payload_kernel(chunk, size_ref, parent_ref, send_leaf_ref, send_mid_ref, charges_ref, basis_ref,
-                   transfer_ref, mid_transfer_ref, out_ref, top_ref, leaf_sc, mid_sc):
+                   transfer_ref, mid_transfer_ref, out_ref, mid_out_ref, top_ref, leaf_sc, mid_sc):
     i = pl.program_id(0)
     leaves, rank, points = basis_ref.shape
     mids = mid_transfer_ref.shape[0]
@@ -83,21 +84,21 @@
                                 preferred_element_type=jnp.float32)
         top_ref[...] = top
 
-    per = chunk // 4
+    per = chunk // 2
     for q in range(per):
         r = i * per + q
         for j in range(2):
             a = send_leaf_ref[r * 2 + j]
-            out_ref[q * 4 + j] = jnp.where(a < leaves, leaf_sc[jnp.minimum(a, leaves - 1)], 0.0)
+            out_ref[q * 2 + j] = jnp.where(a < leaves, leaf_sc[jnp.minimum(a, leaves - 1)], 0.0)
             b = send_mid_ref[r * 2 + j]
-            out_ref[q * 4 + 2 + j] = jnp.where(b < mids, mid_sc[jnp.minimum(b, mids - 1)], 0.0)
+            mid_out_ref[q * 2 + j] = jnp.where(b < mids, mid_sc[jnp.minimum(b, mids - 1)], 0.0)
 
 def build_payload(charges, leaf_size, leaf_parent, send_leaf, send_mid, leaf_basis, leaf_transfer, mid_transfer, steps=8):
     leaves, rank, points = leaf_basis.shape
     ports = charges.shape[1]
     mids = mid_transfer.shape[0]
     owners = send_leaf.shape[0] // 2
-    total = owners * 4
+    total = owners * 2
     chunk = total // steps
     full = lambda shape: pl.BlockSpec(shape, lambda i, *_: (0,) * len(shape), pipeline_mode=pl.Buffered(1))
     grid_spec = pltpu.PrefetchScalarGridSpec(
@@ -105,15 +106,18 @@
         grid=(steps,),
         in_specs=[full(charges.shape), full(leaf_basis.shape), full(leaf_transfer.shape), full(mid_transfer.shape)],
         out_specs=[pl.BlockSpec((chunk, rank, ports), lambda i, *_: (i, 0, 0)),
+                   pl.BlockSpec((chunk, rank, ports), lambda i, *_: (i, 0, 0)),
                    pl.BlockSpec((rank, ports), lambda i, *_: (0, 0))],
         scratch_shapes=[pltpu.VMEM((leaves, rank, ports), jnp.float32), pltpu.VMEM((mids, rank, ports), jnp.float32)],
     )
     return pl.pallas_call(
         functools.partial(payload_kernel, chunk),
         grid_spec=grid_spec,
-        out_shape=[jax.ShapeDtypeStruct((total, rank, ports), jnp.float32), jax.ShapeDtypeStruct((rank, ports), jnp.float32)],
+        out_shape=[jax.ShapeDtypeStruct((total, rank, ports), jnp.float32),
+                   jax.ShapeDtypeStruct((total, rank, ports), jnp.float32),
+                   jax.ShapeDtypeStruct((rank, ports), jnp.float32)],
         compiler_params=pltpu.CompilerParams(vmem_limit_bytes=60 * 1024 * 1024, dimension_semantics=("arbitrary",)),
-        cost_estimate=pl.CostEstimate(flops=2 * leaves * rank * points * ports, bytes_accessed=4 * (charges.size + leaf_basis.size + total * rank * ports), transcendentals=0),
+        cost_estimate=pl.CostEstimate(flops=2 * leaves * rank * points * ports, bytes_accessed=4 * (charges.size + leaf_basis.size + 2 * total * rank * ports), transcendentals=0),
     )(leaf_size, leaf_parent, send_leaf, send_mid, charges, leaf_basis, leaf_transfer, mid_transfer)
 
 def far_kernel(nb, size_ref, parent_ref, near_ref, transfer_ref, basis_ref, down_mid_ref, out_ref):
@@ -151,7 +155,115 @@
     )(leaf_size, leaf_parent, near_leaf, leaf_transfer, leaf_basis, down_mid)
 
 
+def couple_rows(pairs_ref, land_ref, coupling_ref, out_ref, listed):
+    total = land_ref.shape[0]
+    rank = land_ref.shape[1]
+
+    def target(t, carry):
+        acc = jnp.zeros(out_ref.shape[1:], jnp.float32)
+        for k in range(listed):
+            r = pairs_ref[t * listed + k]
+            blk = land_ref[jnp.minimum(r, total - 1)]
+            c = coupling_ref[t, :, k * rank : (k + 1) * rank]
+            prod = jnp.dot(c, blk, precision=lax.Precision.HIGH, preferred_element_type=jnp.float32)
+            acc = acc + jnp.where(r < total, prod, 0.0)
+        out_ref[t] = acc
+        return carry
+
+    lax.fori_loop(0, out_ref.shape[0], target, 0)
+
+
+def exchange_couple_kernel(axes, sizes, pair_leaf_ref, pair_mid_ref, leaf_pay_ref, mid_pay_ref,
+                           leaf_coupling_ref, mid_coupling_ref, near_leaf_ref, near_mid_ref,
+                           leaf_land, mid_land, sems):
+    outer, inner = sizes
+    count = outer * inner
+    me = lax.axis_index(axes[0]) * inner + lax.axis_index(axes[1])
+    barrier = pltpu.get_barrier_semaphore()
+
+    def greet(q, carry):
+        peer = lax.rem(me + q, count)
+        pl.semaphore_signal(barrier, 1, device_id=(peer // inner, peer % inner),
+                            device_id_type=pl.DeviceIdType.MESH)
+        return carry
+
+    lax.fori_loop(1, count, greet, 0)
+    pl.semaphore_wait(barrier, count - 1)
+    stride = 37 if math.gcd(37, count) == 1 else 1
+    slots = leaf_pay_ref.shape[0] // count
+
+    def sender(pay_ref, land_ref, send_sem, recv_sem):
+        def send(k, carry):
+            peer = lax.rem(me + lax.rem(k * stride, count), count)
+            pltpu.make_async_remote_copy(
+                src_ref=pay_ref.at[pl.ds(peer * slots, slots)],
+                dst_ref=land_ref.at[pl.ds(me * slots, slots)],
+                send_sem=send_sem,
+                recv_sem=recv_sem,
+                device_id=(peer // inner, peer % inner),
+                device_id_type=pl.DeviceIdType.MESH,
+            ).start()
+            return carry
+
+        lax.fori_loop(1, count, send, 0)
+
+    def everything(pay_ref, land_ref, send_sem, recv_sem):
+        return pltpu.make_async_remote_copy(
+            src_ref=pay_ref.at[pl.ds(0, (count - 1) * slots)],
+            dst_ref=land_ref.at[pl.ds(0, (count - 1) * slots)],
+            send_sem=send_sem,
+            recv_sem=recv_sem,
+            device_id=(0, 0),
+            device_id_type=pl.DeviceIdType.MESH,
+        )
+
+    sender(leaf_pay_ref, leaf_land, sems.at[0], sems.at[1])
+    own_leaf = pltpu.make_async_copy(leaf_pay_ref.at[pl.ds(me * slots, slots)],
+                                     leaf_land.at[pl.ds(me * slots, slots)], sems.at[4])
+    own_leaf.start()
+    sender(mid_pay_ref, mid_land, sems.at[2], sems.at[3])
+    own_mid = pltpu.make_async_copy(mid_pay_ref.at[pl.ds(me * slots, slots)],
+                                    mid_land.at[pl.ds(me * slots, slots)], sems.at[5])
+    own_mid.start()
+
+    leaf_all = everything(leaf_pay_ref, leaf_land, sems.at[0], sems.at[1])
+    mid_all = everything(mid_pay_ref, mid_land, sems.at[2], sems.at[3])
+    own_leaf.wait()
+    leaf_all.wait_recv()
+    couple_rows(pair_leaf_ref, leaf_land, leaf_coupling_ref, near_leaf_ref, pair_leaf_ref.shape[0] // near_leaf_ref.shape[0])
+    own_mid.wait()
+    mid_all.wait_recv()
+    couple_rows(pair_mid_ref, mid_land, mid_coupling_ref, near_mid_ref, pair_mid_ref.shape[0] // near_mid_ref.shape[0])
+    leaf_all.wait_send()
+    mid_all.wait_send()
+
+
+def exchange_couple(pair_leaf, pair_mid, leaf_pay, mid_pay, leaf_coupling, mid_coupling, axes, sizes):
+    rank, ports = leaf_pay.shape[1:]
+    n_leaf = leaf_coupling.shape[0]
+    n_mid = mid_coupling.shape[0]
+    vmem = pl.BlockSpec(memory_space=pltpu.VMEM)
+    smem = pl.BlockSpec(memory_space=pltpu.SMEM)
+    hbm = pl.BlockSpec(memory_space=pl.ANY)
+    return pl.pallas_call(
+        functools.partial(exchange_couple_kernel, axes, sizes),
+        out_shape=[jax.ShapeDtypeStruct((n_leaf, rank, ports), jnp.float32),
+                   jax.ShapeDtypeStruct((n_mid, rank, ports), jnp.float32)],
+        in_specs=[smem, smem, hbm, hbm, vmem, vmem],
+        out_specs=[vmem, vmem],
+        scratch_shapes=[pltpu.VMEM(leaf_pay.shape, jnp.float32), pltpu.VMEM(mid_pay.shape, jnp.float32),
+                        pltpu.SemaphoreType.DMA((6,))],
+        compiler_params=pltpu.CompilerParams(collective_id=0, has_side_effects=True,
+                                             vmem_limit_bytes=62 * 1024 * 1024),
+        cost_estimate=pl.CostEstimate(
+            flops=2 * (leaf_coupling.size + mid_coupling.size) * ports,
+            bytes_accessed=4 * (leaf_pay.size + mid_pay.size + leaf_coupling.size + mid_coupling.size),
+            transcendentals=0),
+    )(pair_leaf.reshape(-1), pair_mid.reshape(-1), leaf_pay, mid_pay, leaf_coupling, mid_coupling)
+
+
 def body(
+    sizes,
     charges,
     leaf_size,
     leaf_basis,
@@ -172,11 +284,11 @@
     mid_count = mid_transfer.shape[0]
     owners = send_leaf.shape[0] // 2
     slots = 2
-    arrived_rows, coef_top = build_payload(
+    leaf_pay, mid_pay, coef_top = build_payload(
         charges, leaf_size, leaf_parent, send_leaf, send_mid, leaf_basis, leaf_transfer, mid_transfer
     )
-    arrived = lax.all_to_all(
-        arrived_rows, ("group", "cluster"), split_axis=0, concat_axis=0, tiled=True
+    near_leaf, near_mid = exchange_couple(
+        pair_leaf, pair_mid, leaf_pay, mid_pay, leaf_coupling, mid_coupling, ("group", "cluster"), sizes
     )
 
     listed = top_pairs.shape[1]
@@ -196,13 +308,6 @@
         precision=exact_mode,
     )
 
-    total_rows = owners * 2 * slots
-    live_leaf = pair_leaf < owners * slots
-    leaf_rows = jnp.where(live_leaf, pair_leaf + (pair_leaf // slots) * slots, total_rows)
-    near_leaf = couple_pallas(leaf_coupling, arrived, leaf_rows, 4)
-    live_mid = pair_mid < owners * slots
-    mid_rows = jnp.where(live_mid, pair_mid + (pair_mid // slots + 1) * slots, total_rows)
-    near_mid = couple_pallas(mid_coupling, arrived, mid_rows, 2)
     down_mid = near_mid + jnp.einsum("mjk,jp->mkp", mid_transfer, near_top, precision=exact_mode)
     return far_field_pallas(near_leaf, leaf_transfer, leaf_basis, down_mid, leaf_size, leaf_parent)
 
@@ -225,4 +330,5 @@
         P("group", None, None),
     )
     out_specs = P(("group", "cluster"), None)
-    return jax.shard_map(body, mesh=mesh, in_specs=in_specs, out_specs=out_specs, check_vma=False)
+    sizes = (mesh.shape["group"], mesh.shape["cluster"])
+    return jax.shard_map(functools.partial(body, sizes), mesh=mesh, in_specs=in_specs, out_specs=out_specs, check_vma=False)

time: 336 us -> 285 us (0.85)
  waiting for transfers between devices: 236 us -> 3.55 us
  Pallas kernels: 63.2 us -> 257 us
  starting transfers between devices: 11 us -> 0.03 us
    all_gather x1, waiting for transfers between devices: 236 us -> 3.53 us  [body(): lax.all_gather(coef_top[None], ('group', 'cluster'), axis=0, tiled=True)]
    pallas_call x2 -> x1, Pallas kernels: 34.5 us -> 228 us  [exchange_couple(): pl.pallas_call(functools.partial(exchange_couple_kernel, axes, sizes), ou...]
    all_to_all x1 -> x0, starting transfers between devices: 10.7 us -> none  [body(): lax.all_to_all(arrived_rows, ('group', 'cluster'), split_axis=0, concat_a...]
  transfers between devices with their start and end apart: 2 -> 1, of which waited for: 1 -> 1; matrix products, arithmetic and copies ran while one was open for 2% -> 1% of each run, Pallas kernels for 0% -> 81%
where the time goes in v9:
time: 285 us; the launch traced here: 282 us
  Pallas kernels  257 us (90%)
  between operations  13.5 us (5%)
  local copies, waits for them, and re-layouts  4.33 us (2%)
  waiting for transfers between devices  3.55 us (1%)
    pallas_call x1, Pallas kernels, exchange_couple(): pl.pallas_call(functools.partial(exchange_couple_kernel, axes, sizes), ou...  228 us
    pallas_call x1, Pallas kernels, build_payload(): pl.pallas_call(functools.partial(payload_kernel, chunk), grid_spec=grid_s...  18.8 us
    pallas_call x1, Pallas kernels, far_field_pallas(): pl.pallas_call(functools.partial(far_kernel, nb), grid_spec=grid_spec, ou...  10.1 us
  transfers between devices with their start and end apart: 1, of which 1 were waited for; matrix products, arithmetic and copies ran while one was open for 1% of the time, Pallas kernels for 81%

profile of v9, /device:TPU:24, one launch (start us, length us, event | category | flops | bytes accessed | tf_op | source)
XLA Modules:
  0.0 281.7 jit_solution(13166101423009939729)
XLA Ops:
  6.5 0.0 copy-start
  6.5 0.0 copy-start.1
  6.5 0.0 copy-start.2
  6.5 0.0 all-gather.3.cloned.1.call-start
  6.6 18.8 %shard_map.136 = (f32[256,64,128]{2,1,0:T(8,128)}, f32[256,64,128]{2,1,0:T(8,128)}, f32[64,128]{1,0:T(8,128)}) custom-call(s32[32]{0:T(128)} %size_ref.3, s32[32]{0:T(128)} %parent_ref.3, s32[256]{0:T(256)} %send_leaf_ref.1, s32[256]{0:T(256)} %send_mid_ref.1, f32[8192,128]{1,0:T(8,128)} %charges_ref.1, f32[32,64,256]{2,1,0:T(8,128)} %basis_ref.3, ...), custom_call_target="tpu_custom_call" | custom-call | flops 134217728 | bytes 23068672 | tf_op jit(solution)/shard_map/pallas_call | solution.py:113
  25.3 0.0 all-gather.3.cloned.1.call-update
  25.4 0.0 copy-done
  25.4 0.1 copy.17
  25.5 0.0 copy-done.1
  25.5 0.1 copy.16
  25.6 0.7 reshape.109.pair_leaf_ref
  26.3 0.0 copy-done.3
  26.3 0.7 reshape.110.pair_mid_ref
  27.0 0.0 copy-done.2
  27.0 0.2 clamp_reduce_fusion
  27.2 0.2 and_reduce_fusion
  27.4 227.8 %shard_map.137 = (f32[32,64,128]{2,1,0:T(8,128)}, f32[8,64,128]{2,1,0:T(8,128)}) custom-call(s32[384]{0:T(512)} %reshape.109.pair_leaf_ref, s32[256]{0:T(256)} %reshape.110.pair_mid_ref, f32[256,64,128]{2,1,0:T(8,128)} %get-tuple-element.10.leaf_pay_ref, f32[256,64,128]{2,1,0:T(8,128)} %get-tuple-element.11.mid_pay_ref, f32[32,64,768]{2,1,0:T(8,128)} %leaf_coupling_ref.1, ...), custom_call_target="tpu_custom_call" | custom-call | flops 671088640 | bytes 27262976 | tf_op jit(solution)/shard_map/pallas_call | solution.py:248
  255.2 3.5 %all-gather.3.cloned.1.call-done = f32[8192,128]{1,0:T(8,128)} async-done(((f32[64,128]{1,0:T(8,128)}), f32[8192,128]{1,0:T(8,128)}) %all-gather.3.cloned.1.call-update) | async-done | bytes 4194320 | tf_op jit(solution)/shard_map/all_gather | solution.py:298
  258.7 2.7 gather_fusion
  261.5 0.1 select_select_fusion
  261.6 1.1 fusion
  262.6 0.4 fusion.5
  263.0 1.7 add.25.down_mid_ref
  264.7 10.1 %shard_map.138 = f32[8192,128]{1,0:T(8,128)} custom-call(s32[32]{0:T(128)} %size_ref.3, s32[32]{0:T(128)} %parent_ref.3, f32[32,64,128]{2,1,0:T(8,128)} %get-tuple-element.12.near_ref, f32[32,64,64]{2,1,0:T(8,128)} %transfer_ref.3, f32[32,64,256]{2,1,0:T(8,128)} %basis_ref.3, f32[8,64,128]{2,1,0:T(8,128)} %add.25.down_mid_ref), custom_call_target="tpu_custom_call" | custom-call | flops 134217728 | bytes 10485760 | tf_op jit(solution)/shard_map/pallas_call | solution.py:149
  (4 shorter events, 0.0 us)
Async XLA Ops:
  6.5 18.8 %copy-start = (f32[8,64,64]{2,1,0:T(8,128)S(1)}, f32[8,64,64]{2,1,0:T(8,128)}, u32[]{:S(2)}) copy-start(f32[8,64,64]{2,1,0:T(8,128)} %mid_transfer_ref.1) | copy-start | bytes 393220
  6.5 19.0 %copy-start.1 = (s32[32,12]{0,1:T(8,128)S(1)}, s32[32,12]{0,1:T(8,128)}, u32[]{:S(2)}) copy-start(s32[32,12]{0,1:T(8,128)} %param.21) | copy-start | bytes 4612
  6.5 19.8 %copy-start.3 = (s32[8,32]{1,0:T(8,128)S(1)}, s32[8,32]{1,0:T(8,128)}, u32[]{:S(2)}) copy-start(s32[8,32]{1,0:T(8,128)} %param.24) | copy-start | bytes 3076
  6.5 20.4 %copy-start.2 = (s32[32,4]{0,1:T(4,128)S(1)}, s32[32,4]{0,1:T(4,128)}, u32[]{:S(2)}) copy-start(s32[32,4]{0,1:T(4,128)} %param.26) | copy-start | bytes 1540
  6.5 252.2 %all-gather.3.cloned.1.call-start = ((), (), s32[]{:S(2)}) async-start(), calls=%async_computation | async-start | bytes 4227072 | tf_op jit(solution)/shard_map/all_gather | solution.py:298
Sparse Core Ops, SparseCore 0:
  25.5 233.2 all-gather.2

commit v10 on v9

--- a/solution.py
+++ b/solution.py
@@ -189,7 +189,7 @@
 
     lax.fori_loop(1, count, greet, 0)
     pl.semaphore_wait(barrier, count - 1)
-    stride = 37 if math.gcd(37, count) == 1 else 1
+    stride = 2 * lax.rem(me * 37, count // 2) + 1 if count % 2 == 0 else 1
     slots = leaf_pay_ref.shape[0] // count
 
     def sender(pay_ref, land_ref, send_sem, recv_sem):

time: 285 us -> 290 us (1.018)
  Pallas kernels: 257 us -> 265 us
  waiting for transfers between devices: 3.55 us -> 0.04 us
    pallas_call x1, Pallas kernels: 228 us -> 236 us  [exchange_couple(): pl.pallas_call(functools.partial(exchange_couple_kernel, axes, sizes), ou...]
    all_gather x1, waiting for transfers between devices: 3.53 us -> 0.02 us  [body(): lax.all_gather(coef_top[None], ('group', 'cluster'), axis=0, tiled=True)]
  transfers between devices with their start and end apart: 1 -> 1, of which waited for: 1 -> 0; matrix products, arithmetic and copies ran while one was open for 1% -> 1% of each run, Pallas kernels for 81% -> 82%
where the time goes in v10:
time: 290 us; the launch traced here: 286 us
  Pallas kernels  265 us (91%)
  between operations  13.5 us (5%)
  local copies, waits for them, and re-layouts  4.34 us (1%)
    pallas_call x1, Pallas kernels, exchange_couple(): pl.pallas_call(functools.partial(exchange_couple_kernel, axes, sizes), ou...  236 us
    pallas_call x1, Pallas kernels, build_payload(): pl.pallas_call(functools.partial(payload_kernel, chunk), grid_spec=grid_s...  18.8 us
    pallas_call x1, Pallas kernels, far_field_pallas(): pl.pallas_call(functools.partial(far_kernel, nb), grid_spec=grid_spec, ou...  10.1 us
  transfers between devices with their start and end apart: 1, of which 0 were waited for; matrix products, arithmetic and copies ran while one was open for 1% of the time, Pallas kernels for 82%

profile of v10, /device:TPU:24, one launch (start us, length us, event | category | flops | bytes accessed | tf_op | source)
XLA Modules:
  0.0 286.4 jit_solution(13640124165583051995)
XLA Ops:
  6.5 0.0 copy-start
  6.5 0.0 copy-start.1
  6.5 0.0 copy-start.2
  6.5 0.0 all-gather.3.cloned.1.call-start
  6.6 18.8 %shard_map.136 = (f32[256,64,128]{2,1,0:T(8,128)}, f32[256,64,128]{2,1,0:T(8,128)}, f32[64,128]{1,0:T(8,128)}) custom-call(s32[32]{0:T(128)} %size_ref.3, s32[32]{0:T(128)} %parent_ref.3, s32[256]{0:T(256)} %send_leaf_ref.1, s32[256]{0:T(256)} %send_mid_ref.1, f32[8192,128]{1,0:T(8,128)} %charges_ref.1, f32[32,64,256]{2,1,0:T(8,128)} %basis_ref.3, ...), custom_call_target="tpu_custom_call" | custom-call | flops 134217728 | bytes 23068672 | tf_op jit(solution)/shard_map/pallas_call | solution.py:113
  25.3 0.0 all-gather.3.cloned.1.call-update
  25.4 0.0 copy-done
  25.4 0.1 copy.17
  25.5 0.0 copy-done.1
  25.5 0.1 copy.16
  25.6 0.7 reshape.109.pair_leaf_ref
  26.3 0.0 copy-done.3
  26.3 0.7 reshape.110.pair_mid_ref
  27.0 0.0 copy-done.2
  27.0 0.2 clamp_reduce_fusion
  27.2 0.2 and_reduce_fusion
  27.4 236.0 %shard_map.137 = (f32[32,64,128]{2,1,0:T(8,128)}, f32[8,64,128]{2,1,0:T(8,128)}) custom-call(s32[384]{0:T(512)} %reshape.109.pair_leaf_ref, s32[256]{0:T(256)} %reshape.110.pair_mid_ref, f32[256,64,128]{2,1,0:T(8,128)} %get-tuple-element.10.leaf_pay_ref, f32[256,64,128]{2,1,0:T(8,128)} %get-tuple-element.11.mid_pay_ref, f32[32,64,768]{2,1,0:T(8,128)} %leaf_coupling_ref.1, ...), custom_call_target="tpu_custom_call" | custom-call | flops 671088640 | bytes 27262976 | tf_op jit(solution)/shard_map/pallas_call | solution.py:248
  263.4 0.0 all-gather.3.cloned.1.call-done
  263.4 2.7 gather_fusion
  266.2 0.1 select_select_fusion
  266.3 1.1 fusion
  267.4 0.4 fusion.5
  267.7 1.7 add.25.down_mid_ref
  269.4 10.1 %shard_map.138 = f32[8192,128]{1,0:T(8,128)} custom-call(s32[32]{0:T(128)} %size_ref.3, s32[32]{0:T(128)} %parent_ref.3, f32[32,64,128]{2,1,0:T(8,128)} %get-tuple-element.12.near_ref, f32[32,64,64]{2,1,0:T(8,128)} %transfer_ref.3, f32[32,64,256]{2,1,0:T(8,128)} %basis_ref.3, f32[8,64,128]{2,1,0:T(8,128)} %add.25.down_mid_ref), custom_call_target="tpu_custom_call" | custom-call | flops 134217728 | bytes 10485760 | tf_op jit(solution)/shard_map/pallas_call | solution.py:149
  (4 shorter events, 0.0 us)
Async XLA Ops:
  6.5 18.8 %copy-start = (f32[8,64,64]{2,1,0:T(8,128)S(1)}, f32[8,64,64]{2,1,0:T(8,128)}, u32[]{:S(2)}) copy-start(f32[8,64,64]{2,1,0:T(8,128)} %mid_transfer_ref.1) | copy-start | bytes 393220
  6.5 19.0 %copy-start.1 = (s32[32,12]{0,1:T(8,128)S(1)}, s32[32,12]{0,1:T(8,128)}, u32[]{:S(2)}) copy-start(s32[32,12]{0,1:T(8,128)} %param.21) | copy-start | bytes 4612
  6.5 19.8 %copy-start.3 = (s32[8,32]{1,0:T(8,128)S(1)}, s32[8,32]{1,0:T(8,128)}, u32[]{:S(2)}) copy-start(s32[8,32]{1,0:T(8,128)} %param.24) | copy-start | bytes 3076
  6.5 20.4 %copy-start.2 = (s32[32,4]{0,1:T(4,128)S(1)}, s32[32,4]{0,1:T(4,128)}, u32[]{:S(2)}) copy-start(s32[32,4]{0,1:T(4,128)} %param.26) | copy-start | bytes 1540
  6.5 256.9 %all-gather.3.cloned.1.call-start = ((), (), s32[]{:S(2)}) async-start(), calls=%async_computation | async-start | bytes 4227072 | tf_op jit(solution)/shard_map/all_gather | solution.py:298
Sparse Core Ops, SparseCore 0:
  25.5 234.5 all-gather.2

commit v11 on v9

--- a/solution.py
+++ b/solution.py
@@ -60,65 +60,46 @@
     )(rows.reshape(-1), arrived, coupling)
 
 
-def payload_kernel(chunk, size_ref, parent_ref, send_leaf_ref, send_mid_ref, charges_ref, basis_ref,
-                   transfer_ref, mid_transfer_ref, out_ref, mid_out_ref, top_ref, leaf_sc, mid_sc):
-    i = pl.program_id(0)
+def coef_kernel(size_ref, parent_ref, charges_ref, basis_ref, transfer_ref, mid_transfer_ref,
+                leaf_ref, mid_ref, top_ref):
     leaves, rank, points = basis_ref.shape
     mids = mid_transfer_ref.shape[0]
-
-    @pl.when(i == 0)
-    def _():
-        mid_sc[...] = jnp.zeros(mid_sc.shape, jnp.float32)
-        rows = lax.broadcasted_iota(jnp.int32, (points, 1), 0)
-        for l in range(leaves):
-            blk = charges_ref[l * points:(l + 1) * points, :]
-            blk = jnp.where(rows < size_ref[l], blk, 0.0)
-            coef = jnp.dot(basis_ref[l], blk, precision=exact_mode, preferred_element_type=jnp.float32)
-            leaf_sc[l] = coef
-            up = jnp.dot(transfer_ref[l], coef, precision=exact_mode, preferred_element_type=jnp.float32)
-            p = parent_ref[l]
-            mid_sc[p] = mid_sc[p] + up
-        top = jnp.zeros(top_ref.shape, jnp.float32)
-        for c in range(mids):
-            top = top + jnp.dot(mid_transfer_ref[c], mid_sc[c], precision=exact_mode,
-                                preferred_element_type=jnp.float32)
-        top_ref[...] = top
-
-    per = chunk // 2
-    for q in range(per):
-        r = i * per + q
-        for j in range(2):
-            a = send_leaf_ref[r * 2 + j]
-            out_ref[q * 2 + j] = jnp.where(a < leaves, leaf_sc[jnp.minimum(a, leaves - 1)], 0.0)
-            b = send_mid_ref[r * 2 + j]
-            mid_out_ref[q * 2 + j] = jnp.where(b < mids, mid_sc[jnp.minimum(b, mids - 1)], 0.0)
-
-def build_payload(charges, leaf_size, leaf_parent, send_leaf, send_mid, leaf_basis, leaf_transfer, mid_transfer, steps=8):
+    mid_ref[...] = jnp.zeros(mid_ref.shape, jnp.float32)
+    rows = lax.broadcasted_iota(jnp.int32, (points, 1), 0)
+    for l in range(leaves):
+        blk = charges_ref[l * points:(l + 1) * points, :]
+        blk = jnp.where(rows < size_ref[l], blk, 0.0)
+        coef = jnp.dot(basis_ref[l], blk, precision=exact_mode, preferred_element_type=jnp.float32)
+        leaf_ref[l] = coef
+        up = jnp.dot(transfer_ref[l], coef, precision=exact_mode, preferred_element_type=jnp.float32)
+        p = parent_ref[l]
+        mid_ref[p] = mid_ref[p] + up
+    top = jnp.zeros(top_ref.shape, jnp.float32)
+    for c in range(mids):
+        top = top + jnp.dot(mid_transfer_ref[c], mid_ref[c], precision=exact_mode,
+                            preferred_element_type=jnp.float32)
+    top_ref[...] = top
+
+
+def build_coefs(charges, leaf_size, leaf_parent, leaf_basis, leaf_transfer, mid_transfer):
     leaves, rank, points = leaf_basis.shape
     ports = charges.shape[1]
     mids = mid_transfer.shape[0]
-    owners = send_leaf.shape[0] // 2
-    total = owners * 2
-    chunk = total // steps
-    full = lambda shape: pl.BlockSpec(shape, lambda i, *_: (0,) * len(shape), pipeline_mode=pl.Buffered(1))
-    grid_spec = pltpu.PrefetchScalarGridSpec(
-        num_scalar_prefetch=4,
-        grid=(steps,),
-        in_specs=[full(charges.shape), full(leaf_basis.shape), full(leaf_transfer.shape), full(mid_transfer.shape)],
-        out_specs=[pl.BlockSpec((chunk, rank, ports), lambda i, *_: (i, 0, 0)),
-                   pl.BlockSpec((chunk, rank, ports), lambda i, *_: (i, 0, 0)),
-                   pl.BlockSpec((rank, ports), lambda i, *_: (0, 0))],
-        scratch_shapes=[pltpu.VMEM((leaves, rank, ports), jnp.float32), pltpu.VMEM((mids, rank, ports), jnp.float32)],
-    )
+    vmem = pl.BlockSpec(memory_space=pltpu.VMEM)
+    smem = pl.BlockSpec(memory_space=pltpu.SMEM)
     return pl.pallas_call(
-        functools.partial(payload_kernel, chunk),
-        grid_spec=grid_spec,
-        out_shape=[jax.ShapeDtypeStruct((total, rank, ports), jnp.float32),
-                   jax.ShapeDtypeStruct((total, rank, ports), jnp.float32),
+        coef_kernel,
+        out_shape=[jax.ShapeDtypeStruct((leaves, rank, ports), jnp.float32),
+                   jax.ShapeDtypeStruct((mids, rank, ports), jnp.float32),
                    jax.ShapeDtypeStruct((rank, ports), jnp.float32)],
-        compiler_params=pltpu.CompilerParams(vmem_limit_bytes=60 * 1024 * 1024, dimension_semantics=("arbitrary",)),
-        cost_estimate=pl.CostEstimate(flops=2 * leaves * rank * points * ports, bytes_accessed=4 * (charges.size + leaf_basis.size + 2 * total * rank * ports), transcendentals=0),
-    )(leaf_size, leaf_parent, send_leaf, send_mid, charges, leaf_basis, leaf_transfer, mid_transfer)
+        in_specs=[smem, smem, vmem, vmem, vmem, vmem],
+        out_specs=[vmem, vmem, vmem],
+        compiler_params=pltpu.CompilerParams(vmem_limit_bytes=60 * 1024 * 1024),
+        cost_estimate=pl.CostEstimate(flops=2 * leaves * rank * points * ports,
+                                      bytes_accessed=4 * (charges.size + leaf_basis.size),
+                                      transcendentals=0),
+    )(leaf_size, leaf_parent, charges, leaf_basis, leaf_transfer, mid_transfer)
+
 
 def far_kernel(nb, size_ref, parent_ref, near_ref, transfer_ref, basis_ref, down_mid_ref, out_ref):
     i = pl.program_id(0)
@@ -173,12 +154,26 @@
     lax.fori_loop(0, out_ref.shape[0], target, 0)
 
 
-def exchange_couple_kernel(axes, sizes, pair_leaf_ref, pair_mid_ref, leaf_pay_ref, mid_pay_ref,
+def fill_slots(send_ref, coef_ref, pay_ref):
+    held = coef_ref.shape[0]
+
+    def fill(i, carry):
+        a = send_ref[i]
+        pay_ref[i] = jnp.where(a < held, coef_ref[jnp.minimum(a, held - 1)], 0.0)
+        return carry
+
+    lax.fori_loop(0, pay_ref.shape[0], fill, 0)
+
+
+def exchange_couple_kernel(axes, sizes, pair_leaf_ref, pair_mid_ref, send_leaf_ref, send_mid_ref,
+                           coef_leaf_ref, coef_mid_ref,
                            leaf_coupling_ref, mid_coupling_ref, near_leaf_ref, near_mid_ref,
-                           leaf_land, mid_land, sems):
+                           leaf_pay_ref, mid_pay_ref, leaf_land, mid_land, sems):
     outer, inner = sizes
     count = outer * inner
     me = lax.axis_index(axes[0]) * inner + lax.axis_index(axes[1])
+    fill_slots(send_leaf_ref, coef_leaf_ref, leaf_pay_ref)
+    fill_slots(send_mid_ref, coef_mid_ref, mid_pay_ref)
     barrier = pltpu.get_barrier_semaphore()
 
     def greet(q, carry):
@@ -238,8 +233,10 @@
     mid_all.wait_send()
 
 
-def exchange_couple(pair_leaf, pair_mid, leaf_pay, mid_pay, leaf_coupling, mid_coupling, axes, sizes):
-    rank, ports = leaf_pay.shape[1:]
+def exchange_couple(pair_leaf, pair_mid, send_leaf, send_mid, coef_leaf, coef_mid, leaf_coupling,
+                    mid_coupling, axes, sizes):
+    rank, ports = coef_leaf.shape[1:]
+    pay_shape = (send_leaf.shape[0], rank, ports)
     n_leaf = leaf_coupling.shape[0]
     n_mid = mid_coupling.shape[0]
     vmem = pl.BlockSpec(memory_space=pltpu.VMEM)
@@ -249,17 +246,19 @@
         functools.partial(exchange_couple_kernel, axes, sizes),
         out_shape=[jax.ShapeDtypeStruct((n_leaf, rank, ports), jnp.float32),
                    jax.ShapeDtypeStruct((n_mid, rank, ports), jnp.float32)],
-        in_specs=[smem, smem, hbm, hbm, vmem, vmem],
+        in_specs=[smem, smem, smem, smem, vmem, vmem, vmem, vmem],
         out_specs=[vmem, vmem],
-        scratch_shapes=[pltpu.VMEM(leaf_pay.shape, jnp.float32), pltpu.VMEM(mid_pay.shape, jnp.float32),
+        scratch_shapes=[pltpu.VMEM(pay_shape, jnp.float32), pltpu.VMEM(pay_shape, jnp.float32),
+                        pltpu.VMEM(pay_shape, jnp.float32), pltpu.VMEM(pay_shape, jnp.float32),
                         pltpu.SemaphoreType.DMA((6,))],
         compiler_params=pltpu.CompilerParams(collective_id=0, has_side_effects=True,
                                              vmem_limit_bytes=62 * 1024 * 1024),
         cost_estimate=pl.CostEstimate(
             flops=2 * (leaf_coupling.size + mid_coupling.size) * ports,
-            bytes_accessed=4 * (leaf_pay.size + mid_pay.size + leaf_coupling.size + mid_coupling.size),
+            bytes_accessed=4 * (coef_leaf.size + coef_mid.size + leaf_coupling.size + mid_coupling.size),
             transcendentals=0),
-    )(pair_leaf.reshape(-1), pair_mid.reshape(-1), leaf_pay, mid_pay, leaf_coupling, mid_coupling)
+    )(pair_leaf.reshape(-1), pair_mid.reshape(-1), send_leaf, send_mid, coef_leaf, coef_mid,
+      leaf_coupling, mid_coupling)
 
 
 def body(
@@ -284,11 +283,12 @@
     mid_count = mid_transfer.shape[0]
     owners = send_leaf.shape[0] // 2
     slots = 2
-    leaf_pay, mid_pay, coef_top = build_payload(
-        charges, leaf_size, leaf_parent, send_leaf, send_mid, leaf_basis, leaf_transfer, mid_transfer
+    coef_leaf, coef_mid, coef_top = build_coefs(
+        charges, leaf_size, leaf_parent, leaf_basis, leaf_transfer, mid_transfer
     )
     near_leaf, near_mid = exchange_couple(
-        pair_leaf, pair_mid, leaf_pay, mid_pay, leaf_coupling, mid_coupling, ("group", "cluster"), sizes
+        pair_leaf, pair_mid, send_leaf, send_mid, coef_leaf, coef_mid, leaf_coupling, mid_coupling,
+        ("group", "cluster"), sizes,
     )
 
     listed = top_pairs.shape[1]

time: 285 us -> 281 us (0.986)
  waiting for transfers between devices: 3.55 us -> 0.04 us
    pallas_call x1, Pallas kernels: 228 us -> 237 us  [exchange_couple(): pl.pallas_call(functools.partial(exchange_couple_kernel, axes, sizes), ou...]
    pallas_call x1, Pallas kernels: 18.8 us -> 11.4 us  [build_coefs(): pl.pallas_call(coef_kernel, out_shape=[jax.ShapeDtypeStruct((leaves, rank...]
    all_gather x1, waiting for transfers between devices: 3.53 us -> 0.02 us  [body(): lax.all_gather(coef_top[None], ('group', 'cluster'), axis=0, tiled=True)]
  transfers between devices with their start and end apart: 1 -> 1, of which waited for: 1 -> 0; matrix products, arithmetic and copies ran while one was open for 1% -> 1% of each run, Pallas kernels for 81% -> 85%
where the time goes in v11:
time: 281 us; the launch traced here: 280 us
  Pallas kernels  258 us (92%)
  between operations  13.5 us (5%)
  local copies, waits for them, and re-layouts  4.33 us (2%)
    pallas_call x1, Pallas kernels, exchange_couple(): pl.pallas_call(functools.partial(exchange_couple_kernel, axes, sizes), ou...  237 us
    pallas_call x1, Pallas kernels, build_coefs(): pl.pallas_call(coef_kernel, out_shape=[jax.ShapeDtypeStruct((leaves, rank...  11.4 us
    pallas_call x1, Pallas kernels, far_field_pallas(): pl.pallas_call(functools.partial(far_kernel, nb), grid_spec=grid_spec, ou...  10.1 us
  transfers between devices with their start and end apart: 1, of which 0 were waited for; matrix products, arithmetic and copies ran while one was open for 1% of the time, Pallas kernels for 85%

profile of v11, /device:TPU:24, one launch (start us, length us, event | category | flops | bytes accessed | tf_op | source)
XLA Modules:
  0.0 279.9 jit_solution(11658172259348776165)
XLA Ops:
  6.5 0.0 copy-start
  6.5 0.0 copy-start.1
  6.5 0.0 copy-start.2
  6.5 0.0 all-gather.3.cloned.1.call-start
  6.6 11.4 %shard_map.136 = (f32[32,64,128]{2,1,0:T(8,128)}, f32[8,64,128]{2,1,0:T(8,128)}, f32[64,128]{1,0:T(8,128)}) custom-call(s32[32]{0:T(128)} %size_ref.3, s32[32]{0:T(128)} %parent_ref.3, f32[8192,128]{1,0:T(8,128)} %charges_ref.1, f32[32,64,256]{2,1,0:T(8,128)} %basis_ref.3, f32[32,64,64]{2,1,0:T(8,128)} %transfer_ref.3, f32[8,64,64]{2,1,0:T(8,128)} %mid_transfer_ref.1), custom_call_target="tpu_custom_call" | custom-call | flops 134217728 | bytes 6291456 | tf_op jit(solution)/shard_map/pallas_call | solution.py:90
  17.9 0.0 all-gather.3.cloned.1.call-update
  18.0 0.0 copy-done
  18.0 0.1 copy.17
  18.1 0.0 copy-done.1
  18.1 0.1 copy.16
  18.2 0.7 reshape.109.pair_leaf_ref
  18.9 0.0 copy-done.3
  18.9 0.7 reshape.110.pair_mid_ref
  19.6 0.0 copy-done.2
  19.6 0.2 clamp_reduce_fusion
  19.8 0.2 and_reduce_fusion
  20.0 236.9 %shard_map.137 = (f32[32,64,128]{2,1,0:T(8,128)}, f32[8,64,128]{2,1,0:T(8,128)}) custom-call(s32[384]{0:T(512)} %reshape.109.pair_leaf_ref, s32[256]{0:T(256)} %reshape.110.pair_mid_ref, s32[256]{0:T(256)} %send_leaf_ref.1, s32[256]{0:T(256)} %send_mid_ref.1, f32[32,64,128]{2,1,0:T(8,128)} %get-tuple-element.10.coef_leaf_ref, ...), custom_call_target="tpu_custom_call" | custom-call | flops 671088640 | bytes 11796480 | tf_op jit(solution)/shard_map/pallas_call | solution.py:245
  256.9 0.0 all-gather.3.cloned.1.call-done
  257.0 2.7 gather_fusion
  259.7 0.1 select_select_fusion
  259.8 1.1 fusion
  260.9 0.4 fusion.5
  261.2 1.7 add.25.down_mid_ref
  262.9 10.1 %shard_map.138 = f32[8192,128]{1,0:T(8,128)} custom-call(s32[32]{0:T(128)} %size_ref.3, s32[32]{0:T(128)} %parent_ref.3, f32[32,64,128]{2,1,0:T(8,128)} %get-tuple-element.12.near_ref, f32[32,64,64]{2,1,0:T(8,128)} %transfer_ref.3, f32[32,64,256]{2,1,0:T(8,128)} %basis_ref.3, f32[8,64,128]{2,1,0:T(8,128)} %add.25.down_mid_ref), custom_call_target="tpu_custom_call" | custom-call | flops 134217728 | bytes 10485760 | tf_op jit(solution)/shard_map/pallas_call | solution.py:130
  (4 shorter events, 0.0 us)
Async XLA Ops:
  6.5 11.4 %copy-start = (f32[8,64,64]{2,1,0:T(8,128)S(1)}, f32[8,64,64]{2,1,0:T(8,128)}, u32[]{:S(2)}) copy-start(f32[8,64,64]{2,1,0:T(8,128)} %mid_transfer_ref.1) | copy-start | bytes 393220
  6.5 11.6 %copy-start.1 = (s32[32,12]{0,1:T(8,128)S(1)}, s32[32,12]{0,1:T(8,128)}, u32[]{:S(2)}) copy-start(s32[32,12]{0,1:T(8,128)} %param.21) | copy-start | bytes 4612
  6.5 12.4 %copy-start.3 = (s32[8,32]{1,0:T(8,128)S(1)}, s32[8,32]{1,0:T(8,128)}, u32[]{:S(2)}) copy-start(s32[8,32]{1,0:T(8,128)} %param.24) | copy-start | bytes 3076
  6.5 13.0 %copy-start.2 = (s32[32,4]{0,1:T(4,128)S(1)}, s32[32,4]{0,1:T(4,128)}, u32[]{:S(2)}) copy-start(s32[32,4]{0,1:T(4,128)} %param.26) | copy-start | bytes 1540
  6.5 250.4 %all-gather.3.cloned.1.call-start = ((), (), s32[]{:S(2)}) async-start(), calls=%async_computation | async-start | bytes 4227072 | tf_op jit(solution)/shard_map/all_gather | solution.py:298
Sparse Core Ops, SparseCore 0:
  18.1 231.1 all-gather.2

commit v12 on v11

--- a/solution.py
+++ b/solution.py
@@ -111,8 +111,8 @@
         l = i * nb + t
         p = parent_ref[l]
         dm = down_mid_ref[p]
-        dl = near_ref[t] + lax.dot_general(transfer_ref[t], dm, tdims, precision=exact_mode, preferred_element_type=jnp.float32)
-        far = lax.dot_general(basis_ref[t], dl, tdims, precision=exact_mode, preferred_element_type=jnp.float32)
+        dl = near_ref[t] + lax.dot_general(transfer_ref[t], dm, tdims, precision=lax.Precision.HIGH, preferred_element_type=jnp.float32)
+        far = lax.dot_general(basis_ref[t], dl, tdims, precision=lax.Precision.HIGH, preferred_element_type=jnp.float32)
         out_ref[t * points:(t + 1) * points, :] = jnp.where(rows < size_ref[l], far, 0.0)
 
 def far_field_pallas(near_leaf, leaf_transfer, leaf_basis, down_mid, leaf_size, leaf_parent, nb=8):

time: 281 us -> 278 us (0.989)
  no operation moved by 1% of the time
where the time goes in v12:
time: 278 us; the launch traced here: 277 us
  Pallas kernels  256 us (92%)
  between operations  13.5 us (5%)
  local copies, waits for them, and re-layouts  4.33 us (2%)
    pallas_call x1, Pallas kernels, exchange_couple(): pl.pallas_call(functools.partial(exchange_couple_kernel, axes, sizes), ou...  236 us
    pallas_call x1, Pallas kernels, build_coefs(): pl.pallas_call(coef_kernel, out_shape=[jax.ShapeDtypeStruct((leaves, rank...  11.4 us
    pallas_call x1, Pallas kernels, far_field_pallas(): pl.pallas_call(functools.partial(far_kernel, nb), grid_spec=grid_spec, ou...  8.41 us
  transfers between devices with their start and end apart: 1, of which 0 were waited for; matrix products, arithmetic and copies ran while one was open for 1% of the time, Pallas kernels for 85%

profile of v12, /device:TPU:24, one launch (start us, length us, event | category | flops | bytes accessed | tf_op | source)
XLA Modules:
  0.0 277.5 jit_solution(4926174212179043025)
XLA Ops:
  6.5 0.0 copy-start
  6.5 0.0 copy-start.1
  6.5 0.0 copy-start.2
  6.5 0.0 all-gather.3.cloned.1.call-start
  6.6 11.4 %shard_map.136 = (f32[32,64,128]{2,1,0:T(8,128)}, f32[8,64,128]{2,1,0:T(8,128)}, f32[64,128]{1,0:T(8,128)}) custom-call(s32[32]{0:T(128)} %size_ref.3, s32[32]{0:T(128)} %parent_ref.3, f32[8192,128]{1,0:T(8,128)} %charges_ref.1, f32[32,64,256]{2,1,0:T(8,128)} %basis_ref.3, f32[32,64,64]{2,1,0:T(8,128)} %transfer_ref.3, f32[8,64,64]{2,1,0:T(8,128)} %mid_transfer_ref.1), custom_call_target="tpu_custom_call" | custom-call | flops 134217728 | bytes 6291456 | tf_op jit(solution)/shard_map/pallas_call | solution.py:90
  17.9 0.0 all-gather.3.cloned.1.call-update
  18.0 0.0 copy-done
  18.0 0.1 copy.17
  18.1 0.0 copy-done.1
  18.1 0.1 copy.16
  18.2 0.7 reshape.109.pair_leaf_ref
  18.9 0.0 copy-done.3
  18.9 0.7 reshape.110.pair_mid_ref
  19.6 0.0 copy-done.2
  19.6 0.2 clamp_reduce_fusion
  19.8 0.2 and_reduce_fusion
  20.0 236.2 %shard_map.137 = (f32[32,64,128]{2,1,0:T(8,128)}, f32[8,64,128]{2,1,0:T(8,128)}) custom-call(s32[384]{0:T(512)} %reshape.109.pair_leaf_ref, s32[256]{0:T(256)} %reshape.110.pair_mid_ref, s32[256]{0:T(256)} %send_leaf_ref.1, s32[256]{0:T(256)} %send_mid_ref.1, f32[32,64,128]{2,1,0:T(8,128)} %get-tuple-element.10.coef_leaf_ref, ...), custom_call_target="tpu_custom_call" | custom-call | flops 671088640 | bytes 11796480 | tf_op jit(solution)/shard_map/pallas_call | solution.py:245
  256.2 0.0 all-gather.3.cloned.1.call-done
  256.3 2.7 gather_fusion
  259.0 0.1 select_select_fusion
  259.1 1.1 fusion
  260.2 0.4 fusion.5
  260.5 1.7 add.25.down_mid_ref
  262.2 8.4 %shard_map.138 = f32[8192,128]{1,0:T(8,128)} custom-call(s32[32]{0:T(128)} %size_ref.3, s32[32]{0:T(128)} %parent_ref.3, f32[32,64,128]{2,1,0:T(8,128)} %get-tuple-element.12.near_ref, f32[32,64,64]{2,1,0:T(8,128)} %transfer_ref.3, f32[32,64,256]{2,1,0:T(8,128)} %basis_ref.3, f32[8,64,128]{2,1,0:T(8,128)} %add.25.down_mid_ref), custom_call_target="tpu_custom_call" | custom-call | flops 134217728 | bytes 10485760 | tf_op jit(solution)/shard_map/pallas_call | solution.py:130
  (4 shorter events, 0.0 us)
Async XLA Ops:
  6.5 11.4 %copy-start = (f32[8,64,64]{2,1,0:T(8,128)S(1)}, f32[8,64,64]{2,1,0:T(8,128)}, u32[]{:S(2)}) copy-start(f32[8,64,64]{2,1,0:T(8,128)} %mid_transfer_ref.1) | copy-start | bytes 393220
  6.5 11.6 %copy-start.1 = (s32[32,12]{0,1:T(8,128)S(1)}, s32[32,12]{0,1:T(8,128)}, u32[]{:S(2)}) copy-start(s32[32,12]{0,1:T(8,128)} %param.21) | copy-start | bytes 4612
  6.5 12.4 %copy-start.3 = (s32[8,32]{1,0:T(8,128)S(1)}, s32[8,32]{1,0:T(8,128)}, u32[]{:S(2)}) copy-start(s32[8,32]{1,0:T(8,128)} %param.24) | copy-start | bytes 3076
  6.5 13.0 %copy-start.2 = (s32[32,4]{0,1:T(4,128)S(1)}, s32[32,4]{0,1:T(4,128)}, u32[]{:S(2)}) copy-start(s32[32,4]{0,1:T(4,128)} %param.26) | copy-start | bytes 1540
  6.5 249.7 %all-gather.3.cloned.1.call-start = ((), (), s32[]{:S(2)}) async-start(), calls=%async_computation | async-start | bytes 4227072 | tf_op jit(solution)/shard_map/all_gather | solution.py:298
Sparse Core Ops, SparseCore 0:
  18.1 225.4 all-gather.2

commit v13 on v12

--- a/solution.py
+++ b/solution.py
@@ -101,39 +101,72 @@
     )(leaf_size, leaf_parent, charges, leaf_basis, leaf_transfer, mid_transfer)
 
 
-def far_kernel(nb, size_ref, parent_ref, near_ref, transfer_ref, basis_ref, down_mid_ref, out_ref):
+def far_kernel(nb, listed, coarse, size_ref, parent_ref, wanted_ref, pos_ref, near_ref, transfer_ref,
+               basis_ref, near_mid_ref, mid_transfer_ref, top_coupling_ref, *rest):
+    row_refs = rest[:listed]
+    out_ref = rest[listed]
+    down_mid = rest[listed + 1]
     i = pl.program_id(0)
     rank = near_ref.shape[1]
     points = basis_ref.shape[2]
+    tdims = (((0,), (0,)), ((), ()))
+
+    @pl.when(i == 0)
+    def _():
+        near_top = jnp.zeros(near_mid_ref.shape[1:], jnp.float32)
+        for k in range(listed):
+            c = top_coupling_ref[0, :, k * rank : (k + 1) * rank]
+            prod = jnp.dot(c, row_refs[k][0], precision=exact_mode, preferred_element_type=jnp.float32)
+            near_top = near_top + jnp.where(wanted_ref[k] < coarse, prod, 0.0)
+        for c in range(near_mid_ref.shape[0]):
+            down_mid[c] = near_mid_ref[c] + lax.dot_general(
+                mid_transfer_ref[c], near_top, tdims, precision=exact_mode,
+                preferred_element_type=jnp.float32)
+
     rows = lax.broadcasted_iota(jnp.int32, (points, 1), 0)
-    tdims = (((0,), (0,)), ((), ()))
     for t in range(nb):
         l = i * nb + t
         p = parent_ref[l]
-        dm = down_mid_ref[p]
+        dm = down_mid[p]
         dl = near_ref[t] + lax.dot_general(transfer_ref[t], dm, tdims, precision=lax.Precision.HIGH, preferred_element_type=jnp.float32)
         far = lax.dot_general(basis_ref[t], dl, tdims, precision=lax.Precision.HIGH, preferred_element_type=jnp.float32)
         out_ref[t * points:(t + 1) * points, :] = jnp.where(rows < size_ref[l], far, 0.0)
 
-def far_field_pallas(near_leaf, leaf_transfer, leaf_basis, down_mid, leaf_size, leaf_parent, nb=8):
+
+def far_field_pallas(near_leaf, leaf_transfer, leaf_basis, near_mid, mid_transfer, top_coupling,
+                     shard_rows, wanted, position, leaf_size, leaf_parent, nb=8):
     leaves, rank, points = leaf_basis.shape
     ports = near_leaf.shape[2]
+    listed = wanted.shape[0]
+    coarse = shard_rows.shape[0]
+
+    def row_spec(k):
+        return pl.BlockSpec(
+            (1, rank, ports), lambda i, s, p, w, q: (jnp.minimum(w[k], coarse - 1), 0, 0)
+        )
+
     grid_spec = pltpu.PrefetchScalarGridSpec(
-        num_scalar_prefetch=2,
+        num_scalar_prefetch=4,
         grid=(leaves // nb,),
         in_specs=[pl.BlockSpec((nb, rank, ports), lambda i, *_: (i, 0, 0)),
                   pl.BlockSpec((nb, rank, rank), lambda i, *_: (i, 0, 0)),
                   pl.BlockSpec((nb, rank, points), lambda i, *_: (i, 0, 0)),
-                  pl.BlockSpec(down_mid.shape, lambda i, *_: (0, 0, 0))],
+                  pl.BlockSpec(near_mid.shape, lambda i, *_: (0, 0, 0)),
+                  pl.BlockSpec(mid_transfer.shape, lambda i, *_: (0, 0, 0)),
+                  pl.BlockSpec((1,) + top_coupling.shape[1:], lambda i, s, p, w, q: (q[0], 0, 0))]
+                 + [row_spec(k) for k in range(listed)],
         out_specs=pl.BlockSpec((nb * points, ports), lambda i, *_: (i, 0)),
+        scratch_shapes=[pltpu.VMEM(near_mid.shape, jnp.float32)],
     )
     return pl.pallas_call(
-        functools.partial(far_kernel, nb),
+        functools.partial(far_kernel, nb, listed, coarse),
         grid_spec=grid_spec,
         out_shape=jax.ShapeDtypeStruct((leaves * points, ports), jnp.float32),
-        compiler_params=pltpu.CompilerParams(vmem_limit_bytes=60 * 1024 * 1024),
+        compiler_params=pltpu.CompilerParams(vmem_limit_bytes=60 * 1024 * 1024,
+                                             dimension_semantics=("arbitrary",)),
         cost_estimate=pl.CostEstimate(flops=2 * leaves * rank * points * ports, bytes_accessed=4 * (leaf_basis.size + 2 * leaves * points * ports), transcendentals=0),
-    )(leaf_size, leaf_parent, near_leaf, leaf_transfer, leaf_basis, down_mid)
+    )(leaf_size, leaf_parent, wanted, position, near_leaf, leaf_transfer, leaf_basis, near_mid,
+      mid_transfer, top_coupling, *([shard_rows] * listed))
 
 
 def couple_rows(pairs_ref, land_ref, coupling_ref, out_ref, listed):
@@ -291,25 +324,11 @@
         ("group", "cluster"), sizes,
     )
 
-    listed = top_pairs.shape[1]
-    position = lax.axis_index("cluster")
-    wanted = lax.dynamic_slice_in_dim(top_pairs, position, 1, 0)[0]
-    own_coupling = lax.dynamic_slice_in_dim(top_coupling, position, 1, 0)[0]
+    position = lax.axis_index("cluster").astype(jnp.int32).reshape(1)
+    wanted = lax.dynamic_slice_in_dim(top_pairs, position[0], 1, 0)[0]
     shard_rows = lax.all_gather(coef_top[None], ("group", "cluster"), axis=0, tiled=True)
-    inside = (wanted >= 0) & (wanted < shard_rows.shape[0])
-    taken_rows = jnp.take(shard_rows, jnp.clip(wanted, 0, shard_rows.shape[0] - 1), axis=0)
-    picked = jnp.where(
-        inside[:, None, None], taken_rows, jnp.zeros((listed, coef_rank, port_count), jnp.float32)
-    )
-    near_top = jnp.einsum(
-        "kq,qp->kp",
-        own_coupling,
-        picked.reshape(listed * coef_rank, port_count),
-        precision=exact_mode,
-    )
-
-    down_mid = near_mid + jnp.einsum("mjk,jp->mkp", mid_transfer, near_top, precision=exact_mode)
-    return far_field_pallas(near_leaf, leaf_transfer, leaf_basis, down_mid, leaf_size, leaf_parent)
+    return far_field_pallas(near_leaf, leaf_transfer, leaf_basis, near_mid, mid_transfer, top_coupling,
+                            shard_rows, wanted, position, leaf_size, leaf_parent)
 
 
 def solution(mesh):

time: 278 us -> 273 us (0.982); the launches traced: 277 us -> 270 us
  transfers between devices with their start and end apart: 1 -> 1, of which waited for: 0 -> 0; matrix products, arithmetic and copies ran while one was open for 1% -> 1% of each run, Pallas kernels for 85% -> 87%
where the time goes in v13:
time: 273 us; the launch traced here: 270 us
  Pallas kernels  254 us (93%)
  between operations  13.4 us (5%)
    pallas_call x1, Pallas kernels, exchange_couple(): pl.pallas_call(functools.partial(exchange_couple_kernel, axes, sizes), ou...  234 us
    pallas_call x1, Pallas kernels, build_coefs(): pl.pallas_call(coef_kernel, out_shape=[jax.ShapeDtypeStruct((leaves, rank...  11.3 us
    pallas_call x1, Pallas kernels, far_field_pallas(): pl.pallas_call(functools.partial(far_kernel, nb, listed, coarse), grid_sp...  9.2 us
  transfers between devices with their start and end apart: 1, of which 0 were waited for; matrix products, arithmetic and copies ran while one was open for 1% of the time, Pallas kernels for 87%

profile of v13, /device:TPU:24, one launch (start us, length us, event | category | flops | bytes accessed | tf_op | source)
XLA Modules:
  0.0 269.6 jit_solution(1562161072942902641)
XLA Ops:
  6.5 0.0 copy-start
  6.5 0.0 copy-start.2
  6.5 0.0 copy-start.1
  6.5 0.0 all-gather.3.cloned.1.call-start
  6.5 11.3 %shard_map.136 = (f32[32,64,128]{2,1,0:T(8,128)}, f32[8,64,128]{2,1,0:T(8,128)}, f32[64,128]{1,0:T(8,128)}) custom-call(s32[32]{0:T(128)} %size_ref.3, s32[32]{0:T(128)} %parent_ref.3, f32[8192,128]{1,0:T(8,128)} %charges_ref.1, f32[32,64,256]{2,1,0:T(8,128)} %basis_ref.3, f32[32,64,64]{2,1,0:T(8,128)} %transfer_ref.3, f32[8,64,64]{2,1,0:T(8,128)} %mid_transfer_ref.3), custom_call_target="tpu_custom_call" | custom-call | flops 134217728 | bytes 6291456 | tf_op jit(solution)/shard_map/pallas_call | solution.py:90
  17.9 0.0 all-gather.3.cloned.1.call-update
  17.9 0.0 copy-done.2
  17.9 0.6 reshape.11.pair_mid_ref
  18.5 0.0 copy-done.1
  18.5 0.1 copy.15
  18.6 0.7 reshape.10.pair_leaf_ref
  19.3 0.0 copy-done
  19.3 0.7 dynamic-slice_reduce_fusion.wanted_ref
  20.0 233.5 %shard_map.137 = (f32[32,64,128]{2,1,0:T(8,128)}, f32[8,64,128]{2,1,0:T(8,128)}) custom-call(s32[384]{0:T(512)} %reshape.10.pair_leaf_ref, s32[256]{0:T(256)} %reshape.11.pair_mid_ref, s32[256]{0:T(256)} %send_leaf_ref.1, s32[256]{0:T(256)} %send_mid_ref.1, f32[32,64,128]{2,1,0:T(8,128)} %get-tuple-element.10.coef_leaf_ref, ...), custom_call_target="tpu_custom_call" | custom-call | flops 671088640 | bytes 11796480 | tf_op jit(solution)/shard_map/pallas_call | solution.py:278
  253.5 0.0 all-gather.3.cloned.1.call-done
  253.6 9.2 %shard_map.138 = f32[8192,128]{1,0:T(8,128)} custom-call(s32[32]{0:T(128)} %size_ref.3, s32[32]{0:T(128)} %parent_ref.3, s32[4]{0:T(128)} %dynamic-slice_reduce_fusion.wanted_ref, s32[1]{0:T(128)} %bitcast.pos_ref, f32[32,64,128]{2,1,0:T(8,128)} %get-tuple-element.12.near_ref, f32[32,64,64]{2,1,0:T(8,128)} %transfer_ref.3, f32[32,64,256]{2,1,0:T(8,128)} %basis_ref.3, ...), custom_call_target="tpu_custom_call" | custom-call | flops 134217728 | bytes 10485760 | tf_op jit(solution)/shard_map/pallas_call | solution.py:161
Async XLA Ops:
  6.5 12.8 %copy-start = (s32[32,4]{0,1:T(4,128)S(1)}, s32[32,4]{0,1:T(4,128)}, u32[]{:S(2)}) copy-start(s32[32,4]{0,1:T(4,128)} %param.26) | copy-start | bytes 1540
  6.5 11.4 %copy-start.2 = (s32[8,32]{1,0:T(8,128)S(1)}, s32[8,32]{1,0:T(8,128)}, u32[]{:S(2)}) copy-start(s32[8,32]{1,0:T(8,128)} %param.24) | copy-start | bytes 3076
  6.5 12.0 %copy-start.1 = (s32[32,12]{0,1:T(8,128)S(1)}, s32[32,12]{0,1:T(8,128)}, u32[]{:S(2)}) copy-start(s32[32,12]{0,1:T(8,128)} %param.21) | copy-start | bytes 4612
  6.5 247.0 %all-gather.3.cloned.1.call-start = ((), (), s32[]{:S(2)}) async-start(), calls=%async_computation | async-start | bytes 4227072 | tf_op jit(solution)/shard_map/all_gather | solution.py:329
Sparse Core Ops, SparseCore 0:
  18.0 232.1 all-gather.2

commit v14 on v13

--- a/solution.py
+++ b/solution.py
@@ -9,55 +9,6 @@
 from jax.sharding import PartitionSpec as P
 
 exact_mode = lax.Precision.HIGHEST
-
-
-def couple(coupling, coef, index):
-    stacked = jnp.take(coef, index, axis=0, mode="fill", fill_value=0.0)
-    stacked = stacked.reshape(index.shape[0], index.shape[1] * coef.shape[1], coef.shape[2])
-    return jnp.einsum("nkq,nqp->nkp", coupling, stacked, precision=exact_mode)
-
-
-def couple_kernel(nb, listed, total, idx_ref, arrived_ref, coupling_ref, out_ref):
-    i = pl.program_id(0)
-    rank = arrived_ref.shape[1]
-    for t in range(nb):
-        acc = jnp.zeros(out_ref.shape[1:], jnp.float32)
-        for k in range(listed):
-            r = idx_ref[(i * nb + t) * listed + k]
-            valid = r < total
-            blk = arrived_ref[jnp.minimum(r, total - 1)]
-            c = coupling_ref[t, :, k * rank : (k + 1) * rank]
-            prod = jnp.dot(c, blk, precision=lax.Precision.HIGH, preferred_element_type=jnp.float32)
-            acc = acc + jnp.where(valid, prod, 0.0)
-        out_ref[t] = acc
-
-
-def couple_pallas(coupling, arrived, rows, nb):
-    n, rank, width = coupling.shape
-    listed = rows.shape[1]
-    total, _, ports = arrived.shape
-    grid_spec = pltpu.PrefetchScalarGridSpec(
-        num_scalar_prefetch=1,
-        grid=(n // nb,),
-        in_specs=[
-            pl.BlockSpec(
-                (total, rank, ports), lambda i, idx: (0, 0, 0), pipeline_mode=pl.Buffered(1)
-            ),
-            pl.BlockSpec((nb, rank, width), lambda i, idx: (i, 0, 0)),
-        ],
-        out_specs=pl.BlockSpec((nb, rank, ports), lambda i, idx: (i, 0, 0)),
-    )
-    return pl.pallas_call(
-        functools.partial(couple_kernel, nb, listed, total),
-        grid_spec=grid_spec,
-        out_shape=jax.ShapeDtypeStruct((n, rank, ports), jnp.float32),
-        compiler_params=pltpu.CompilerParams(vmem_limit_bytes=60 * 1024 * 1024),
-        cost_estimate=pl.CostEstimate(
-            flops=2 * n * rank * width * ports,
-            bytes_accessed=4 * (n * rank * width + total * rank * ports + n * rank * ports),
-            transcendentals=0,
-        ),
-    )(rows.reshape(-1), arrived, coupling)
 
 
 def coef_kernel(size_ref, parent_ref, charges_ref, basis_ref, transfer_ref, mid_transfer_ref,
@@ -176,7 +127,7 @@
     def target(t, carry):
         acc = jnp.zeros(out_ref.shape[1:], jnp.float32)
         for k in range(listed):
-            r = pairs_ref[t * listed + k]
+            r = pairs_ref[t, k]
             blk = land_ref[jnp.minimum(r, total - 1)]
             c = coupling_ref[t, :, k * rank : (k + 1) * rank]
             prod = jnp.dot(c, blk, precision=lax.Precision.HIGH, preferred_element_type=jnp.float32)
@@ -258,10 +209,10 @@
     mid_all = everything(mid_pay_ref, mid_land, sems.at[2], sems.at[3])
     own_leaf.wait()
     leaf_all.wait_recv()
-    couple_rows(pair_leaf_ref, leaf_land, leaf_coupling_ref, near_leaf_ref, pair_leaf_ref.shape[0] // near_leaf_ref.shape[0])
+    couple_rows(pair_leaf_ref, leaf_land, leaf_coupling_ref, near_leaf_ref, pair_leaf_ref.shape[1])
     own_mid.wait()
     mid_all.wait_recv()
-    couple_rows(pair_mid_ref, mid_land, mid_coupling_ref, near_mid_ref, pair_mid_ref.shape[0] // near_mid_ref.shape[0])
+    couple_rows(pair_mid_ref, mid_land, mid_coupling_ref, near_mid_ref, pair_mid_ref.shape[1])
     leaf_all.wait_send()
     mid_all.wait_send()
 
@@ -290,7 +241,7 @@
             flops=2 * (leaf_coupling.size + mid_coupling.size) * ports,
             bytes_accessed=4 * (coef_leaf.size + coef_mid.size + leaf_coupling.size + mid_coupling.size),
             transcendentals=0),
-    )(pair_leaf.reshape(-1), pair_mid.reshape(-1), send_leaf, send_mid, coef_leaf, coef_mid,
+    )(pair_leaf, pair_mid, send_leaf, send_mid, coef_leaf, coef_mid,
       leaf_coupling, mid_coupling)
 
 

time: 273 us -> 274 us (level)
  Pallas kernels: 254 us -> 258 us
    pallas_call x1, Pallas kernels: 234 us -> 238 us  [exchange_couple(): pl.pallas_call(functools.partial(exchange_couple_kernel, axes, sizes), ou...]
where the time goes in v14:
time: 274 us; the launch traced here: 273 us
  Pallas kernels  258 us (94%)
  between operations  13.4 us (5%)
    pallas_call x1, Pallas kernels, exchange_couple(): pl.pallas_call(functools.partial(exchange_couple_kernel, axes, sizes), ou...  238 us
    pallas_call x1, Pallas kernels, build_coefs(): pl.pallas_call(coef_kernel, out_shape=[jax.ShapeDtypeStruct((leaves, rank...  11.3 us
    pallas_call x1, Pallas kernels, far_field_pallas(): pl.pallas_call(functools.partial(far_kernel, nb, listed, coarse), grid_sp...  9.2 us
  transfers between devices with their start and end apart: 1, of which 0 were waited for; matrix products, arithmetic and copies ran while one was open for 1% of the time, Pallas kernels for 87%

profile of v14, /device:TPU:24, one launch (start us, length us, event | category | flops | bytes accessed | tf_op | source)
XLA Modules:
  0.0 273.0 jit_solution(9958395748319329940)
XLA Ops:
  6.5 0.0 copy-start
  6.5 0.0 copy-start.1
  6.5 0.0 all-gather.3.cloned.1.call-start
  6.5 11.3 %shard_map.136 = (f32[32,64,128]{2,1,0:T(8,128)}, f32[8,64,128]{2,1,0:T(8,128)}, f32[64,128]{1,0:T(8,128)}) custom-call(s32[32]{0:T(128)} %size_ref.3, s32[32]{0:T(128)} %parent_ref.3, f32[8192,128]{1,0:T(8,128)} %charges_ref.1, f32[32,64,256]{2,1,0:T(8,128)} %basis_ref.3, f32[32,64,64]{2,1,0:T(8,128)} %transfer_ref.3, f32[8,64,64]{2,1,0:T(8,128)} %mid_transfer_ref.3), custom_call_target="tpu_custom_call" | custom-call | flops 134217728 | bytes 6291456 | tf_op jit(solution)/shard_map/pallas_call | solution.py:41
  17.9 0.0 all-gather.3.cloned.1.call-update
  17.9 0.0 copy-done.1
  17.9 0.7 copy.15.pair_leaf_ref
  18.6 0.0 copy-done
  18.6 0.7 dynamic-slice_reduce_fusion.wanted_ref
  19.3 237.6 %shard_map.137 = (f32[32,64,128]{2,1,0:T(8,128)}, f32[8,64,128]{2,1,0:T(8,128)}) custom-call(s32[32,12]{1,0:T(8,128)} %copy.15.pair_leaf_ref, s32[8,32]{1,0:T(8,128)} %pair_mid_ref.1, s32[256]{0:T(256)} %send_leaf_ref.1, s32[256]{0:T(256)} %send_mid_ref.1, f32[32,64,128]{2,1,0:T(8,128)} %get-tuple-element.10.coef_leaf_ref, ...), custom_call_target="tpu_custom_call" | custom-call | flops 671088640 | bytes 11796480 | tf_op jit(solution)/shard_map/pallas_call | solution.py:229
  256.9 0.0 all-gather.3.cloned.1.call-done
  256.9 9.2 %shard_map.138 = f32[8192,128]{1,0:T(8,128)} custom-call(s32[32]{0:T(128)} %size_ref.3, s32[32]{0:T(128)} %parent_ref.3, s32[4]{0:T(128)} %dynamic-slice_reduce_fusion.wanted_ref, s32[1]{0:T(128)} %bitcast.pos_ref, f32[32,64,128]{2,1,0:T(8,128)} %get-tuple-element.12.near_ref, f32[32,64,64]{2,1,0:T(8,128)} %transfer_ref.3, f32[32,64,256]{2,1,0:T(8,128)} %basis_ref.3, ...), custom_call_target="tpu_custom_call" | custom-call | flops 134217728 | bytes 10485760 | tf_op jit(solution)/shard_map/pallas_call | solution.py:112
Async XLA Ops:
  6.5 12.1 %copy-start = (s32[32,4]{0,1:T(4,128)S(1)}, s32[32,4]{0,1:T(4,128)}, u32[]{:S(2)}) copy-start(s32[32,4]{0,1:T(4,128)} %param.26) | copy-start | bytes 1540
  6.5 11.4 %copy-start.1 = (s32[32,12]{0,1:T(8,128)S(1)}, s32[32,12]{0,1:T(8,128)}, u32[]{:S(2)}) copy-start(s32[32,12]{0,1:T(8,128)} %param.21) | copy-start | bytes 4612
  6.5 250.4 %all-gather.3.cloned.1.call-start = ((), (), s32[]{:S(2)}) async-start(), calls=%async_computation | async-start | bytes 4227072 | tf_op jit(solution)/shard_map/all_gather | solution.py:280
Sparse Core Ops, SparseCore 0:
  18.0 230.5 all-gather.2

commit v15 on v14

--- a/solution.py
+++ b/solution.py
@@ -120,18 +120,21 @@
       mid_transfer, top_coupling, *([shard_rows] * listed))
 
 
-def couple_rows(pairs_ref, land_ref, coupling_ref, out_ref, listed):
+def couple_rows(pairs_ref, land_ref, coupling_ref, out_ref, listed, keep=None, add=False):
     total = land_ref.shape[0]
     rank = land_ref.shape[1]
 
     def target(t, carry):
-        acc = jnp.zeros(out_ref.shape[1:], jnp.float32)
+        acc = out_ref[t] if add else jnp.zeros(out_ref.shape[1:], jnp.float32)
         for k in range(listed):
             r = pairs_ref[t, k]
             blk = land_ref[jnp.minimum(r, total - 1)]
             c = coupling_ref[t, :, k * rank : (k + 1) * rank]
             prod = jnp.dot(c, blk, precision=lax.Precision.HIGH, preferred_element_type=jnp.float32)
-            acc = acc + jnp.where(r < total, prod, 0.0)
+            live = r < total
+            if keep is not None:
+                live = live & keep(r)
+            acc = acc + jnp.where(live, prod, 0.0)
         out_ref[t] = acc
         return carry
 
@@ -152,7 +155,7 @@
 def exchange_couple_kernel(axes, sizes, pair_leaf_ref, pair_mid_ref, send_leaf_ref, send_mid_ref,
                            coef_leaf_ref, coef_mid_ref,
                            leaf_coupling_ref, mid_coupling_ref, near_leaf_ref, near_mid_ref,
-                           leaf_pay_ref, mid_pay_ref, leaf_land, mid_land, sems):
+                           leaf_pay_ref, mid_pay_ref, leaf_land, mid_land, mid_late, sems):
     outer, inner = sizes
     count = outer * inner
     me = lax.axis_index(axes[0]) * inner + lax.axis_index(axes[1])
@@ -171,7 +174,7 @@
     stride = 37 if math.gcd(37, count) == 1 else 1
     slots = leaf_pay_ref.shape[0] // count
 
-    def sender(pay_ref, land_ref, send_sem, recv_sem):
+    def sender(pay_ref, land_ref, send_sem, recv_sem, first=1, last=count):
         def send(k, carry):
             peer = lax.rem(me + lax.rem(k * stride, count), count)
             pltpu.make_async_remote_copy(
@@ -184,12 +187,12 @@
             ).start()
             return carry
 
-        lax.fori_loop(1, count, send, 0)
-
-    def everything(pay_ref, land_ref, send_sem, recv_sem):
+        lax.fori_loop(first, last, send, 0)
+
+    def everything(pay_ref, land_ref, send_sem, recv_sem, copies=count - 1):
         return pltpu.make_async_remote_copy(
-            src_ref=pay_ref.at[pl.ds(0, (count - 1) * slots)],
-            dst_ref=land_ref.at[pl.ds(0, (count - 1) * slots)],
+            src_ref=pay_ref.at[pl.ds(0, copies * slots)],
+            dst_ref=land_ref.at[pl.ds(0, copies * slots)],
             send_sem=send_sem,
             recv_sem=recv_sem,
             device_id=(0, 0),
@@ -200,21 +203,33 @@
     own_leaf = pltpu.make_async_copy(leaf_pay_ref.at[pl.ds(me * slots, slots)],
                                      leaf_land.at[pl.ds(me * slots, slots)], sems.at[4])
     own_leaf.start()
-    sender(mid_pay_ref, mid_land, sems.at[2], sems.at[3])
+    half = count // 2
+    sender(mid_pay_ref, mid_land, sems.at[2], sems.at[3], 1, half)
+    sender(mid_pay_ref, mid_late, sems.at[6], sems.at[7], half, count)
     own_mid = pltpu.make_async_copy(mid_pay_ref.at[pl.ds(me * slots, slots)],
                                     mid_land.at[pl.ds(me * slots, slots)], sems.at[5])
     own_mid.start()
 
     leaf_all = everything(leaf_pay_ref, leaf_land, sems.at[0], sems.at[1])
-    mid_all = everything(mid_pay_ref, mid_land, sems.at[2], sems.at[3])
+    early_all = everything(mid_pay_ref, mid_land, sems.at[2], sems.at[3], half - 1)
+    late_all = everything(mid_pay_ref, mid_late, sems.at[6], sems.at[7], count - half)
     own_leaf.wait()
     leaf_all.wait_recv()
     couple_rows(pair_leaf_ref, leaf_land, leaf_coupling_ref, near_leaf_ref, pair_leaf_ref.shape[1])
+    inverse = pow(stride, -1, count)
+
+    def early(r):
+        return lax.rem((me - r // slots + count) * inverse, count) < half
+
     own_mid.wait()
-    mid_all.wait_recv()
-    couple_rows(pair_mid_ref, mid_land, mid_coupling_ref, near_mid_ref, pair_mid_ref.shape[1])
+    early_all.wait_recv()
+    couple_rows(pair_mid_ref, mid_land, mid_coupling_ref, near_mid_ref, pair_mid_ref.shape[1], early)
+    late_all.wait_recv()
+    couple_rows(pair_mid_ref, mid_late, mid_coupling_ref, near_mid_ref, pair_mid_ref.shape[1],
+                lambda r: jnp.logical_not(early(r)), True)
     leaf_all.wait_send()
-    mid_all.wait_send()
+    early_all.wait_send()
+    late_all.wait_send()
 
 
 def exchange_couple(pair_leaf, pair_mid, send_leaf, send_mid, coef_leaf, coef_mid, leaf_coupling,
@@ -234,7 +249,7 @@
         out_specs=[vmem, vmem],
         scratch_shapes=[pltpu.VMEM(pay_shape, jnp.float32), pltpu.VMEM(pay_shape, jnp.float32),
                         pltpu.VMEM(pay_shape, jnp.float32), pltpu.VMEM(pay_shape, jnp.float32),
-                        pltpu.SemaphoreType.DMA((6,))],
+                        pltpu.VMEM(pay_shape, jnp.float32), pltpu.SemaphoreType.DMA((8,))],
         compiler_params=pltpu.CompilerParams(collective_id=0, has_side_effects=True,
                                              vmem_limit_bytes=62 * 1024 * 1024),
         cost_estimate=pl.CostEstimate(

time: 274 us -> 275 us (level)
  no operation moved by 1% of the time
where the time goes in v15:
time: 275 us; the launch traced here: 272 us
  Pallas kernels  258 us (94%)
  between operations  13.4 us (5%)
    pallas_call x1, Pallas kernels, exchange_couple(): pl.pallas_call(functools.partial(exchange_couple_kernel, axes, sizes), ou...  237 us
    pallas_call x1, Pallas kernels, build_coefs(): pl.pallas_call(coef_kernel, out_shape=[jax.ShapeDtypeStruct((leaves, rank...  11.3 us
    pallas_call x1, Pallas kernels, far_field_pallas(): pl.pallas_call(functools.partial(far_kernel, nb, listed, coarse), grid_sp...  9.2 us
  transfers between devices with their start and end apart: 1, of which 0 were waited for; matrix products, arithmetic and copies ran while one was open for 1% of the time, Pallas kernels for 87%

profile of v15, /device:TPU:24, one launch (start us, length us, event | category | flops | bytes accessed | tf_op | source)
XLA Modules:
  0.0 272.5 jit_solution(16886256424434676030)
XLA Ops:
  6.5 0.0 copy-start
  6.5 0.0 copy-start.1
  6.5 0.0 all-gather.3.cloned.1.call-start
  6.5 11.3 %shard_map.136 = (f32[32,64,128]{2,1,0:T(8,128)}, f32[8,64,128]{2,1,0:T(8,128)}, f32[64,128]{1,0:T(8,128)}) custom-call(s32[32]{0:T(128)} %size_ref.3, s32[32]{0:T(128)} %parent_ref.3, f32[8192,128]{1,0:T(8,128)} %charges_ref.1, f32[32,64,256]{2,1,0:T(8,128)} %basis_ref.3, f32[32,64,64]{2,1,0:T(8,128)} %transfer_ref.3, f32[8,64,64]{2,1,0:T(8,128)} %mid_transfer_ref.3), custom_call_target="tpu_custom_call" | custom-call | flops 134217728 | bytes 6291456 | tf_op jit(solution)/shard_map/pallas_call | solution.py:41
  17.9 0.0 all-gather.3.cloned.1.call-update
  17.9 0.0 copy-done.1
  17.9 0.7 copy.15.pair_leaf_ref
  18.6 0.0 copy-done
  18.6 0.7 dynamic-slice_reduce_fusion.wanted_ref
  19.3 237.1 %shard_map.137 = (f32[32,64,128]{2,1,0:T(8,128)}, f32[8,64,128]{2,1,0:T(8,128)}) custom-call(s32[32,12]{1,0:T(8,128)} %copy.15.pair_leaf_ref, s32[8,32]{1,0:T(8,128)} %pair_mid_ref.1, s32[256]{0:T(256)} %send_leaf_ref.1, s32[256]{0:T(256)} %send_mid_ref.1, f32[32,64,128]{2,1,0:T(8,128)} %get-tuple-element.10.coef_leaf_ref, ...), custom_call_target="tpu_custom_call" | custom-call | flops 671088640 | bytes 11796480 | tf_op jit(solution)/shard_map/pallas_call | solution.py:244
  256.4 0.0 all-gather.3.cloned.1.call-done
  256.4 9.2 %shard_map.138 = f32[8192,128]{1,0:T(8,128)} custom-call(s32[32]{0:T(128)} %size_ref.3, s32[32]{0:T(128)} %parent_ref.3, s32[4]{0:T(128)} %dynamic-slice_reduce_fusion.wanted_ref, s32[1]{0:T(128)} %bitcast.pos_ref, f32[32,64,128]{2,1,0:T(8,128)} %get-tuple-element.12.near_ref, f32[32,64,64]{2,1,0:T(8,128)} %transfer_ref.3, f32[32,64,256]{2,1,0:T(8,128)} %basis_ref.3, ...), custom_call_target="tpu_custom_call" | custom-call | flops 134217728 | bytes 10485760 | tf_op jit(solution)/shard_map/pallas_call | solution.py:112
Async XLA Ops:
  6.5 12.1 %copy-start = (s32[32,4]{0,1:T(4,128)S(1)}, s32[32,4]{0,1:T(4,128)}, u32[]{:S(2)}) copy-start(s32[32,4]{0,1:T(4,128)} %param.26) | copy-start | bytes 1540
  6.5 11.4 %copy-start.1 = (s32[32,12]{0,1:T(8,128)S(1)}, s32[32,12]{0,1:T(8,128)}, u32[]{:S(2)}) copy-start(s32[32,12]{0,1:T(8,128)} %param.21) | copy-start | bytes 4612
  6.5 249.9 %all-gather.3.cloned.1.call-start = ((), (), s32[]{:S(2)}) async-start(), calls=%async_computation | async-start | bytes 4227072 | tf_op jit(solution)/shard_map/all_gather | solution.py:295
Sparse Core Ops, SparseCore 0:
  18.0 226.5 all-gather.2

commit v16 on v14

--- a/solution.py
+++ b/solution.py
@@ -11,41 +11,59 @@
 exact_mode = lax.Precision.HIGHEST
 
 
-def coef_kernel(size_ref, parent_ref, charges_ref, basis_ref, transfer_ref, mid_transfer_ref,
+def coef_kernel(nb, size_ref, parent_ref, charges_ref, basis_ref, transfer_ref, mid_transfer_ref,
                 leaf_ref, mid_ref, top_ref):
-    leaves, rank, points = basis_ref.shape
+    i = pl.program_id(0)
+    rank, points = basis_ref.shape[1:]
     mids = mid_transfer_ref.shape[0]
-    mid_ref[...] = jnp.zeros(mid_ref.shape, jnp.float32)
+
+    @pl.when(i == 0)
+    def _():
+        mid_ref[...] = jnp.zeros(mid_ref.shape, jnp.float32)
+
     rows = lax.broadcasted_iota(jnp.int32, (points, 1), 0)
-    for l in range(leaves):
-        blk = charges_ref[l * points:(l + 1) * points, :]
+    for t in range(nb):
+        l = i * nb + t
+        blk = charges_ref[t * points:(t + 1) * points, :]
         blk = jnp.where(rows < size_ref[l], blk, 0.0)
-        coef = jnp.dot(basis_ref[l], blk, precision=exact_mode, preferred_element_type=jnp.float32)
-        leaf_ref[l] = coef
-        up = jnp.dot(transfer_ref[l], coef, precision=exact_mode, preferred_element_type=jnp.float32)
+        coef = jnp.dot(basis_ref[t], blk, precision=exact_mode, preferred_element_type=jnp.float32)
+        leaf_ref[t] = coef
+        up = jnp.dot(transfer_ref[t], coef, precision=exact_mode, preferred_element_type=jnp.float32)
         p = parent_ref[l]
         mid_ref[p] = mid_ref[p] + up
-    top = jnp.zeros(top_ref.shape, jnp.float32)
-    for c in range(mids):
-        top = top + jnp.dot(mid_transfer_ref[c], mid_ref[c], precision=exact_mode,
-                            preferred_element_type=jnp.float32)
-    top_ref[...] = top
-
-
-def build_coefs(charges, leaf_size, leaf_parent, leaf_basis, leaf_transfer, mid_transfer):
+
+    @pl.when(i == pl.num_programs(0) - 1)
+    def _():
+        top = jnp.zeros(top_ref.shape, jnp.float32)
+        for c in range(mids):
+            top = top + jnp.dot(mid_transfer_ref[c], mid_ref[c], precision=exact_mode,
+                                preferred_element_type=jnp.float32)
+        top_ref[...] = top
+
+
+def build_coefs(charges, leaf_size, leaf_parent, leaf_basis, leaf_transfer, mid_transfer, nb=8):
     leaves, rank, points = leaf_basis.shape
     ports = charges.shape[1]
     mids = mid_transfer.shape[0]
-    vmem = pl.BlockSpec(memory_space=pltpu.VMEM)
-    smem = pl.BlockSpec(memory_space=pltpu.SMEM)
+    grid_spec = pltpu.PrefetchScalarGridSpec(
+        num_scalar_prefetch=2,
+        grid=(leaves // nb,),
+        in_specs=[pl.BlockSpec((nb * points, ports), lambda i, *_: (i, 0)),
+                  pl.BlockSpec((nb, rank, points), lambda i, *_: (i, 0, 0)),
+                  pl.BlockSpec((nb, rank, rank), lambda i, *_: (i, 0, 0)),
+                  pl.BlockSpec(mid_transfer.shape, lambda i, *_: (0, 0, 0))],
+        out_specs=[pl.BlockSpec((nb, rank, ports), lambda i, *_: (i, 0, 0)),
+                   pl.BlockSpec((mids, rank, ports), lambda i, *_: (0, 0, 0)),
+                   pl.BlockSpec((rank, ports), lambda i, *_: (0, 0))],
+    )
     return pl.pallas_call(
-        coef_kernel,
+        functools.partial(coef_kernel, nb),
+        grid_spec=grid_spec,
         out_shape=[jax.ShapeDtypeStruct((leaves, rank, ports), jnp.float32),
                    jax.ShapeDtypeStruct((mids, rank, ports), jnp.float32),
                    jax.ShapeDtypeStruct((rank, ports), jnp.float32)],
-        in_specs=[smem, smem, vmem, vmem, vmem, vmem],
-        out_specs=[vmem, vmem, vmem],
-        compiler_params=pltpu.CompilerParams(vmem_limit_bytes=60 * 1024 * 1024),
+        compiler_params=pltpu.CompilerParams(vmem_limit_bytes=60 * 1024 * 1024,
+                                             dimension_semantics=("arbitrary",)),
         cost_estimate=pl.CostEstimate(flops=2 * leaves * rank * points * ports,
                                       bytes_accessed=4 * (charges.size + leaf_basis.size),
                                       transcendentals=0),

time: 274 us -> 270 us (0.985)
  Pallas kernels: 258 us -> 254 us
    pallas_call x1, Pallas kernels: 238 us -> 234 us  [exchange_couple(): pl.pallas_call(functools.partial(exchange_couple_kernel, axes, sizes), ou...]
where the time goes in v16:
time: 270 us; the launch traced here: 269 us
  Pallas kernels  254 us (94%)
  between operations  13.4 us (5%)
    pallas_call x1, Pallas kernels, exchange_couple(): pl.pallas_call(functools.partial(exchange_couple_kernel, axes, sizes), ou...  234 us
    pallas_call x1, Pallas kernels, build_coefs(): pl.pallas_call(functools.partial(coef_kernel, nb), grid_spec=grid_spec, o...  10.8 us
    pallas_call x1, Pallas kernels, far_field_pallas(): pl.pallas_call(functools.partial(far_kernel, nb, listed, coarse), grid_sp...  9.2 us
  transfers between devices with their start and end apart: 1, of which 0 were waited for; matrix products, arithmetic and copies ran while one was open for 1% of the time, Pallas kernels for 87%

profile of v16, /device:TPU:24, one launch (start us, length us, event | category | flops | bytes accessed | tf_op | source)
XLA Modules:
  0.0 269.0 jit_solution(1260781901655432250)
XLA Ops:
  6.5 0.0 copy-start
  6.5 0.0 copy-start.1
  6.5 0.0 all-gather.3.cloned.1.call-start
  6.5 10.8 %shard_map.136 = (f32[32,64,128]{2,1,0:T(8,128)}, f32[8,64,128]{2,1,0:T(8,128)}, f32[64,128]{1,0:T(8,128)}) custom-call(s32[32]{0:T(128)} %size_ref.3, s32[32]{0:T(128)} %parent_ref.3, f32[8192,128]{1,0:T(8,128)} %charges_ref.1, f32[32,64,256]{2,1,0:T(8,128)} %basis_ref.3, f32[32,64,64]{2,1,0:T(8,128)} %transfer_ref.3, f32[8,64,64]{2,1,0:T(8,128)} %mid_transfer_ref.3), custom_call_target="tpu_custom_call" | custom-call | flops 134217728 | bytes 6291456 | tf_op jit(solution)/shard_map/pallas_call | solution.py:59
  17.3 0.0 all-gather.3.cloned.1.call-update
  17.4 0.0 copy-done.1
  17.4 0.7 copy.15.pair_leaf_ref
  18.1 0.0 copy-done
  18.1 0.7 dynamic-slice_reduce_fusion.wanted_ref
  18.8 234.1 %shard_map.137 = (f32[32,64,128]{2,1,0:T(8,128)}, f32[8,64,128]{2,1,0:T(8,128)}) custom-call(s32[32,12]{1,0:T(8,128)} %copy.15.pair_leaf_ref, s32[8,32]{1,0:T(8,128)} %pair_mid_ref.1, s32[256]{0:T(256)} %send_leaf_ref.1, s32[256]{0:T(256)} %send_mid_ref.1, f32[32,64,128]{2,1,0:T(8,128)} %get-tuple-element.10.coef_leaf_ref, ...), custom_call_target="tpu_custom_call" | custom-call | flops 671088640 | bytes 11796480 | tf_op jit(solution)/shard_map/pallas_call | solution.py:247
  252.9 0.0 all-gather.3.cloned.1.call-done
  252.9 9.2 %shard_map.138 = f32[8192,128]{1,0:T(8,128)} custom-call(s32[32]{0:T(128)} %size_ref.3, s32[32]{0:T(128)} %parent_ref.3, s32[4]{0:T(128)} %dynamic-slice_reduce_fusion.wanted_ref, s32[1]{0:T(128)} %bitcast.pos_ref, f32[32,64,128]{2,1,0:T(8,128)} %get-tuple-element.12.near_ref, f32[32,64,64]{2,1,0:T(8,128)} %transfer_ref.3, f32[32,64,256]{2,1,0:T(8,128)} %basis_ref.3, ...), custom_call_target="tpu_custom_call" | custom-call | flops 134217728 | bytes 10485760 | tf_op jit(solution)/shard_map/pallas_call | solution.py:130
Async XLA Ops:
  6.5 11.5 %copy-start = (s32[32,4]{0,1:T(4,128)S(1)}, s32[32,4]{0,1:T(4,128)}, u32[]{:S(2)}) copy-start(s32[32,4]{0,1:T(4,128)} %param.26) | copy-start | bytes 1540
  6.5 10.8 %copy-start.1 = (s32[32,12]{0,1:T(8,128)S(1)}, s32[32,12]{0,1:T(8,128)}, u32[]{:S(2)}) copy-start(s32[32,12]{0,1:T(8,128)} %param.21) | copy-start | bytes 4612
  6.5 246.4 %all-gather.3.cloned.1.call-start = ((), (), s32[]{:S(2)}) async-start(), calls=%async_computation | async-start | bytes 4227072 | tf_op jit(solution)/shard_map/all_gather | solution.py:298
Sparse Core Ops, SparseCore 0:
  17.5 227.7 all-gather.2

commit v17 on v16

--- a/solution.py
+++ b/solution.py
@@ -103,7 +103,7 @@
 
 
 def far_field_pallas(near_leaf, leaf_transfer, leaf_basis, near_mid, mid_transfer, top_coupling,
-                     shard_rows, wanted, position, leaf_size, leaf_parent, nb=8):
+                     shard_rows, wanted, position, leaf_size, leaf_parent, nb=16):
     leaves, rank, points = leaf_basis.shape
     ports = near_leaf.shape[2]
     listed = wanted.shape[0]

time: 270 us -> 270 us (level)
  no operation moved by 1% of the time
where the time goes in v17:
time: 270 us; the launch traced here: 269 us
  Pallas kernels  254 us (94%)
  between operations  13.4 us (5%)
    pallas_call x1, Pallas kernels, exchange_couple(): pl.pallas_call(functools.partial(exchange_couple_kernel, axes, sizes), ou...  234 us
    pallas_call x1, Pallas kernels, build_coefs(): pl.pallas_call(functools.partial(coef_kernel, nb), grid_spec=grid_spec, o...  10.8 us
    pallas_call x1, Pallas kernels, far_field_pallas(): pl.pallas_call(functools.partial(far_kernel, nb, listed, coarse), grid_sp...  9.08 us
  transfers between devices with their start and end apart: 1, of which 0 were waited for; matrix products, arithmetic and copies ran while one was open for 1% of the time, Pallas kernels for 87%

profile of v17, /device:TPU:24, one launch (start us, length us, event | category | flops | bytes accessed | tf_op | source)
XLA Modules:
  0.0 268.9 jit_solution(17606524098825465336)
XLA Ops:
  6.5 0.0 copy-start
  6.5 0.0 copy-start.1
  6.5 0.0 all-gather.3.cloned.1.call-start
  6.5 10.8 %shard_map.136 = (f32[32,64,128]{2,1,0:T(8,128)}, f32[8,64,128]{2,1,0:T(8,128)}, f32[64,128]{1,0:T(8,128)}) custom-call(s32[32]{0:T(128)} %size_ref.3, s32[32]{0:T(128)} %parent_ref.3, f32[8192,128]{1,0:T(8,128)} %charges_ref.1, f32[32,64,256]{2,1,0:T(8,128)} %basis_ref.3, f32[32,64,64]{2,1,0:T(8,128)} %transfer_ref.3, f32[8,64,64]{2,1,0:T(8,128)} %mid_transfer_ref.3), custom_call_target="tpu_custom_call" | custom-call | flops 134217728 | bytes 6291456 | tf_op jit(solution)/shard_map/pallas_call | solution.py:59
  17.3 0.0 all-gather.3.cloned.1.call-update
  17.4 0.0 copy-done.1
  17.4 0.7 copy.15.pair_leaf_ref
  18.1 0.0 copy-done
  18.1 0.7 dynamic-slice_reduce_fusion.wanted_ref
  18.8 234.1 %shard_map.137 = (f32[32,64,128]{2,1,0:T(8,128)}, f32[8,64,128]{2,1,0:T(8,128)}) custom-call(s32[32,12]{1,0:T(8,128)} %copy.15.pair_leaf_ref, s32[8,32]{1,0:T(8,128)} %pair_mid_ref.1, s32[256]{0:T(256)} %send_leaf_ref.1, s32[256]{0:T(256)} %send_mid_ref.1, f32[32,64,128]{2,1,0:T(8,128)} %get-tuple-element.10.coef_leaf_ref, ...), custom_call_target="tpu_custom_call" | custom-call | flops 671088640 | bytes 11796480 | tf_op jit(solution)/shard_map/pallas_call | solution.py:247
  252.9 0.0 all-gather.3.cloned.1.call-done
  252.9 9.1 %shard_map.138 = f32[8192,128]{1,0:T(8,128)} custom-call(s32[32]{0:T(128)} %size_ref.3, s32[32]{0:T(128)} %parent_ref.3, s32[4]{0:T(128)} %dynamic-slice_reduce_fusion.wanted_ref, s32[1]{0:T(128)} %bitcast.pos_ref, f32[32,64,128]{2,1,0:T(8,128)} %get-tuple-element.12.near_ref, f32[32,64,64]{2,1,0:T(8,128)} %transfer_ref.3, f32[32,64,256]{2,1,0:T(8,128)} %basis_ref.3, ...), custom_call_target="tpu_custom_call" | custom-call | flops 134217728 | bytes 10485760 | tf_op jit(solution)/shard_map/pallas_call | solution.py:130
Async XLA Ops:
  6.5 11.5 %copy-start = (s32[32,4]{0,1:T(4,128)S(1)}, s32[32,4]{0,1:T(4,128)}, u32[]{:S(2)}) copy-start(s32[32,4]{0,1:T(4,128)} %param.26) | copy-start | bytes 1540
  6.5 10.8 %copy-start.1 = (s32[32,12]{0,1:T(8,128)S(1)}, s32[32,12]{0,1:T(8,128)}, u32[]{:S(2)}) copy-start(s32[32,12]{0,1:T(8,128)} %param.21) | copy-start | bytes 4612
  6.5 246.4 %all-gather.3.cloned.1.call-start = ((), (), s32[]{:S(2)}) async-start(), calls=%async_computation | async-start | bytes 4227072 | tf_op jit(solution)/shard_map/all_gather | solution.py:298
Sparse Core Ops, SparseCore 0:
  17.5 227.7 all-gather.2

commit v18 on v16

--- a/solution.py
+++ b/solution.py
@@ -186,7 +186,7 @@
 
     lax.fori_loop(1, count, greet, 0)
     pl.semaphore_wait(barrier, count - 1)
-    stride = 37 if math.gcd(37, count) == 1 else 1
+    stride = 45 if math.gcd(45, count) == 1 else 1
     slots = leaf_pay_ref.shape[0] // count
 
     def sender(pay_ref, land_ref, send_sem, recv_sem):

time: 270 us -> 273 us (1.011)
  Pallas kernels: 254 us -> 258 us
    pallas_call x1, Pallas kernels: 234 us -> 238 us  [exchange_couple(): pl.pallas_call(functools.partial(exchange_couple_kernel, axes, sizes), ou...]
where the time goes in v18:
time: 273 us
  Pallas kernels  258 us (95%)
  between operations  13.4 us (5%)
    pallas_call x1, Pallas kernels, exchange_couple(): pl.pallas_call(functools.partial(exchange_couple_kernel, axes, sizes), ou...  238 us
    pallas_call x1, Pallas kernels, build_coefs(): pl.pallas_call(functools.partial(coef_kernel, nb), grid_spec=grid_spec, o...  10.8 us
    pallas_call x1, Pallas kernels, far_field_pallas(): pl.pallas_call(functools.partial(far_kernel, nb, listed, coarse), grid_sp...  9.21 us
  transfers between devices with their start and end apart: 1, of which 0 were waited for; matrix products, arithmetic and copies ran while one was open for 1% of the time, Pallas kernels for 87%

profile of v18, /device:TPU:24, one launch (start us, length us, event | category | flops | bytes accessed | tf_op | source)
XLA Modules:
  0.0 273.1 jit_solution(8015834414491597028)
XLA Ops:
  6.5 0.0 copy-start
  6.5 0.0 copy-start.1
  6.5 0.0 all-gather.3.cloned.1.call-start
  6.5 10.8 %shard_map.136 = (f32[32,64,128]{2,1,0:T(8,128)}, f32[8,64,128]{2,1,0:T(8,128)}, f32[64,128]{1,0:T(8,128)}) custom-call(s32[32]{0:T(128)} %size_ref.3, s32[32]{0:T(128)} %parent_ref.3, f32[8192,128]{1,0:T(8,128)} %charges_ref.1, f32[32,64,256]{2,1,0:T(8,128)} %basis_ref.3, f32[32,64,64]{2,1,0:T(8,128)} %transfer_ref.3, f32[8,64,64]{2,1,0:T(8,128)} %mid_transfer_ref.3), custom_call_target="tpu_custom_call" | custom-call | flops 134217728 | bytes 6291456 | tf_op jit(solution)/shard_map/pallas_call | solution.py:59
  17.3 0.0 all-gather.3.cloned.1.call-update
  17.4 0.0 copy-done.1
  17.4 0.7 copy.15.pair_leaf_ref
  18.1 0.0 copy-done
  18.1 0.7 dynamic-slice_reduce_fusion.wanted_ref
  18.8 238.3 %shard_map.137 = (f32[32,64,128]{2,1,0:T(8,128)}, f32[8,64,128]{2,1,0:T(8,128)}) custom-call(s32[32,12]{1,0:T(8,128)} %copy.15.pair_leaf_ref, s32[8,32]{1,0:T(8,128)} %pair_mid_ref.1, s32[256]{0:T(256)} %send_leaf_ref.1, s32[256]{0:T(256)} %send_mid_ref.1, f32[32,64,128]{2,1,0:T(8,128)} %get-tuple-element.10.coef_leaf_ref, ...), custom_call_target="tpu_custom_call" | custom-call | flops 671088640 | bytes 11796480 | tf_op jit(solution)/shard_map/pallas_call | solution.py:247
  257.0 0.0 all-gather.3.cloned.1.call-done
  257.1 9.2 %shard_map.138 = f32[8192,128]{1,0:T(8,128)} custom-call(s32[32]{0:T(128)} %size_ref.3, s32[32]{0:T(128)} %parent_ref.3, s32[4]{0:T(128)} %dynamic-slice_reduce_fusion.wanted_ref, s32[1]{0:T(128)} %bitcast.pos_ref, f32[32,64,128]{2,1,0:T(8,128)} %get-tuple-element.12.near_ref, f32[32,64,64]{2,1,0:T(8,128)} %transfer_ref.3, f32[32,64,256]{2,1,0:T(8,128)} %basis_ref.3, ...), custom_call_target="tpu_custom_call" | custom-call | flops 134217728 | bytes 10485760 | tf_op jit(solution)/shard_map/pallas_call | solution.py:130
Async XLA Ops:
  6.5 11.5 %copy-start = (s32[32,4]{0,1:T(4,128)S(1)}, s32[32,4]{0,1:T(4,128)}, u32[]{:S(2)}) copy-start(s32[32,4]{0,1:T(4,128)} %param.26) | copy-start | bytes 1540
  6.5 10.8 %copy-start.1 = (s32[32,12]{0,1:T(8,128)S(1)}, s32[32,12]{0,1:T(8,128)}, u32[]{:S(2)}) copy-start(s32[32,12]{0,1:T(8,128)} %param.21) | copy-start | bytes 4612
  6.5 250.5 %all-gather.3.cloned.1.call-start = ((), (), s32[]{:S(2)}) async-start(), calls=%async_computation | async-start | bytes 4227072 | tf_op jit(solution)/shard_map/all_gather | solution.py:298
Sparse Core Ops, SparseCore 0:
  17.5 216.1 all-gather.2

commit v19 on v16

--- a/solution.py
+++ b/solution.py
@@ -41,7 +41,7 @@
         top_ref[...] = top
 
 
-def build_coefs(charges, leaf_size, leaf_parent, leaf_basis, leaf_transfer, mid_transfer, nb=8):
+def build_coefs(charges, leaf_size, leaf_parent, leaf_basis, leaf_transfer, mid_transfer, nb=4):
     leaves, rank, points = leaf_basis.shape
     ports = charges.shape[1]
     mids = mid_transfer.shape[0]

time: 270 us -> 271 us (level)
  no operation moved by 1% of the time
where the time goes in v19:
time: 271 us; the launch traced here: 268 us
  Pallas kernels  253 us (93%)
  between operations  13.4 us (5%)
    pallas_call x1, Pallas kernels, exchange_couple(): pl.pallas_call(functools.partial(exchange_couple_kernel, axes, sizes), ou...  233 us
    pallas_call x1, Pallas kernels, build_coefs(): pl.pallas_call(functools.partial(coef_kernel, nb), grid_spec=grid_spec, o...  11.7 us
    pallas_call x1, Pallas kernels, far_field_pallas(): pl.pallas_call(functools.partial(far_kernel, nb, listed, coarse), grid_sp...  9.2 us
  transfers between devices with their start and end apart: 1, of which 0 were waited for; matrix products, arithmetic and copies ran while one was open for 1% of the time, Pallas kernels for 87%

profile of v19, /device:TPU:24, one launch (start us, length us, event | category | flops | bytes accessed | tf_op | source)
XLA Modules:
  0.0 268.3 jit_solution(14194739744190439507)
XLA Ops:
  6.5 0.0 copy-start
  6.5 0.0 copy-start.1
  6.5 0.0 all-gather.3.cloned.1.call-start
  6.5 11.7 %shard_map.136 = (f32[32,64,128]{2,1,0:T(8,128)}, f32[8,64,128]{2,1,0:T(8,128)}, f32[64,128]{1,0:T(8,128)}) custom-call(s32[32]{0:T(128)} %size_ref.3, s32[32]{0:T(128)} %parent_ref.3, f32[8192,128]{1,0:T(8,128)} %charges_ref.1, f32[32,64,256]{2,1,0:T(8,128)} %basis_ref.3, f32[32,64,64]{2,1,0:T(8,128)} %transfer_ref.3, f32[8,64,64]{2,1,0:T(8,128)} %mid_transfer_ref.3), custom_call_target="tpu_custom_call" | custom-call | flops 134217728 | bytes 6291456 | tf_op jit(solution)/shard_map/pallas_call | solution.py:59
  18.2 0.0 all-gather.3.cloned.1.call-update
  18.2 0.0 copy-done.1
  18.2 0.7 copy.15.pair_leaf_ref
  18.9 0.0 copy-done
  18.9 0.7 dynamic-slice_reduce_fusion.wanted_ref
  19.6 232.5 %shard_map.137 = (f32[32,64,128]{2,1,0:T(8,128)}, f32[8,64,128]{2,1,0:T(8,128)}) custom-call(s32[32,12]{1,0:T(8,128)} %copy.15.pair_leaf_ref, s32[8,32]{1,0:T(8,128)} %pair_mid_ref.1, s32[256]{0:T(256)} %send_leaf_ref.1, s32[256]{0:T(256)} %send_mid_ref.1, f32[32,64,128]{2,1,0:T(8,128)} %get-tuple-element.10.coef_leaf_ref, ...), custom_call_target="tpu_custom_call" | custom-call | flops 671088640 | bytes 11796480 | tf_op jit(solution)/shard_map/pallas_call | solution.py:247
  252.2 0.0 all-gather.3.cloned.1.call-done
  252.2 9.2 %shard_map.138 = f32[8192,128]{1,0:T(8,128)} custom-call(s32[32]{0:T(128)} %size_ref.3, s32[32]{0:T(128)} %parent_ref.3, s32[4]{0:T(128)} %dynamic-slice_reduce_fusion.wanted_ref, s32[1]{0:T(128)} %bitcast.pos_ref, f32[32,64,128]{2,1,0:T(8,128)} %get-tuple-element.12.near_ref, f32[32,64,64]{2,1,0:T(8,128)} %transfer_ref.3, f32[32,64,256]{2,1,0:T(8,128)} %basis_ref.3, ...), custom_call_target="tpu_custom_call" | custom-call | flops 134217728 | bytes 10485760 | tf_op jit(solution)/shard_map/pallas_call | solution.py:130
Async XLA Ops:
  6.5 12.4 %copy-start = (s32[32,4]{0,1:T(4,128)S(1)}, s32[32,4]{0,1:T(4,128)}, u32[]{:S(2)}) copy-start(s32[32,4]{0,1:T(4,128)} %param.26) | copy-start | bytes 1540
  6.5 11.7 %copy-start.1 = (s32[32,12]{0,1:T(8,128)S(1)}, s32[32,12]{0,1:T(8,128)}, u32[]{:S(2)}) copy-start(s32[32,12]{0,1:T(8,128)} %param.21) | copy-start | bytes 4612
  6.5 245.7 %all-gather.3.cloned.1.call-start = ((), (), s32[]{:S(2)}) async-start(), calls=%async_computation | async-start | bytes 4227072 | tf_op jit(solution)/shard_map/all_gather | solution.py:298
Sparse Core Ops, SparseCore 0:
  18.3 229.7 all-gather.2
